TPU v7x, 32 devices: a whole 2x2x4 slice. The times are simulated.
32 devices in a mesh: space: 2 (over x), mom: 16 (over z, y, core).
Axes of the slice: x: 2, y: 2, z: 4, core: 2. Of those that a mesh axis runs over, the one named last changes fastest.
Arguments:
- distribution: float32 [8, 16, 8, 1024], P('space', 'mom'), may hold values from 0.1 to 2
- a_factor: bfloat16 [1024, 8192], P(None, 'mom'), may hold values from -0.1875 to 0.1875
- b_factor: bfloat16 [1024, 8192], P(None, 'mom'), may hold values from -0.1875 to 0.1875
- velocity: float32 [3, 1024], replicated, may hold values from -1 to 1
- drift: float32 [1024], replicated, may hold values from 0.05 to 0.5
Outputs:
- distribution_out: float32 [8, 16, 8, 1024], P('space', 'mom')
All inputs are finite; a program needn't handle non-finite values.
Results may differ from a plain program's by a relative error of at most 0.001.
Values may be sent and summed in bfloat16 or wider, within the bound.
No kernel may reach another device: no remote copies, remote signals or barrier semaphores. Data moves between devices by JAX's collectives and lax.ppermute only.
A program may use at most 64 MiB of HBM per device.

v0:
```python
import jax
import jax.numpy as jnp
from jax import lax
from jax.sharding import PartitionSpec as P

P_SIZE = 1024
RANK = 8
NDIR = 16
ITERS = 2


collide_rate = 0.1
courant = 0.3


def extended(cells, sides, width):
    for axis, dim in sides:
        count = lax.axis_size(axis)
        head = lax.slice_in_dim(cells, 0, width, axis=dim)
        tail = lax.slice_in_dim(cells, cells.shape[dim] - width, cells.shape[dim], axis=dim)
        cells = jnp.concatenate(
            [
                lax.ppermute(tail, axis, [(i, (i + 1) % count) for i in range(count)]),
                cells,
                lax.ppermute(head, axis, [((i + 1) % count, i) for i in range(count)]),
            ],
            axis=dim,
        )
    return cells


def upwind(center, behind, beyond, speeds):
    return jnp.maximum(speeds, 0.0) * (center - behind) + jnp.minimum(speeds, 0.0) * (
        beyond - center
    )


def rank_sum(proj_a, proj_b, width):
    return (proj_a * proj_b).reshape(proj_a.shape[0], width, RANK).sum(axis=2)


def per_device(distribution, a_factor, b_factor, velocity, drift):
    width = a_factor.shape[1] // RANK
    state = distribution
    for substep in range(ITERS):
        state_in = state.astype(jnp.bfloat16)
        piece = lax.all_gather(state_in, "mom", axis=1, tiled=True)
        rows_flat = piece.reshape(-1, P_SIZE)
        proj_a = jnp.dot(rows_flat, a_factor, preferred_element_type=jnp.float32)
        proj_b = jnp.dot(rows_flat, b_factor, preferred_element_type=jnp.float32)
        summed = rank_sum(proj_a, proj_b, width)
        terms = summed.reshape(piece.shape[0], piece.shape[1], piece.shape[2], width)
        collision = lax.all_to_all(
            terms.astype(jnp.bfloat16), "mom", split_axis=1, concat_axis=3, tiled=True
        ).astype(terms.dtype)
        collided = state + collide_rate * collision
        padded = extended(collided, (("space", 0), ("mom", 1)), 1)
        read = collided - courant * upwind(
            collided, padded[:-2, 1:-1], padded[2:, 1:-1], velocity[0]
        )
        read = read - courant * upwind(collided, padded[1:-1, :-2], padded[1:-1, 2:], velocity[1])
        read = read - courant * upwind(
            collided, jnp.roll(collided, 1, axis=2), jnp.roll(collided, -1, axis=2), velocity[2]
        )
        upper = jnp.concatenate(
            [read[..., NDIR:], jnp.zeros(read.shape[:3] + (NDIR,), jnp.float32)], axis=3
        )
        state = read + drift * (upper - read)
    return state


def solution(mesh):
    in_specs = (P("space", "mom", None, None), P(None, "mom"), P(None, "mom"), P(), P())
    out_specs = P("space", "mom", None, None)
    return jax.shard_map(
        per_device, mesh=mesh, in_specs=in_specs, out_specs=out_specs, check_vma=False
    )
```

profile of v0, /device:TPU:0, one launch (start us, length us, event | category | flops | bytes accessed | tf_op | source)
XLA Modules:
  0.0 150.7 jit_solution(6483268718144067877)
XLA Ops:
  6.5 1.6 %convert_element_type.46 = bf16[4,1,8,1024]{3,2,1,0:T(8,128)(2,1)} convert(f32[4,1,8,1024]{3,2,1,0:T(8,128)} %param.5) | non-fusion elementwise | flops 32768 | bytes 196608 | tf_op jit(solution)/shard_map/convert_element_type | solution.py:46
  8.2 0.0 all-gather.3.cloned.1.call-update
  8.2 41.9 %all-gather.3.cloned.1.call-done = bf16[4,16,8,1024]{3,2,1,0:T(8,128)(2,1)} async-done(((bf16[4,1,8,1024]{3,2,1,0:T(8,128)(2,1)}), bf16[4,16,8,1024]{3,2,1,0:T(8,128)(2,1)}) %all-gather.3.cloned.1.call-update) | async-done | bytes 1048592 | tf_op jit(solution)/shard_map/all_gather | solution.py:47
  50.1 2.1 %fusion.46 = f32[512,512]{0,1:T(8,128)S(1)} fusion(bf16[512,1024]{1,0:T(8,128)(2,1)} %bitcast.74, bf16[1024,512]{1,0:T(8,128)(2,1)S(1)} %copy-done), kind=kOutput, calls=%fused_computation.75 | convolution fusion | flops 536870912 | bytes 3145728 | tf_op jit(solution)/shard_map/dot_general | solution.py:49
  52.3 0.9 fusion.2
  53.2 0.1 copy.15
  53.4 0.8 reshape.121
  54.2 3.8 %all-to-all-start = ((bf16[16,2,1024]{2,1,0:T(2,128)(2,1)}), bf16[16,2,1024]{2,1,0:T(2,128)(2,1)S(1)}, u32[]{:S(2)}, u32[]{:S(2)}) async-start(bf16[16,2,1024]{2,1,0:T(2,128)(2,1)} %reshape.121), calls=%async_computation | async-start | bytes 131072 | tf_op jit(solution)/shard_map/all_to_all | solution.py:53
  58.0 0.0 all-gather.5.cloned.1.call-start
  58.1 6.8 %all-to-all-done = bf16[16,2,1024]{2,1,0:T(2,128)(2,1)S(1)} async-done(((bf16[16,2,1024]{2,1,0:T(2,128)(2,1)}), bf16[16,2,1024]{2,1,0:T(2,128)(2,1)S(1)}, u32[]{:S(2)}, u32[]{:S(2)}) %all-to-all-start) | async-done | bytes 65568 | tf_op jit(solution)/shard_map/all_to_all | solution.py:53
  64.9 0.1 reshape.122
  65.1 0.2 copy.17
  65.2 0.1 mul.166
  65.4 0.8 copy-done.1
  66.2 1.5 %collective-permute-start = (f32[1,1,8,1024]{3,2,0,1:T(8,128)S(1)}, f32[1,1,8,1024]{3,2,0,1:T(8,128)S(1)}, u32[]{:S(2)}, u32[]{:S(2)}) collective-permute-start(f32[1,1,8,1024]{3,2,0,1:T(8,128)S(1)} %get-tuple-element.15), channel_id=1, source_target_pairs={{0,16},{16,0},{1,17},{17,1},{2,18},{18,2},{3,19},{19,3},{4,20},{20... | collective-permute-start | bytes 98312 | tf_op jit(solution)/shard_map/ppermute | solution.py:23
  67.7 0.6 collective-permute-start.1
  68.3 2.0 %collective-permute-done = f32[1,1,8,1024]{3,2,0,1:T(8,128)S(1)} collective-permute-done((f32[1,1,8,1024]{3,2,0,1:T(8,128)S(1)}, f32[1,1,8,1024]{3,2,0,1:T(8,128)S(1)}, u32[]{:S(2)}, u32[]{:S(2)}) %collective-permute-start) | collective-permute-done | bytes 32800 | tf_op jit(solution)/shard_map/ppermute | solution.py:23
  70.3 1.3 collective-permute-done.1
  71.6 0.1 collective-permute-start.3
  71.7 0.5 collective-permute-start.2
  72.2 2.7 %collective-permute-done.3 = f32[6,1,8,1024]{3,2,0,1:T(8,128)S(1)} collective-permute-done((f32[6,1,8,1024]{3,2,0,1:T(8,128)S(1)}, f32[6,1,8,1024]{3,2,0,1:T(8,128)S(1)}, u32[]{:S(2)}, u32[]{:S(2)}) %collective-permute-start.3) | collective-permute-done | bytes 196640 | tf_op jit(solution)/shard_map/ppermute | solution.py:25
  74.9 4.7 %collective-permute-done.2 = f32[6,1,8,1024]{3,2,0,1:T(8,128)S(1)} collective-permute-done((f32[6,1,8,1024]{3,2,0,1:T(8,128)S(1)}, f32[6,1,8,1024]{3,2,0,1:T(8,128)S(1)}, u32[]{:S(2)}, u32[]{:S(2)}) %collective-permute-start.2) | collective-permute-done | bytes 196640 | tf_op jit(solution)/shard_map/ppermute | solution.py:23
  79.5 0.1 fusion.21
  79.7 0.1 slice.119
  79.8 0.6 copy-done.2
  80.4 0.7 fusion.39
  81.0 0.0 all-gather.5.cloned.1.call-update
  81.1 34.3 %all-gather.5.cloned.1.call-done = bf16[4,16,8,1024]{3,2,0,1:T(8,128)(2,1)} async-done(((bf16[4,1,8,1024]{3,2,0,1:T(8,128)(2,1)}), bf16[4,16,8,1024]{3,2,0,1:T(8,128)(2,1)}) %all-gather.5.cloned.1.call-update) | async-done | bytes 1048592 | tf_op jit(solution)/shard_map/all_gather | solution.py:47
  115.4 1.3 copy.19
  116.7 0.8 fusion.47
  117.5 0.9 fusion.3
  118.4 0.1 copy.20
  118.6 0.1 reshape.123
  118.7 10.4 %all_to_all.8 = bf16[16,2,1024]{2,1,0:T(2,128)(2,1)S(1)} all-to-all(bf16[16,2,1024]{2,1,0:T(2,128)(2,1)S(1)} %reshape.123), channel_id=1, replica_groups=mesh['space'=2,'mom'=16] {'mom'}, dimensions={0} | all-to-all | bytes 131072 | tf_op jit(solution)/shard_map/all_to_all | solution.py:53
  129.1 0.1 reshape.124
  129.3 0.2 copy.22
  129.4 0.1 mul.188
  129.6 1.5 %collective-permute-start.4 = (f32[1,1,8,1024]{3,2,0,1:T(8,128)S(1)}, f32[1,1,8,1024]{3,2,0,1:T(8,128)S(1)}, u32[]{:S(2)}, u32[]{:S(2)}) collective-permute-start(f32[1,1,8,1024]{3,2,0,1:T(8,128)S(1)} %get-tuple-element.9), channel_id=1, source_target_pairs={{0,16},{16,0},{1,17},{17,1},{2,18},{18,2},{3,19},{19,3},{4,20},{20... | collective-permute-start | bytes 98312 | tf_op jit(solution)/shard_map/ppermute | solution.py:23
  131.1 0.6 collective-permute-start.5
  131.7 2.0 %collective-permute-done.4 = f32[1,1,8,1024]{3,2,0,1:T(8,128)S(1)} collective-permute-done((f32[1,1,8,1024]{3,2,0,1:T(8,128)S(1)}, f32[1,1,8,1024]{3,2,0,1:T(8,128)S(1)}, u32[]{:S(2)}, u32[]{:S(2)}) %collective-permute-start.4) | collective-permute-done | bytes 32800 | tf_op jit(solution)/shard_map/ppermute | solution.py:23
  133.7 1.3 collective-permute-done.5
  135.1 0.1 collective-permute-start.7
  135.1 0.5 collective-permute-start.6
  135.6 2.7 %collective-permute-done.7 = f32[6,1,8,1024]{3,2,0,1:T(8,128)S(1)} collective-permute-done((f32[6,1,8,1024]{3,2,0,1:T(8,128)S(1)}, f32[6,1,8,1024]{3,2,0,1:T(8,128)S(1)}, u32[]{:S(2)}, u32[]{:S(2)}) %collective-permute-start.7) | collective-permute-done | bytes 196640 | tf_op jit(solution)/shard_map/ppermute | solution.py:25
  138.3 4.7 %collective-permute-done.6 = f32[6,1,8,1024]{3,2,0,1:T(8,128)S(1)} collective-permute-done((f32[6,1,8,1024]{3,2,0,1:T(8,128)S(1)}, f32[6,1,8,1024]{3,2,0,1:T(8,128)S(1)}, u32[]{:S(2)}, u32[]{:S(2)}) %collective-permute-start.6) | collective-permute-done | bytes 196640 | tf_op jit(solution)/shard_map/ppermute | solution.py:23
  143.0 0.1 fusion.8
  143.1 0.1 slice.128
  143.2 0.7 add_bitcast_fusion
  (26 shorter events, 0.3 us)
Async XLA Ops:
  6.5 43.6 %copy-start = (bf16[1024,512]{1,0:T(8,128)(2,1)S(1)}, bf16[1024,512]{1,0:T(8,128)(2,1)}, u32[]{:S(2)}) copy-start(bf16[1024,512]{1,0:T(8,128)(2,1)} %param.6) | copy-start | bytes 3145732
  6.5 43.6 %all-gather.3.cloned.1.call-start = ((), (), s32[]{:S(2)}) async-start(), calls=%async_computation.2 | async-start | bytes 1114112 | tf_op jit(solution)/shard_map/all_gather | solution.py:47
  50.1 2.1 %copy-start.4 = (bf16[1024,512]{1,0:T(8,128)(2,1)S(1)}, bf16[1024,512]{1,0:T(8,128)(2,1)}, u32[]{:S(2)}) copy-start(bf16[1024,512]{1,0:T(8,128)(2,1)} %param.7) | copy-start | bytes 3145732
  50.1 2.1 %copy-start.5 = (bf16[4,16,8,1024]{3,2,1,0:T(8,128)(2,1)S(1)}, bf16[4,16,8,1024]{3,2,1,0:T(8,128)(2,1)}, u32[]{:S(2)}) copy-start(bf16[4,16,8,1024]{3,2,1,0:T(8,128)(2,1)} %all-gather.3.cloned.1.call-done) | copy-start | bytes 3145732
  54.2 3.9 %copy-start.3 = (f32[3,1024]{1,0:T(4,128)S(1)}, f32[3,1024]{1,0:T(4,128)}, u32[]{:S(2)}) copy-start(f32[3,1024]{1,0:T(4,128)} %param.8) | copy-start | bytes 36868
  54.2 10.7 %all-to-all-start = ((bf16[16,2,1024]{2,1,0:T(2,128)(2,1)}), bf16[16,2,1024]{2,1,0:T(2,128)(2,1)S(1)}, u32[]{:S(2)}, u32[]{:S(2)}) async-start(bf16[16,2,1024]{2,1,0:T(2,128)(2,1)} %reshape.121), calls=%async_computation | async-start | bytes 131072 | tf_op jit(solution)/shard_map/all_to_all | solution.py:53
  58.0 57.4 %all-gather.5.cloned.1.call-start = ((), (), s32[]{:S(2)}) async-start(), calls=%async_computation.3 | async-start | bytes 1114112 | tf_op jit(solution)/shard_map/all_gather | solution.py:47
  65.2 0.9 copy-start.1
  66.2 4.1 %collective-permute-start = (f32[1,1,8,1024]{3,2,0,1:T(8,128)S(1)}, f32[1,1,8,1024]{3,2,0,1:T(8,128)S(1)}, u32[]{:S(2)}, u32[]{:S(2)}) collective-permute-start(f32[1,1,8,1024]{3,2,0,1:T(8,128)S(1)} %get-tuple-element.15), channel_id=1, source_target_pairs={{0,16},{16,0},{1,17},{17,1},{2,18},{18,2},{3,19},{19,3},{4,20},{20... | collective-permute-start | bytes 98312 | tf_op jit(solution)/shard_map/ppermute | solution.py:23
  67.7 3.9 %collective-permute-start.1 = (f32[1,1,8,1024]{3,2,0,1:T(8,128)S(1)}, f32[1,1,8,1024]{3,2,0,1:T(8,128)S(1)}, u32[]{:S(2)}, u32[]{:S(2)}) collective-permute-start(f32[1,1,8,1024]{3,2,0,1:T(8,128)S(1)} %get-tuple-element.16), channel_id=1, source_target_pairs={{16,0},{0,16},{17,1},{1,17},{18,2},{2,18},{19,3},{3,19},{20,4},{4,... | collective-permute-start | bytes 98312 | tf_op jit(solution)/shard_map/ppermute | solution.py:25
  71.6 3.2 %collective-permute-start.3 = (f32[6,1,8,1024]{3,2,0,1:T(8,128)S(1)}, f32[6,1,8,1024]{3,2,0,1:T(8,128)S(1)}, u32[]{:S(2)}, u32[]{:S(2)}) collective-permute-start(f32[6,1,8,1024]{3,2,0,1:T(8,128)S(1)} %pad_maximum_fusion), channel_id=1, source_target_pairs={{1,0},{2,1},{3,2},{4,3},{5,4},{6,5},{7,6},{8,7},{9,8},{10,9},{11,1... | collective-permute-start | bytes 589832 | tf_op jit(solution)/shard_map/ppermute | solution.py:25
  71.7 7.8 %collective-permute-start.2 = (f32[6,1,8,1024]{3,2,0,1:T(8,128)S(1)}, f32[6,1,8,1024]{3,2,0,1:T(8,128)S(1)}, u32[]{:S(2)}, u32[]{:S(2)}) collective-permute-start(f32[6,1,8,1024]{3,2,0,1:T(8,128)S(1)} %pad_maximum_fusion), channel_id=1, source_target_pairs={{0,1},{1,2},{2,3},{3,4},{4,5},{5,6},{6,7},{7,8},{8,9},{9,10},{10,1... | collective-permute-start | bytes 589832 | tf_op jit(solution)/shard_map/ppermute | solution.py:23
  79.7 0.7 copy-start.2
  129.6 4.1 %collective-permute-start.4 = (f32[1,1,8,1024]{3,2,0,1:T(8,128)S(1)}, f32[1,1,8,1024]{3,2,0,1:T(8,128)S(1)}, u32[]{:S(2)}, u32[]{:S(2)}) collective-permute-start(f32[1,1,8,1024]{3,2,0,1:T(8,128)S(1)} %get-tuple-element.9), channel_id=1, source_target_pairs={{0,16},{16,0},{1,17},{17,1},{2,18},{18,2},{3,19},{19,3},{4,20},{20... | collective-permute-start | bytes 98312 | tf_op jit(solution)/shard_map/ppermute | solution.py:23
  131.1 3.9 %collective-permute-start.5 = (f32[1,1,8,1024]{3,2,0,1:T(8,128)S(1)}, f32[1,1,8,1024]{3,2,0,1:T(8,128)S(1)}, u32[]{:S(2)}, u32[]{:S(2)}) collective-permute-start(f32[1,1,8,1024]{3,2,0,1:T(8,128)S(1)} %get-tuple-element.10), channel_id=1, source_target_pairs={{16,0},{0,16},{17,1},{1,17},{18,2},{2,18},{19,3},{3,19},{20,4},{4,... | collective-permute-start | bytes 98312 | tf_op jit(solution)/shard_map/ppermute | solution.py:25
  135.1 3.2 %collective-permute-start.7 = (f32[6,1,8,1024]{3,2,0,1:T(8,128)S(1)}, f32[6,1,8,1024]{3,2,0,1:T(8,128)S(1)}, u32[]{:S(2)}, u32[]{:S(2)}) collective-permute-start(f32[6,1,8,1024]{3,2,0,1:T(8,128)S(1)} %pad_maximum_fusion.1), channel_id=1, source_target_pairs={{1,0},{2,1},{3,2},{4,3},{5,4},{6,5},{7,6},{8,7},{9,8},{10,9},{11,1... | collective-permute-start | bytes 589832 | tf_op jit(solution)/shard_map/ppermute | solution.py:25
  135.1 7.8 %collective-permute-start.6 = (f32[6,1,8,1024]{3,2,0,1:T(8,128)S(1)}, f32[6,1,8,1024]{3,2,0,1:T(8,128)S(1)}, u32[]{:S(2)}, u32[]{:S(2)}) collective-permute-start(f32[6,1,8,1024]{3,2,0,1:T(8,128)S(1)} %pad_maximum_fusion.1), channel_id=1, source_target_pairs={{0,1},{1,2},{2,3},{3,4},{4,5},{5,6},{6,7},{7,8},{8,9},{9,10},{10,1... | collective-permute-start | bytes 589832 | tf_op jit(solution)/shard_map/ppermute | solution.py:23
Sparse Core Ops, SparseCore 0:
  9.5 40.5 all-gather.2
  81.2 34.1 all-gather.4
where the time goes:
time: 151 us
  waiting for transfers between devices  104 us (69%)
  between operations  13.6 us (9%)
  blocking collectives  10.4 us (7%)
  starting transfers between devices  9.15 us (6%)
  local copies, waits for them, and re-layouts  4.98 us (3%)
  matrix products  4.76 us (3%)
  other arithmetic  3.39 us (2%)
    all_gather x2, waiting for transfers between devices, per_device(): piece = lax.all_gather(state_in, 'mom', axis=1, tiled=True)  76.3 us
    ppermute x4, waiting for transfers between devices, extended(): lax.ppermute(tail, axis, [(i, (i + 1) % count) for i in range(count)])  13.3 us
    all_to_all x1, blocking collectives, per_device(): lax.all_to_all(terms.astype(jnp.bfloat16), 'mom', split_axis=1, concat_ax...  10.4 us
    ppermute x4, waiting for transfers between devices, extended(): lax.ppermute(head, axis, [((i + 1) % count, i) for i in range(count)])  8 us
    all_to_all x1, waiting for transfers between devices, per_device(): lax.all_to_all(terms.astype(jnp.bfloat16), 'mom', split_axis=1, concat_ax...  6.81 us
    ppermute x4, starting transfers between devices, extended(): lax.ppermute(tail, axis, [(i, (i + 1) % count) for i in range(count)])  4.05 us
    all_to_all x1, starting transfers between devices, per_device(): lax.all_to_all(terms.astype(jnp.bfloat16), 'mom', split_axis=1, concat_ax...  3.82 us
  transfers between devices with their start and end apart: 11, of which 11 were waited for; matrix products, arithmetic and copies ran while one was open for 0% of the time, Pallas kernels for 0%

commit v1 on v0

v1 whole, which is shorter than its diff:
```python
import jax
import jax.numpy as jnp
from jax import lax
from jax.sharding import PartitionSpec as P

P_SIZE = 1024
RANK = 8
NDIR = 16
ITERS = 2


collide_rate = 0.1
courant = 0.3


def swap(block, axis, bits):
    count = lax.axis_size(axis)
    return lax.ppermute(block, axis, [(i, i ^ bits) for i in range(count)])


def gathered(own, axis):
    count = lax.axis_size(axis)
    if count % 4 or count & (count - 1):
        return lax.all_gather(own, axis, axis=0, tiled=False)
    me = lax.axis_index(axis)
    blocks = {0: own}
    for bits in range(4, count, 4):
        blocks[bits] = swap(own, axis, bits)
    for bits in range(0, count, 4):
        blocks[bits ^ 2] = swap(blocks[bits], axis, 2)
    even = jnp.stack([blocks[bits] for bits in range(0, count, 2)])
    odd = swap(even, axis, 1)
    whole = jnp.zeros((count,) + own.shape, own.dtype)
    for at in range(count // 2):
        whole = lax.dynamic_update_index_in_dim(whole, even[at], me ^ (2 * at), 0)
        whole = lax.dynamic_update_index_in_dim(whole, odd[at], me ^ (2 * at) ^ 1, 0)
    return whole


def halo(cells, axis, dim, dtype):
    count = lax.axis_size(axis)
    size = cells.shape[dim]
    head = lax.slice_in_dim(cells, 0, 1, axis=dim).astype(dtype)
    tail = lax.slice_in_dim(cells, size - 1, size, axis=dim).astype(dtype)
    if count == 2:
        both = swap(jnp.concatenate([tail, head], axis=dim), axis, 1)
        behind = lax.slice_in_dim(both, 0, 1, axis=dim)
        ahead = lax.slice_in_dim(both, 1, 2, axis=dim)
    elif count % 2 == 0:
        odd = lax.axis_index(axis) % 2 == 1
        near = swap(jnp.where(odd, head, tail), axis, 1)
        pairs = [(i, (i + 1) % count if i % 2 else (i - 1) % count) for i in range(count)]
        far = lax.ppermute(jnp.where(odd, tail, head), axis, pairs)
        behind = jnp.where(odd, near, far)
        ahead = jnp.where(odd, far, near)
    else:
        behind = lax.ppermute(tail, axis, [(i, (i + 1) % count) for i in range(count)])
        ahead = lax.ppermute(head, axis, [((i + 1) % count, i) for i in range(count)])
    return behind.astype(cells.dtype), ahead.astype(cells.dtype)


def shifted(cells, behind, ahead, dim):
    size = cells.shape[dim]
    back = jnp.concatenate([behind, lax.slice_in_dim(cells, 0, size - 1, axis=dim)], axis=dim)
    forth = jnp.concatenate([lax.slice_in_dim(cells, 1, size, axis=dim), ahead], axis=dim)
    return back, forth


def upwind(center, behind, beyond, speeds):
    return jnp.maximum(speeds, 0.0) * (center - behind) + jnp.minimum(speeds, 0.0) * (
        beyond - center
    )


def rank_sum(proj_a, proj_b, width):
    return (proj_a * proj_b).reshape(proj_a.shape[0], width, RANK).sum(axis=2)


def per_device(distribution, a_factor, b_factor, velocity, drift):
    width = a_factor.shape[1] // RANK
    state = distribution
    for substep in range(ITERS):
        piece = gathered(state.astype(jnp.bfloat16), "mom")
        rows_flat = piece.reshape(-1, P_SIZE)
        proj_a = jnp.dot(rows_flat, a_factor, preferred_element_type=jnp.float32)
        proj_b = jnp.dot(rows_flat, b_factor, preferred_element_type=jnp.float32)
        summed = rank_sum(proj_a, proj_b, width)
        terms = summed.reshape(piece.shape[:4] + (width,)).astype(jnp.bfloat16)
        collision = lax.all_to_all(terms, "mom", split_axis=0, concat_axis=0, tiled=True)
        collision = jnp.moveaxis(collision, 0, 3).reshape(state.shape).astype(jnp.float32)
        collided = state + collide_rate * collision
        x_behind, x_ahead = halo(collided, "space", 0, jnp.bfloat16)
        y_behind, y_ahead = halo(collided, "mom", 1, jnp.bfloat16)
        read = collided - courant * upwind(
            collided, *shifted(collided, x_behind, x_ahead, 0), velocity[0]
        )
        read = read - courant * upwind(
            collided, *shifted(collided, y_behind, y_ahead, 1), velocity[1]
        )
        read = read - courant * upwind(
            collided, jnp.roll(collided, 1, axis=2), jnp.roll(collided, -1, axis=2), velocity[2]
        )
        upper = jnp.concatenate(
            [read[..., NDIR:], jnp.zeros(read.shape[:3] + (NDIR,), jnp.float32)], axis=3
        )
        state = read + drift * (upper - read)
    return state


def solution(mesh):
    in_specs = (P("space", "mom", None, None), P(None, "mom"), P(None, "mom"), P(), P())
    out_specs = P("space", "mom", None, None)
    return jax.shard_map(
        per_device, mesh=mesh, in_specs=in_specs, out_specs=out_specs, check_vma=False
    )
```

time: 151 us -> 78.6 us (0.52)
  waiting for transfers between devices: 104 us -> 31.3 us
  starting transfers between devices: 9.15 us -> 25.6 us
  between operations: 13.6 us -> 0.77 us
    all_gather x2 -> x0, waiting for transfers between devices: 76.3 us -> none  [per_device(): piece = lax.all_gather(state_in, 'mom', axis=1, tiled=True)]
    ppermute x8 -> x22, starting transfers between devices: 5.29 us -> 22 us  [the longest x20 20.5 us: swap(): return lax.ppermute(block, axis, [(i, i ^ bits) for i in range(count)])]
    ppermute x8 -> x22, waiting for transfers between devices: 21.3 us -> 24.4 us  [the longest x20 21.1 us: swap(): return lax.ppermute(block, axis, [(i, i ^ bits) for i in range(count)])]
    convert_element_type x2, other arithmetic: 2.28 us -> 0.01 us  [halo(): return (behind.astype(cells.dtype), ahead.astype(cells.dtype))]
    unnamed x16 -> x26, local copies, waits for them, and re-layouts: 2.55 us -> 3.08 us
  transfers between devices with their start and end apart: 11 -> 23, of which waited for: 11 -> 13; matrix products, arithmetic and copies ran while one was open for 0% -> 1% of each run, Pallas kernels for 0% -> 0%
where the time goes in v1:
time: 78.6 us; the launch traced here: 78.2 us
  waiting for transfers between devices  31.3 us (40%)
  starting transfers between devices  25.6 us (33%)
  blocking collectives  10.3 us (13%)
  local copies, waits for them, and re-layouts  4.79 us (6%)
  matrix products  3.4 us (4%)
  other arithmetic  2.17 us (3%)
    ppermute x20, waiting for transfers between devices, swap(): return lax.ppermute(block, axis, [(i, i ^ bits) for i in range(count)])  21.1 us
    ppermute x20, starting transfers between devices, swap(): return lax.ppermute(block, axis, [(i, i ^ bits) for i in range(count)])  20.5 us
    all_to_all x1, blocking collectives, per_device(): lax.all_to_all(terms, 'mom', split_axis=0, concat_axis=0, tiled=True)  10.3 us
    all_to_all x1, waiting for transfers between devices, per_device(): lax.all_to_all(terms, 'mom', split_axis=0, concat_axis=0, tiled=True)  6.83 us
    all_to_all x1, starting transfers between devices, per_device(): lax.all_to_all(terms, 'mom', split_axis=0, concat_axis=0, tiled=True)  3.63 us
    ppermute x2, waiting for transfers between devices, halo(): far = lax.ppermute(jnp.where(odd, tail, head), axis, pairs)  3.3 us
    unnamed x26, local copies, waits for them, and re-layouts  3.08 us
    dot_general x2, matrix products, per_device(): proj_a = jnp.dot(rows_flat, a_factor, preferred_element_type=jnp.float32)  1.88 us
  transfers between devices with their start and end apart: 23, of which 13 were waited for; matrix products, arithmetic and copies ran while one was open for 1% of the time, Pallas kernels for 0%

profile of v1, /device:TPU:0, one launch (start us, length us, event | category | flops | bytes accessed | tf_op | source)
XLA Modules:
  0.0 78.2 jit_solution(16129473980147525069)
XLA Ops:
  0.0 1.0 %bitcast_dynamic-update-slice_fusion.30 = (bf16[8,4,1,8,1024]{4,3,1,2,0:T(8,128)(2,1)S(1)}, bf16[4,1,8,1024]{3,2,1,0:T(8,128)(2,1)S(1)}) fusion(f32[4,1,8,1024]{3,2,1,0:T(8,128)} %param.5), kind=kLoop, calls=%fused_computation.87 | loop fusion | flops 32767 | bytes 262144
  1.0 4.1 %collective-permute-start.3 = (bf16[4,1,8,1024]{3,2,0,1:T(8,128)(2,1)S(1)}, bf16[4,1,8,1024]{3,2,0,1:T(8,128)(2,1)S(1)}, u32[]{:S(2)}, u32[]{:S(2)}) collective-permute-start(bf16[4,1,8,1024]{3,2,0,1:T(8,128)(2,1)S(1)} %bitcast.110), channel_id=1, source_target_pairs={{0,8},{1,9},{2,10},{3,11},{4,12},{5,13},{6,14},{7,15},{8,0},{9,1},... | collective-permute-start | bytes 196616 | tf_op jit(solution)/shard_map/ppermute | solution.py:18
  5.1 1.6 %collective-permute-start.1 = (bf16[4,1,8,1024]{3,2,0,1:T(8,128)(2,1)S(1)}, bf16[4,1,8,1024]{3,2,0,1:T(8,128)(2,1)S(1)}, u32[]{:S(2)}, u32[]{:S(2)}) collective-permute-start(bf16[4,1,8,1024]{3,2,0,1:T(8,128)(2,1)S(1)} %bitcast.111), channel_id=1, source_target_pairs={{0,4},{1,5},{2,6},{3,7},{4,0},{5,1},{6,2},{7,3},{8,12},{9,13},{10,... | collective-permute-start | bytes 196616 | tf_op jit(solution)/shard_map/ppermute | solution.py:18
  6.7 1.5 %collective-permute-start = (bf16[4,1,8,1024]{3,2,0,1:T(8,128)(2,1)S(1)}, bf16[4,1,8,1024]{3,2,0,1:T(8,128)(2,1)S(1)}, u32[]{:S(2)}, u32[]{:S(2)}) collective-permute-start(bf16[4,1,8,1024]{3,2,0,1:T(8,128)(2,1)S(1)} %bitcast.112), channel_id=1, source_target_pairs={{0,2},{1,3},{2,0},{3,1},{4,6},{5,7},{6,4},{7,5},{8,10},{9,11},{10,... | collective-permute-start | bytes 196616 | tf_op jit(solution)/shard_map/ppermute | solution.py:18
  8.2 0.2 collective-permute-start.5
  8.5 1.6 %collective-permute-start.4 = (bf16[4,1,8,1024]{3,2,0,1:T(8,128)(2,1)S(1)}, bf16[4,1,8,1024]{3,2,0,1:T(8,128)(2,1)S(1)}, u32[]{:S(2)}, u32[]{:S(2)}) collective-permute-start(bf16[4,1,8,1024]{3,2,0,1:T(8,128)(2,1)S(1)} %collective-permute-done.3), channel_id=1, source_target_pairs={{0,2},{1,3},{2,0},{3,1},{4,6},{5,7},{6,4},{7,5},{8,10},{9,11},{10,... | collective-permute-start | bytes 196616 | tf_op jit(solution)/shard_map/ppermute | solution.py:18
  10.1 0.8 %collective-permute-start.2 = (bf16[4,1,8,1024]{3,2,0,1:T(8,128)(2,1)S(1)}, bf16[4,1,8,1024]{3,2,0,1:T(8,128)(2,1)S(1)}, u32[]{:S(2)}, u32[]{:S(2)}) collective-permute-start(bf16[4,1,8,1024]{3,2,0,1:T(8,128)(2,1)S(1)} %collective-permute-done.1), channel_id=1, source_target_pairs={{0,2},{1,3},{2,0},{3,1},{4,6},{5,7},{6,4},{7,5},{8,10},{9,11},{10,... | collective-permute-start | bytes 196616 | tf_op jit(solution)/shard_map/ppermute | solution.py:18
  10.9 0.5 collective-permute-done
  11.4 2.9 %collective-permute-done.5 = bf16[4,1,8,1024]{3,2,1,0:T(8,128)(2,1)S(1)} collective-permute-done((bf16[4,1,8,1024]{3,2,1,0:T(8,128)(2,1)S(1)}, bf16[4,1,8,1024]{3,2,1,0:T(8,128)(2,1)S(1)}, u32[]{:S(2)}, u32[]{:S(2)}) %collective-permute-start.5) | collective-permute-done | bytes 65568 | tf_op jit(solution)/shard_map/ppermute | solution.py:18
  14.3 0.5 collective-permute-start.6
  14.9 3.7 %collective-permute-done.6 = bf16[4,1,8,1024]{3,2,1,0:T(8,128)(2,1)S(1)} collective-permute-done((bf16[4,1,8,1024]{3,2,1,0:T(8,128)(2,1)S(1)}, bf16[4,1,8,1024]{3,2,1,0:T(8,128)(2,1)S(1)}, u32[]{:S(2)}, u32[]{:S(2)}) %collective-permute-start.6) | collective-permute-done | bytes 65568 | tf_op jit(solution)/shard_map/ppermute | solution.py:18
  18.8 1.7 %collective-permute-done.7 = bf16[8,4,1,8,1024]{4,3,1,2,0:T(8,128)(2,1)S(1)} collective-permute-done((bf16[8,4,1,8,1024]{4,3,1,2,0:T(8,128)(2,1)S(1)}, bf16[8,4,1,8,1024]{4,3,1,2,0:T(8,128)(2,1)S(1)}, u32[]{:S(2)}, u32[]{:S(2)}) %collective-permute-start.7) | collective-permute-done | bytes 524320 | tf_op jit(solution)/shard_map/ppermute | solution.py:18
  20.8 0.8 fusion.40
  21.6 0.4 copy-done.4
  22.0 0.9 %fusion.2 = bf16[512,64]{0,1:T(8,128)(2,1)S(1)} fusion(f32[512,512]{0,1:T(8,128)S(1)} %fusion.40, bf16[512,1024]{1,0:T(8,128)(2,1)S(1)} %bitcast.107, bf16[1024,512]{1,0:T(8,128)(2,1)S(1)} %copy-done.4), kind=kOutput, calls=%fused_computation.4 | convolution fusion | flops 537362432 | bytes 3211264 | tf_op jit(solution)/shard_map/dot_general | solution.py:85
  23.1 0.8 reshape.141
  23.9 3.6 %all-to-all-start = ((bf16[16,2,1024]{2,1,0:T(2,128)(2,1)}), bf16[16,2,1024]{2,1,0:T(2,128)(2,1)S(1)}, u32[]{:S(2)}, u32[]{:S(2)}) async-start(bf16[16,2,1024]{2,1,0:T(2,128)(2,1)} %reshape.141), calls=%async_computation | async-start | bytes 131072 | tf_op jit(solution)/shard_map/all_to_all | solution.py:89
  27.5 6.8 %all-to-all-done = bf16[16,2,1024]{2,1,0:T(2,128)(2,1)S(1)} async-done(((bf16[16,2,1024]{2,1,0:T(2,128)(2,1)}), bf16[16,2,1024]{2,1,0:T(2,128)(2,1)S(1)}, u32[]{:S(2)}, u32[]{:S(2)}) %all-to-all-start) | async-done | bytes 65568 | tf_op jit(solution)/shard_map/all_to_all | solution.py:89
  34.4 0.1 reshape.142
  34.5 0.2 copy.30
  34.8 0.8 copy-done.1
  35.7 0.7 collective-permute-start.10
  36.5 1.6 %collective-permute-start.8 = (bf16[2,1,8,1024]{3,2,0,1:T(8,128)(2,1)S(1)}, bf16[2,1,8,1024]{3,2,0,1:T(8,128)(2,1)S(1)}, u32[]{:S(2)}, u32[]{:S(2)}) collective-permute-start(bf16[2,1,8,1024]{3,2,0,1:T(8,128)(2,1)S(1)} %pad_maximum_fusion), channel_id=1, source_target_pairs={{0,16},{16,0},{1,17},{17,1},{2,18},{18,2},{3,19},{19,3},{4,20},{20... | collective-permute-start | bytes 98312 | tf_op jit(solution)/shard_map/ppermute | solution.py:18
  38.1 2.4 %collective-permute-done.8 = bf16[2,1,8,1024]{3,2,0,1:T(8,128)(2,1)S(1)} collective-permute-done((bf16[2,1,8,1024]{3,2,0,1:T(8,128)(2,1)S(1)}, bf16[2,1,8,1024]{3,2,0,1:T(8,128)(2,1)S(1)}, u32[]{:S(2)}, u32[]{:S(2)}) %collective-permute-start.8) | collective-permute-done | bytes 32800 | tf_op jit(solution)/shard_map/ppermute | solution.py:18
  40.5 1.7 %collective-permute-done.10 = bf16[4,1,8,1024]{3,2,0,1:T(8,128)(2,1)S(1)} collective-permute-done((bf16[4,1,8,1024]{3,2,0,1:T(8,128)(2,1)S(1)}, bf16[4,1,8,1024]{3,2,0,1:T(8,128)(2,1)S(1)}, u32[]{:S(2)}, u32[]{:S(2)}) %collective-permute-start.10) | collective-permute-done | bytes 65568 | tf_op jit(solution)/shard_map/ppermute | solution.py:53
  42.2 0.2 fusion.9
  42.4 0.6 copy-done.2
  43.1 0.8 collective-permute-start.14
  43.9 3.6 %collective-permute-start.12 = (bf16[4,1,8,1024]{3,2,0,1:T(8,128)(2,1)S(1)}, bf16[4,1,8,1024]{3,2,0,1:T(8,128)(2,1)S(1)}, u32[]{:S(2)}, u32[]{:S(2)}) collective-permute-start(bf16[4,1,8,1024]{3,2,0,1:T(8,128)(2,1)S(1)} %get-tuple-element.8), channel_id=1, source_target_pairs={{0,4},{1,5},{2,6},{3,7},{4,0},{5,1},{6,2},{7,3},{8,12},{9,13},{10,... | collective-permute-start | bytes 196616 | tf_op jit(solution)/shard_map/ppermute | solution.py:18
  47.5 1.8 %collective-permute-done.16 = bf16[4,1,8,1024]{3,2,0,1:T(8,128)(2,1)S(1)} collective-permute-done((bf16[4,1,8,1024]{3,2,0,1:T(8,128)(2,1)S(1)}, bf16[4,1,8,1024]{3,2,0,1:T(8,128)(2,1)S(1)}, u32[]{:S(2)}, u32[]{:S(2)}) %collective-permute-start.16) | collective-permute-done | bytes 65568 | tf_op jit(solution)/shard_map/ppermute | solution.py:18
  49.3 0.3 collective-permute-start.17
  49.5 0.6 collective-permute-done.14
  50.2 1.2 %collective-permute-start.15 = (bf16[4,1,8,1024]{3,2,0,1:T(8,128)(2,1)S(1)}, bf16[4,1,8,1024]{3,2,0,1:T(8,128)(2,1)S(1)}, u32[]{:S(2)}, u32[]{:S(2)}) collective-permute-start(bf16[4,1,8,1024]{3,2,0,1:T(8,128)(2,1)S(1)} %collective-permute-done.14), channel_id=1, source_target_pairs={{0,2},{1,3},{2,0},{3,1},{4,6},{5,7},{6,4},{7,5},{8,10},{9,11},{10,... | collective-permute-start | bytes 196616 | tf_op jit(solution)/shard_map/ppermute | solution.py:18
  51.3 0.9 %collective-permute-start.13 = (bf16[4,1,8,1024]{3,2,0,1:T(8,128)(2,1)S(1)}, bf16[4,1,8,1024]{3,2,0,1:T(8,128)(2,1)S(1)}, u32[]{:S(2)}, u32[]{:S(2)}) collective-permute-start(bf16[4,1,8,1024]{3,2,0,1:T(8,128)(2,1)S(1)} %collective-permute-done.12), channel_id=1, source_target_pairs={{0,2},{1,3},{2,0},{3,1},{4,6},{5,7},{6,4},{7,5},{8,10},{9,11},{10,... | collective-permute-start | bytes 196616 | tf_op jit(solution)/shard_map/ppermute | solution.py:18
  52.2 3.4 %collective-permute-done.13 = bf16[4,1,8,1024]{3,2,0,1:T(8,128)(2,1)S(1)} collective-permute-done((bf16[4,1,8,1024]{3,2,0,1:T(8,128)(2,1)S(1)}, bf16[4,1,8,1024]{3,2,0,1:T(8,128)(2,1)S(1)}, u32[]{:S(2)}, u32[]{:S(2)}) %collective-permute-start.13) | collective-permute-done | bytes 65568 | tf_op jit(solution)/shard_map/ppermute | solution.py:18
  56.0 1.8 %collective-permute-done.18 = bf16[8,4,1,8,1024]{4,3,1,2,0:T(8,128)(2,1)S(1)} collective-permute-done((bf16[8,4,1,8,1024]{4,3,1,2,0:T(8,128)(2,1)S(1)}, bf16[8,4,1,8,1024]{4,3,1,2,0:T(8,128)(2,1)S(1)}, u32[]{:S(2)}, u32[]{:S(2)}) %collective-permute-start.18) | collective-permute-done | bytes 524320 | tf_op jit(solution)/shard_map/ppermute | solution.py:18
  58.0 0.8 fusion.41
  58.8 0.9 %fusion.3 = bf16[512,64]{0,1:T(8,128)(2,1)S(1)} fusion(f32[512,512]{0,1:T(8,128)S(1)} %fusion.41, bf16[512,1024]{1,0:T(8,128)(2,1)S(1)} %bitcast.105, bf16[1024,512]{1,0:T(8,128)(2,1)S(1)} %copy-done.4), kind=kOutput, calls=%fused_computation.5 | convolution fusion | flops 537362432 | bytes 3211264 | tf_op jit(solution)/shard_map/dot_general | solution.py:85
  59.8 0.1 reshape.143
  60.0 10.3 %all_to_all.10 = bf16[16,2,1024]{2,1,0:T(2,128)(2,1)S(1)} all-to-all(bf16[16,2,1024]{2,1,0:T(2,128)(2,1)S(1)} %reshape.143), channel_id=1, replica_groups=mesh['space'=2,'mom'=16] {'mom'}, dimensions={0} | all-to-all | bytes 131072 | tf_op jit(solution)/shard_map/all_to_all | solution.py:89
  70.3 0.1 reshape.144
  70.4 0.2 copy.34
  70.8 0.7 collective-permute-start.21
  71.7 1.6 %collective-permute-start.19 = (bf16[2,1,8,1024]{3,2,0,1:T(8,128)(2,1)S(1)}, bf16[2,1,8,1024]{3,2,0,1:T(8,128)(2,1)S(1)}, u32[]{:S(2)}, u32[]{:S(2)}) collective-permute-start(bf16[2,1,8,1024]{3,2,0,1:T(8,128)(2,1)S(1)} %pad_maximum_fusion.1), channel_id=1, source_target_pairs={{0,16},{16,0},{1,17},{17,1},{2,18},{18,2},{3,19},{19,3},{4,20},{20... | collective-permute-start | bytes 98312 | tf_op jit(solution)/shard_map/ppermute | solution.py:18
  73.2 2.4 %collective-permute-done.19 = bf16[2,1,8,1024]{3,2,0,1:T(8,128)(2,1)S(1)} collective-permute-done((bf16[2,1,8,1024]{3,2,0,1:T(8,128)(2,1)S(1)}, bf16[2,1,8,1024]{3,2,0,1:T(8,128)(2,1)S(1)}, u32[]{:S(2)}, u32[]{:S(2)}) %collective-permute-start.19) | collective-permute-done | bytes 32800 | tf_op jit(solution)/shard_map/ppermute | solution.py:18
  75.7 1.6 %collective-permute-done.21 = bf16[4,1,8,1024]{3,2,0,1:T(8,128)(2,1)S(1)} collective-permute-done((bf16[4,1,8,1024]{3,2,0,1:T(8,128)(2,1)S(1)}, bf16[4,1,8,1024]{3,2,0,1:T(8,128)(2,1)S(1)}, u32[]{:S(2)}, u32[]{:S(2)}) %collective-permute-start.21) | collective-permute-done | bytes 65568 | tf_op jit(solution)/shard_map/ppermute | solution.py:53
  77.3 0.2 fusion.20
  77.6 0.7 add_bitcast_fusion
  (95 shorter events, 2.0 us)
Async XLA Ops:
  0.0 20.8 %copy-start = (bf16[1024,512]{1,0:T(8,128)(2,1)S(1)}, bf16[1024,512]{1,0:T(8,128)(2,1)}, u32[]{:S(2)}) copy-start(bf16[1024,512]{1,0:T(8,128)(2,1)} %param.7) | copy-start | bytes 3145732
  1.0 7.5 %collective-permute-start.3 = (bf16[4,1,8,1024]{3,2,0,1:T(8,128)(2,1)S(1)}, bf16[4,1,8,1024]{3,2,0,1:T(8,128)(2,1)S(1)}, u32[]{:S(2)}, u32[]{:S(2)}) collective-permute-start(bf16[4,1,8,1024]{3,2,0,1:T(8,128)(2,1)S(1)} %bitcast.110), channel_id=1, source_target_pairs={{0,8},{1,9},{2,10},{3,11},{4,12},{5,13},{6,14},{7,15},{8,0},{9,1},... | collective-permute-start | bytes 196616 | tf_op jit(solution)/shard_map/ppermute | solution.py:18
  5.1 4.9 %collective-permute-start.1 = (bf16[4,1,8,1024]{3,2,0,1:T(8,128)(2,1)S(1)}, bf16[4,1,8,1024]{3,2,0,1:T(8,128)(2,1)S(1)}, u32[]{:S(2)}, u32[]{:S(2)}) collective-permute-start(bf16[4,1,8,1024]{3,2,0,1:T(8,128)(2,1)S(1)} %bitcast.111), channel_id=1, source_target_pairs={{0,4},{1,5},{2,6},{3,7},{4,0},{5,1},{6,2},{7,3},{8,12},{9,13},{10,... | collective-permute-start | bytes 196616 | tf_op jit(solution)/shard_map/ppermute | solution.py:18
  6.7 4.7 %collective-permute-start = (bf16[4,1,8,1024]{3,2,0,1:T(8,128)(2,1)S(1)}, bf16[4,1,8,1024]{3,2,0,1:T(8,128)(2,1)S(1)}, u32[]{:S(2)}, u32[]{:S(2)}) collective-permute-start(bf16[4,1,8,1024]{3,2,0,1:T(8,128)(2,1)S(1)} %bitcast.112), channel_id=1, source_target_pairs={{0,2},{1,3},{2,0},{3,1},{4,6},{5,7},{6,4},{7,5},{8,10},{9,11},{10,... | collective-permute-start | bytes 196616 | tf_op jit(solution)/shard_map/ppermute | solution.py:18
  8.2 6.1 %collective-permute-start.5 = (bf16[4,1,8,1024]{3,2,1,0:T(8,128)(2,1)S(1)}, bf16[4,1,8,1024]{3,2,1,0:T(8,128)(2,1)S(1)}, u32[]{:S(2)}, u32[]{:S(2)}) collective-permute-start(bf16[4,1,8,1024]{3,2,1,0:T(8,128)(2,1)S(1)} %get-tuple-element.12), channel_id=1, source_target_pairs={{0,12},{1,13},{2,14},{3,15},{4,8},{5,9},{6,10},{7,11},{8,4},{9,5},... | collective-permute-start | bytes 196616 | tf_op jit(solution)/shard_map/ppermute | solution.py:18
  8.5 6.4 %collective-permute-start.4 = (bf16[4,1,8,1024]{3,2,0,1:T(8,128)(2,1)S(1)}, bf16[4,1,8,1024]{3,2,0,1:T(8,128)(2,1)S(1)}, u32[]{:S(2)}, u32[]{:S(2)}) collective-permute-start(bf16[4,1,8,1024]{3,2,0,1:T(8,128)(2,1)S(1)} %collective-permute-done.3), channel_id=1, source_target_pairs={{0,2},{1,3},{2,0},{3,1},{4,6},{5,7},{6,4},{7,5},{8,10},{9,11},{10,... | collective-permute-start | bytes 196616 | tf_op jit(solution)/shard_map/ppermute | solution.py:18
  10.1 4.7 %collective-permute-start.2 = (bf16[4,1,8,1024]{3,2,0,1:T(8,128)(2,1)S(1)}, bf16[4,1,8,1024]{3,2,0,1:T(8,128)(2,1)S(1)}, u32[]{:S(2)}, u32[]{:S(2)}) collective-permute-start(bf16[4,1,8,1024]{3,2,0,1:T(8,128)(2,1)S(1)} %collective-permute-done.1), channel_id=1, source_target_pairs={{0,2},{1,3},{2,0},{3,1},{4,6},{5,7},{6,4},{7,5},{8,10},{9,11},{10,... | collective-permute-start | bytes 196616 | tf_op jit(solution)/shard_map/ppermute | solution.py:18
  14.3 4.3 %collective-permute-start.6 = (bf16[4,1,8,1024]{3,2,1,0:T(8,128)(2,1)S(1)}, bf16[4,1,8,1024]{3,2,1,0:T(8,128)(2,1)S(1)}, u32[]{:S(2)}, u32[]{:S(2)}) collective-permute-start(bf16[4,1,8,1024]{3,2,1,0:T(8,128)(2,1)S(1)} %collective-permute-done.5), channel_id=1, source_target_pairs={{0,2},{1,3},{2,0},{3,1},{4,6},{5,7},{6,4},{7,5},{8,10},{9,11},{10,... | collective-permute-start | bytes 196616 | tf_op jit(solution)/shard_map/ppermute | solution.py:18
  18.6 1.9 %collective-permute-start.7 = (bf16[8,4,1,8,1024]{4,3,1,2,0:T(8,128)(2,1)S(1)}, bf16[8,4,1,8,1024]{4,3,1,2,0:T(8,128)(2,1)S(1)}, u32[]{:S(2)}, u32[]{:S(2)}) collective-permute-start(bf16[8,4,1,8,1024]{4,3,1,2,0:T(8,128)(2,1)S(1)} %bitcast_dynamic-update-slice_fusion.17), channel_id=1, source_target_pairs={{0,1},{1,0},{2,3},{3,2},{4,5},{5,4},{6,7},{7,6},{8,9},{9,8},{10,11... | collective-permute-start | bytes 1572872 | tf_op jit(solution)/shard_map/ppermute | solution.py:18
  20.8 1.2 %copy-start.4 = (bf16[1024,512]{1,0:T(8,128)(2,1)S(1)}, bf16[1024,512]{1,0:T(8,128)(2,1)}, u32[]{:S(2)}) copy-start(bf16[1024,512]{1,0:T(8,128)(2,1)} %param.6) | copy-start | bytes 3145732
  23.8 3.6 %copy-start.3 = (f32[3,1024]{1,0:T(4,128)S(1)}, f32[3,1024]{1,0:T(4,128)}, u32[]{:S(2)}) copy-start(f32[3,1024]{1,0:T(4,128)} %param.8) | copy-start | bytes 36868
  23.9 10.5 %all-to-all-start = ((bf16[16,2,1024]{2,1,0:T(2,128)(2,1)}), bf16[16,2,1024]{2,1,0:T(2,128)(2,1)S(1)}, u32[]{:S(2)}, u32[]{:S(2)}) async-start(bf16[16,2,1024]{2,1,0:T(2,128)(2,1)} %reshape.141), calls=%async_computation | async-start | bytes 131072 | tf_op jit(solution)/shard_map/all_to_all | solution.py:89
  34.7 0.9 %copy-start.1 = (f32[4,1,8,1024]{3,2,1,0:T(8,128)S(1)}, f32[4,1,8,1024]{3,2,1,0:T(8,128)}, u32[]{:S(2)}) copy-start(f32[4,1,8,1024]{3,2,1,0:T(8,128)} %param.5) | copy-start | bytes 393220
  35.6 4.9 %collective-permute-start.9 = (bf16[4,1,8,1024]{3,2,0,1:T(8,128)(2,1)S(1)}, bf16[4,1,8,1024]{3,2,0,1:T(8,128)(2,1)S(1)}, u32[]{:S(2)}, u32[]{:S(2)}) collective-permute-start(bf16[4,1,8,1024]{3,2,0,1:T(8,128)(2,1)S(1)} %get-tuple-element.9), channel_id=1, source_target_pairs={{0,1},{1,0},{2,3},{3,2},{4,5},{5,4},{6,7},{7,6},{8,9},{9,8},{10,11... | collective-permute-start | bytes 196616 | tf_op jit(solution)/shard_map/ppermute | solution.py:18
  35.7 6.5 %collective-permute-start.10 = (bf16[4,1,8,1024]{3,2,0,1:T(8,128)(2,1)S(1)}, bf16[4,1,8,1024]{3,2,0,1:T(8,128)(2,1)S(1)}, u32[]{:S(2)}, u32[]{:S(2)}) collective-permute-start(bf16[4,1,8,1024]{3,2,0,1:T(8,128)(2,1)S(1)} %get-tuple-element.9), channel_id=1, source_target_pairs={{0,15},{1,2},{2,1},{3,4},{4,3},{5,6},{6,5},{7,8},{8,7},{9,10},{10,... | collective-permute-start | bytes 196616 | tf_op jit(solution)/shard_map/ppermute | solution.py:53
  36.5 4.0 %collective-permute-start.8 = (bf16[2,1,8,1024]{3,2,0,1:T(8,128)(2,1)S(1)}, bf16[2,1,8,1024]{3,2,0,1:T(8,128)(2,1)S(1)}, u32[]{:S(2)}, u32[]{:S(2)}) collective-permute-start(bf16[2,1,8,1024]{3,2,0,1:T(8,128)(2,1)S(1)} %pad_maximum_fusion), channel_id=1, source_target_pairs={{0,16},{16,0},{1,17},{17,1},{2,18},{18,2},{3,19},{19,3},{4,20},{20... | collective-permute-start | bytes 98312 | tf_op jit(solution)/shard_map/ppermute | solution.py:18
  42.3 0.7 copy-start.2
  43.1 6.2 %collective-permute-start.16 = (bf16[4,1,8,1024]{3,2,0,1:T(8,128)(2,1)S(1)}, bf16[4,1,8,1024]{3,2,0,1:T(8,128)(2,1)S(1)}, u32[]{:S(2)}, u32[]{:S(2)}) collective-permute-start(bf16[4,1,8,1024]{3,2,0,1:T(8,128)(2,1)S(1)} %get-tuple-element.8), channel_id=1, source_target_pairs={{0,12},{1,13},{2,14},{3,15},{4,8},{5,9},{6,10},{7,11},{8,4},{9,5},... | collective-permute-start | bytes 196616 | tf_op jit(solution)/shard_map/ppermute | solution.py:18
  43.1 7.0 %collective-permute-start.14 = (bf16[4,1,8,1024]{3,2,0,1:T(8,128)(2,1)S(1)}, bf16[4,1,8,1024]{3,2,0,1:T(8,128)(2,1)S(1)}, u32[]{:S(2)}, u32[]{:S(2)}) collective-permute-start(bf16[4,1,8,1024]{3,2,0,1:T(8,128)(2,1)S(1)} %get-tuple-element.8), channel_id=1, source_target_pairs={{0,8},{1,9},{2,10},{3,11},{4,12},{5,13},{6,14},{7,15},{8,0},{9,1},... | collective-permute-start | bytes 196616 | tf_op jit(solution)/shard_map/ppermute | solution.py:18
  43.9 7.4 %collective-permute-start.12 = (bf16[4,1,8,1024]{3,2,0,1:T(8,128)(2,1)S(1)}, bf16[4,1,8,1024]{3,2,0,1:T(8,128)(2,1)S(1)}, u32[]{:S(2)}, u32[]{:S(2)}) collective-permute-start(bf16[4,1,8,1024]{3,2,0,1:T(8,128)(2,1)S(1)} %get-tuple-element.8), channel_id=1, source_target_pairs={{0,4},{1,5},{2,6},{3,7},{4,0},{5,1},{6,2},{7,3},{8,12},{9,13},{10,... | collective-permute-start | bytes 196616 | tf_op jit(solution)/shard_map/ppermute | solution.py:18
  47.5 4.7 %collective-permute-start.11 = (bf16[4,1,8,1024]{3,2,0,1:T(8,128)(2,1)S(1)}, bf16[4,1,8,1024]{3,2,0,1:T(8,128)(2,1)S(1)}, u32[]{:S(2)}, u32[]{:S(2)}) collective-permute-start(bf16[4,1,8,1024]{3,2,0,1:T(8,128)(2,1)S(1)} %get-tuple-element.8), channel_id=1, source_target_pairs={{0,2},{1,3},{2,0},{3,1},{4,6},{5,7},{6,4},{7,5},{8,10},{9,11},{10,... | collective-permute-start | bytes 196616 | tf_op jit(solution)/shard_map/ppermute | solution.py:18
  49.3 6.4 %collective-permute-start.17 = (bf16[4,1,8,1024]{3,2,0,1:T(8,128)(2,1)S(1)}, bf16[4,1,8,1024]{3,2,0,1:T(8,128)(2,1)S(1)}, u32[]{:S(2)}, u32[]{:S(2)}) collective-permute-start(bf16[4,1,8,1024]{3,2,0,1:T(8,128)(2,1)S(1)} %collective-permute-done.16), channel_id=1, source_target_pairs={{0,2},{1,3},{2,0},{3,1},{4,6},{5,7},{6,4},{7,5},{8,10},{9,11},{10,... | collective-permute-start | bytes 196616 | tf_op jit(solution)/shard_map/ppermute | solution.py:18
  50.2 5.5 %collective-permute-start.15 = (bf16[4,1,8,1024]{3,2,0,1:T(8,128)(2,1)S(1)}, bf16[4,1,8,1024]{3,2,0,1:T(8,128)(2,1)S(1)}, u32[]{:S(2)}, u32[]{:S(2)}) collective-permute-start(bf16[4,1,8,1024]{3,2,0,1:T(8,128)(2,1)S(1)} %collective-permute-done.14), channel_id=1, source_target_pairs={{0,2},{1,3},{2,0},{3,1},{4,6},{5,7},{6,4},{7,5},{8,10},{9,11},{10,... | collective-permute-start | bytes 196616 | tf_op jit(solution)/shard_map/ppermute | solution.py:18
  51.3 4.3 %collective-permute-start.13 = (bf16[4,1,8,1024]{3,2,0,1:T(8,128)(2,1)S(1)}, bf16[4,1,8,1024]{3,2,0,1:T(8,128)(2,1)S(1)}, u32[]{:S(2)}, u32[]{:S(2)}) collective-permute-start(bf16[4,1,8,1024]{3,2,0,1:T(8,128)(2,1)S(1)} %collective-permute-done.12), channel_id=1, source_target_pairs={{0,2},{1,3},{2,0},{3,1},{4,6},{5,7},{6,4},{7,5},{8,10},{9,11},{10,... | collective-permute-start | bytes 196616 | tf_op jit(solution)/shard_map/ppermute | solution.py:18
  55.7 2.0 %collective-permute-start.18 = (bf16[8,4,1,8,1024]{4,3,1,2,0:T(8,128)(2,1)S(1)}, bf16[8,4,1,8,1024]{4,3,1,2,0:T(8,128)(2,1)S(1)}, u32[]{:S(2)}, u32[]{:S(2)}) collective-permute-start(bf16[8,4,1,8,1024]{4,3,1,2,0:T(8,128)(2,1)S(1)} %bitcast_dynamic-update-slice_fusion.1), channel_id=1, source_target_pairs={{0,1},{1,0},{2,3},{3,2},{4,5},{5,4},{6,7},{7,6},{8,9},{9,8},{10,11... | collective-permute-start | bytes 1572872 | tf_op jit(solution)/shard_map/ppermute | solution.py:18
  70.8 4.9 %collective-permute-start.20 = (bf16[4,1,8,1024]{3,2,0,1:T(8,128)(2,1)S(1)}, bf16[4,1,8,1024]{3,2,0,1:T(8,128)(2,1)S(1)}, u32[]{:S(2)}, u32[]{:S(2)}) collective-permute-start(bf16[4,1,8,1024]{3,2,0,1:T(8,128)(2,1)S(1)} %get-tuple-element.5), channel_id=1, source_target_pairs={{0,1},{1,0},{2,3},{3,2},{4,5},{5,4},{6,7},{7,6},{8,9},{9,8},{10,11... | collective-permute-start | bytes 196616 | tf_op jit(solution)/shard_map/ppermute | solution.py:18
  70.8 6.5 %collective-permute-start.21 = (bf16[4,1,8,1024]{3,2,0,1:T(8,128)(2,1)S(1)}, bf16[4,1,8,1024]{3,2,0,1:T(8,128)(2,1)S(1)}, u32[]{:S(2)}, u32[]{:S(2)}) collective-permute-start(bf16[4,1,8,1024]{3,2,0,1:T(8,128)(2,1)S(1)} %get-tuple-element.5), channel_id=1, source_target_pairs={{0,15},{1,2},{2,1},{3,4},{4,3},{5,6},{6,5},{7,8},{8,7},{9,10},{10,... | collective-permute-start | bytes 196616 | tf_op jit(solution)/shard_map/ppermute | solution.py:53
  71.7 4.0 %collective-permute-start.19 = (bf16[2,1,8,1024]{3,2,0,1:T(8,128)(2,1)S(1)}, bf16[2,1,8,1024]{3,2,0,1:T(8,128)(2,1)S(1)}, u32[]{:S(2)}, u32[]{:S(2)}) collective-permute-start(bf16[2,1,8,1024]{3,2,0,1:T(8,128)(2,1)S(1)} %pad_maximum_fusion.1), channel_id=1, source_target_pairs={{0,16},{16,0},{1,17},{17,1},{2,18},{18,2},{3,19},{19,3},{4,20},{20... | collective-permute-start | bytes 98312 | tf_op jit(solution)/shard_map/ppermute | solution.py:18

commit v2 on v1

v2 whole, which is shorter than its diff:
```python
import functools

import jax
import jax.numpy as jnp
from jax import lax
from jax.experimental import pallas as pl
from jax.experimental.pallas import tpu as pltpu
from jax.sharding import PartitionSpec as P

P_SIZE = 1024
RANK = 8
NDIR = 16
ITERS = 2


collide_rate = 0.1
courant = 0.3


def swap(block, axis, bits):
    count = lax.axis_size(axis)
    return lax.ppermute(block, axis, [(i, i ^ bits) for i in range(count)])


def gathered(own, axis):
    count = lax.axis_size(axis)
    blocks = {0: own}
    for bits in range(4, count, 4):
        blocks[bits] = swap(own, axis, bits)
    for bits in range(0, count, 4):
        blocks[bits ^ 2] = swap(blocks[bits], axis, 2)
    return [blocks[2 * at].reshape(-1, own.shape[-1]) for at in range(count // 2)]


def collide_kernel(chips, *refs):
    blocks, factors = refs[:chips], refs[chips : chips + 4]
    sent_ref, beside_ref = refs[chips + 4 :]
    me = lax.axis_index("mom")
    core, chip = me & 1, me >> 1
    rows, columns = blocks[0].shape[0], factors[0].shape[1]
    width = columns // RANK
    step = min(columns, 256)
    states = jnp.concatenate([block[...] for block in blocks], axis=0)
    total = jnp.zeros((chips * rows, 2 * width), jnp.float32)
    for which in range(2):
        a_ref, b_ref = factors[2 * which : 2 * which + 2]
        first = (core ^ which) * width
        for at in range(0, columns, step):
            proj_a = jnp.dot(states, a_ref[:, at : at + step], preferred_element_type=jnp.float32)
            proj_b = jnp.dot(states, b_ref[:, at : at + step], preferred_element_type=jnp.float32)
            product = proj_a * proj_b
            high = product.astype(jnp.bfloat16)
            low = (product - high.astype(jnp.float32)).astype(jnp.bfloat16)
            source = lax.broadcasted_iota(jnp.int32, (step, 2 * width), 0) + at
            target = lax.broadcasted_iota(jnp.int32, (step, 2 * width), 1)
            adds = jnp.where((source >> 3) + first == target, 1.0, 0.0).astype(jnp.bfloat16)
            total += jnp.dot(high, adds, preferred_element_type=jnp.float32)
            total += jnp.dot(low, adds, preferred_element_type=jnp.float32)
    terms = total.astype(jnp.bfloat16)
    away = 2 * core - 1
    for at in range(chips):
        here = chip ^ at
        part = terms[at * rows : (at + 1) * rows]
        sent_ref[here, 0] = part
        sent_ref[(here + away) & (chips - 1), 1] = part

        @pl.when(here == ((chip - away) & (chips - 1)))
        def _():
            beside_ref[...] = blocks[at][...]


def collide(blocks, factors):
    chips, (rows, size) = len(blocks), blocks[0].shape
    columns = factors[0].shape[1]
    whole = pl.BlockSpec(memory_space=pltpu.VMEM)
    return pl.pallas_call(
        functools.partial(collide_kernel, chips),
        out_shape=(
            jax.ShapeDtypeStruct((chips, 2, rows, 2 * columns // RANK), jnp.bfloat16),
            jax.ShapeDtypeStruct((rows, size), jnp.bfloat16),
        ),
        in_specs=[whole] * (chips + 4),
        out_specs=(whole, whole),
        compiler_params=pltpu.CompilerParams(vmem_limit_bytes=16 << 20),
        cost_estimate=pl.CostEstimate(
            flops=8 * chips * rows * size * columns,
            bytes_accessed=2 * (chips * rows * size + 4 * size * columns),
            transcendentals=0,
        ),
    )(*blocks, *factors)


def x_halo(cells, axis, dtype):
    count = lax.axis_size(axis)
    size = cells.shape[0]
    head = cells[:1].astype(dtype)
    tail = cells[size - 1 :].astype(dtype)
    if count == 2:
        both = swap(jnp.concatenate([tail, head], axis=0), axis, 1)
        behind, ahead = both[:1], both[1:]
    else:
        behind = lax.ppermute(tail, axis, [(i, (i + 1) % count) for i in range(count)])
        ahead = lax.ppermute(head, axis, [((i + 1) % count, i) for i in range(count)])
    return behind.astype(cells.dtype), ahead.astype(cells.dtype)


def upwind(center, behind, beyond, speeds):
    return jnp.maximum(speeds, 0.0) * (center - behind) + jnp.minimum(speeds, 0.0) * (
        beyond - center
    )


def per_device(distribution, a_factor, b_factor, velocity, drift):
    layers, owned, depth, size = distribution.shape
    assert owned == 1
    chips = lax.axis_size("mom") // 2
    odd = lax.axis_index("mom") % 2 == 1
    same = [[c + 2 * k for k in range(chips)] for c in range(2)]
    factors = (a_factor, b_factor, swap(a_factor, "mom", 1), swap(b_factor, "mom", 1))
    state = distribution.reshape(layers, depth, size)
    for substep in range(ITERS):
        sent, beside = collide(gathered(state.astype(jnp.bfloat16), "mom"), factors)
        got = lax.all_to_all(
            sent, "mom", split_axis=0, concat_axis=0, tiled=True, axis_index_groups=same
        )
        got = jnp.moveaxis(got, 0, 2).reshape(2, layers, depth, size).astype(jnp.float32)
        collided = state + collide_rate * got[0]
        beside = beside.astype(jnp.float32).reshape(state.shape) + collide_rate * got[1]
        x_behind, x_ahead = x_halo(collided, "space", jnp.bfloat16)
        near, far = swap(jnp.stack([collided, beside]).astype(jnp.bfloat16), "mom", 1).astype(
            jnp.float32
        )
        y_behind = jnp.where(odd, near, far)
        y_ahead = jnp.where(odd, far, near)
        x_behind = jnp.concatenate([x_behind, collided[:-1]], axis=0)
        x_ahead = jnp.concatenate([collided[1:], x_ahead], axis=0)
        read = collided - courant * upwind(collided, x_behind, x_ahead, velocity[0])
        read = read - courant * upwind(collided, y_behind, y_ahead, velocity[1])
        read = read - courant * upwind(
            collided, jnp.roll(collided, 1, axis=1), jnp.roll(collided, -1, axis=1), velocity[2]
        )
        upper = jnp.concatenate(
            [read[..., NDIR:], jnp.zeros(read.shape[:2] + (NDIR,), jnp.float32)], axis=2
        )
        state = read + drift * (upper - read)
    return state.reshape(distribution.shape)


def solution(mesh):
    in_specs = (P("space", "mom", None, None), P(None, "mom"), P(None, "mom"), P(), P())
    out_specs = P("space", "mom", None, None)
    return jax.shard_map(
        per_device, mesh=mesh, in_specs=in_specs, out_specs=out_specs, check_vma=False
    )
```

time: 78.6 us -> 74 us (0.941)
  waiting for transfers between devices: 31.3 us -> 24.8 us
  Pallas kernels: 0 us -> 4.43 us
  matrix products: 3.4 us -> 0 us
  starting transfers between devices: 25.6 us -> 27 us
    pallas_call x0 -> x2, Pallas kernels: none -> 4.43 us  [collide(): pl.pallas_call(functools.partial(collide_kernel, chips), out_shape=(jax.S...]
    dot_general x4 -> x0, matrix products: 3.4 us -> none  [the longest x2 1.88 us: per_device(): proj_a = jnp.dot(rows_flat, a_factor, preferred_element_type=jnp.float32)]
    ppermute x2 -> x0, waiting for transfers between devices: 3.3 us -> none  [halo(): far = lax.ppermute(jnp.where(odd, tail, head), axis, pairs)]
    ppermute x20, waiting for transfers between devices: 21.1 us -> 18.2 us  [swap(): return lax.ppermute(block, axis, [(i, i ^ bits) for i in range(count)])]
    all_to_all x1, starting transfers between devices: 3.63 us -> 5.49 us  [per_device(): lax.all_to_all(sent, 'mom', split_axis=0, concat_axis=0, tiled=True, axis...]
    ppermute x2 -> x0, starting transfers between devices: 1.49 us -> none  [halo(): far = lax.ppermute(jnp.where(odd, tail, head), axis, pairs)]
    convert_element_type x2 -> x8, other arithmetic: 0.01 us -> 1.11 us  [the longest x2 1.02 us: per_device(): sent, beside = collide(gathered(state.astype(jnp.bfloat16), 'mom'), factors)]
    unnamed x2 -> x0, other arithmetic: 1.03 us -> none
  transfers between devices with their start and end apart: 23 -> 21, of which waited for: 13 -> 13; matrix products, arithmetic and copies ran while one was open for 1% -> 2% of each run, Pallas kernels for 0% -> 0%
where the time goes in v2:
time: 74 us; the launch traced here: 73.6 us
  starting transfers between devices  27 us (36%)
  waiting for transfers between devices  24.8 us (34%)
  blocking collectives  9.91 us (13%)
  local copies, waits for them, and re-layouts  4.8 us (6%)
  Pallas kernels  4.43 us (6%)
  other arithmetic  2.36 us (3%)
    ppermute x20, starting transfers between devices, swap(): return lax.ppermute(block, axis, [(i, i ^ bits) for i in range(count)])  21.5 us
    ppermute x20, waiting for transfers between devices, swap(): return lax.ppermute(block, axis, [(i, i ^ bits) for i in range(count)])  18.2 us
    all_to_all x1, blocking collectives, per_device(): lax.all_to_all(sent, 'mom', split_axis=0, concat_axis=0, tiled=True, axis...  9.91 us
    all_to_all x1, waiting for transfers between devices, per_device(): lax.all_to_all(sent, 'mom', split_axis=0, concat_axis=0, tiled=True, axis...  6.6 us
    all_to_all x1, starting transfers between devices, per_device(): lax.all_to_all(sent, 'mom', split_axis=0, concat_axis=0, tiled=True, axis...  5.49 us
    pallas_call x2, Pallas kernels, collide(): pl.pallas_call(functools.partial(collide_kernel, chips), out_shape=(jax.S...  4.43 us
    unnamed x14, local copies, waits for them, and re-layouts  4.03 us
  transfers between devices with their start and end apart: 21, of which 13 were waited for; matrix products, arithmetic and copies ran while one was open for 2% of the time, Pallas kernels for 0%

profile of v2, /device:TPU:0, one launch (start us, length us, event | category | flops | bytes accessed | tf_op | source)
XLA Modules:
  0.0 73.6 jit_solution(7829277818549698362)
XLA Ops:
  0.0 0.5 collective-permute-start.7
  0.5 1.0 %bitcast_convert_fusion = (bf16[4,8,1024]{2,1,0:T(8,128)(2,1)S(1)}, bf16[32,1024]{1,0:T(8,128)(2,1)S(1)}) fusion(f32[4,1,8,1024]{3,2,1,0:T(8,128)} %param.5), kind=kLoop, calls=%fused_computation.57 | loop fusion | flops 65536 | bytes 262144 | tf_op jit(solution)/shard_map/convert_element_type | solution.py:122
  1.5 5.1 %collective-permute-start.5 = (bf16[4,8,1024]{2,1,0:T(8,128)(2,1)S(1)}, bf16[4,8,1024]{2,1,0:T(8,128)(2,1)S(1)}, u32[]{:S(2)}, u32[]{:S(2)}) collective-permute-start(bf16[4,8,1024]{2,1,0:T(8,128)(2,1)S(1)} %get-tuple-element.33), channel_id=1, source_target_pairs={{0,12},{1,13},{2,14},{3,15},{4,8},{5,9},{6,10},{7,11},{8,4},{9,5},... | collective-permute-start | bytes 196616 | tf_op jit(solution)/shard_map/ppermute | solution.py:22
  6.7 0.6 collective-permute-start.1
  7.3 1.9 %collective-permute-done.5 = bf16[4,8,1024]{2,1,0:T(8,128)(2,1)S(1)} collective-permute-done((bf16[4,8,1024]{2,1,0:T(8,128)(2,1)S(1)}, bf16[4,8,1024]{2,1,0:T(8,128)(2,1)S(1)}, u32[]{:S(2)}, u32[]{:S(2)}) %collective-permute-start.5) | collective-permute-done | bytes 65568 | tf_op jit(solution)/shard_map/ppermute | solution.py:22
  9.2 1.7 %collective-permute-start = (bf16[4,8,1024]{2,1,0:T(8,128)(2,1)S(1)}, bf16[4,8,1024]{2,1,0:T(8,128)(2,1)S(1)}, u32[]{:S(2)}, u32[]{:S(2)}) collective-permute-start(bf16[4,8,1024]{2,1,0:T(8,128)(2,1)S(1)} %get-tuple-element.33), channel_id=1, source_target_pairs={{0,2},{1,3},{2,0},{3,1},{4,6},{5,7},{6,4},{7,5},{8,10},{9,11},{10,... | collective-permute-start | bytes 196616 | tf_op jit(solution)/shard_map/ppermute | solution.py:22
  10.9 1.5 %collective-permute-done.3 = bf16[4,8,1024]{2,1,0:T(8,128)(2,1)S(1)} collective-permute-done((bf16[4,8,1024]{2,1,0:T(8,128)(2,1)S(1)}, bf16[4,8,1024]{2,1,0:T(8,128)(2,1)S(1)}, u32[]{:S(2)}, u32[]{:S(2)}) %collective-permute-start.3) | collective-permute-done | bytes 65568 | tf_op jit(solution)/shard_map/ppermute | solution.py:22
  12.4 1.5 %collective-permute-start.6 = (bf16[4,8,1024]{2,1,0:T(8,128)(2,1)S(1)}, bf16[4,8,1024]{2,1,0:T(8,128)(2,1)S(1)}, u32[]{:S(2)}, u32[]{:S(2)}) collective-permute-start(bf16[4,8,1024]{2,1,0:T(8,128)(2,1)S(1)} %collective-permute-done.5), channel_id=1, source_target_pairs={{0,2},{1,3},{2,0},{3,1},{4,6},{5,7},{6,4},{7,5},{8,10},{9,11},{10,... | collective-permute-start | bytes 196616 | tf_op jit(solution)/shard_map/ppermute | solution.py:22
  13.9 0.5 collective-permute-start.4
  14.5 1.5 %collective-permute-start.2 = (bf16[4,8,1024]{2,1,0:T(8,128)(2,1)S(1)}, bf16[4,8,1024]{2,1,0:T(8,128)(2,1)S(1)}, u32[]{:S(2)}, u32[]{:S(2)}) collective-permute-start(bf16[4,8,1024]{2,1,0:T(8,128)(2,1)S(1)} %collective-permute-done.1), channel_id=1, source_target_pairs={{0,2},{1,3},{2,0},{3,1},{4,6},{5,7},{6,4},{7,5},{8,10},{9,11},{10,... | collective-permute-start | bytes 196616 | tf_op jit(solution)/shard_map/ppermute | solution.py:22
  16.0 1.4 %collective-permute-done.6 = bf16[4,8,1024]{2,1,0:T(8,128)(2,1)S(1)} collective-permute-done((bf16[4,8,1024]{2,1,0:T(8,128)(2,1)S(1)}, bf16[4,8,1024]{2,1,0:T(8,128)(2,1)S(1)}, u32[]{:S(2)}, u32[]{:S(2)}) %collective-permute-start.6) | collective-permute-done | bytes 65568 | tf_op jit(solution)/shard_map/ppermute | solution.py:22
  17.4 1.3 %collective-permute-done.4 = bf16[4,8,1024]{2,1,0:T(8,128)(2,1)S(1)} collective-permute-done((bf16[4,8,1024]{2,1,0:T(8,128)(2,1)S(1)}, bf16[4,8,1024]{2,1,0:T(8,128)(2,1)S(1)}, u32[]{:S(2)}, u32[]{:S(2)}) %collective-permute-start.4) | collective-permute-done | bytes 65568 | tf_op jit(solution)/shard_map/ppermute | solution.py:22
  18.7 0.7 collective-permute-done.2
  19.4 1.2 %copy-done = bf16[1024,512]{1,0:T(8,128)(2,1)S(1)} copy-done((bf16[1024,512]{1,0:T(8,128)(2,1)S(1)}, bf16[1024,512]{1,0:T(8,128)(2,1)}, u32[]{:S(2)}) %copy-start) | copy-done | bytes 1048600
  20.7 1.2 %copy-done.2 = bf16[1024,512]{1,0:T(8,128)(2,1)S(1)} copy-done((bf16[1024,512]{1,0:T(8,128)(2,1)S(1)}, bf16[1024,512]{1,0:T(8,128)(2,1)}, u32[]{:S(2)}) %copy-start.2) | copy-done | bytes 1048600
  21.9 2.5 %shard_map.55 = (bf16[8,2,32,128]{3,2,1,0:T(8,128)(2,1)}, bf16[32,1024]{1,0:T(8,128)(2,1)S(1)}) custom-call(bf16[32,1024]{1,0:T(8,128)(2,1)S(1)} %get-tuple-element.34.refs_0_, bf16[32,1024]{1,0:T(8,128)(2,1)S(1)} %bitcast.91, bf16[32,1024]{1,0:T(8,128)(2,1)S(1)} %bitcast.88, bf16[32,1024]{1,0:T(8,128)(2,1)S(1)} %bitcast.98, bf16[32,1024]{1,0:T(8,128)(2,1)S(1)} %bitcast.87, ...), custom_call_target="tpu_custom_call" | custom-call | flops 1073741824 | bytes 4718592 | tf_op jit(solution)/shard_map/pallas_call | solution.py:76
  24.4 5.5 %all-to-all-start = ((bf16[8,2,32,128]{3,2,1,0:T(8,128)(2,1)}), bf16[8,2,32,128]{3,2,1,0:T(8,128)(2,1)S(1)}, u32[]{:S(2)}, u32[]{:S(2)}) async-start(bf16[8,2,32,128]{3,2,1,0:T(8,128)(2,1)} %get-tuple-element.9), calls=%async_computation | async-start | bytes 262144 | tf_op jit(solution)/shard_map/all_to_all | solution.py:123
  29.9 0.7 copy-done.6
  30.7 6.6 %all-to-all-done = bf16[8,2,32,128]{3,2,1,0:T(8,128)(2,1)S(1)} async-done(((bf16[8,2,32,128]{3,2,1,0:T(8,128)(2,1)}), bf16[8,2,32,128]{3,2,1,0:T(8,128)(2,1)S(1)}, u32[]{:S(2)}, u32[]{:S(2)}) %all-to-all-start) | async-done | bytes 131104 | tf_op jit(solution)/shard_map/all_to_all | solution.py:123
  37.3 0.1 copy.7
  37.4 0.1 copy.6
  37.6 0.9 %copy-done.4 = f32[4,1,8,1024]{3,2,1,0:T(8,128)S(1)} copy-done((f32[4,1,8,1024]{3,2,1,0:T(8,128)S(1)}, f32[4,1,8,1024]{3,2,1,0:T(8,128)}, u32[]{:S(2)}) %copy-start.4) | copy-done | bytes 131096
  38.5 0.1 copy.9
  38.6 1.6 %collective-permute-start.9 = (bf16[2,8,1024]{2,1,0:T(8,128)(2,1)S(1)}, bf16[2,8,1024]{2,1,0:T(8,128)(2,1)S(1)}, u32[]{:S(2)}, u32[]{:S(2)}) collective-permute-start(bf16[2,8,1024]{2,1,0:T(8,128)(2,1)S(1)} %pad_maximum_fusion.2), channel_id=1, source_target_pairs={{0,16},{16,0},{1,17},{17,1},{2,18},{18,2},{3,19},{19,3},{4,20},{20... | collective-permute-start | bytes 98312 | tf_op jit(solution)/shard_map/ppermute | solution.py:22
  40.4 2.3 %collective-permute-done.9 = bf16[2,8,1024]{2,1,0:T(8,128)(2,1)S(1)} collective-permute-done((bf16[2,8,1024]{2,1,0:T(8,128)(2,1)S(1)}, bf16[2,8,1024]{2,1,0:T(8,128)(2,1)S(1)}, u32[]{:S(2)}, u32[]{:S(2)}) %collective-permute-start.9) | collective-permute-done | bytes 32800 | tf_op jit(solution)/shard_map/ppermute | solution.py:22
  42.7 0.2 fusion.5
  42.8 0.1 slice.143
  43.0 0.6 collective-permute-start.16
  43.6 0.8 %collective-permute-start.14 = (bf16[4,8,1024]{2,1,0:T(8,128)(2,1)S(1)}, bf16[4,8,1024]{2,1,0:T(8,128)(2,1)S(1)}, u32[]{:S(2)}, u32[]{:S(2)}) collective-permute-start(bf16[4,8,1024]{2,1,0:T(8,128)(2,1)S(1)} %fusion.34), channel_id=1, source_target_pairs={{0,8},{1,9},{2,10},{3,11},{4,12},{5,13},{6,14},{7,15},{8,0},{9,1},... | collective-permute-start | bytes 196616 | tf_op jit(solution)/shard_map/ppermute | solution.py:22
  44.4 3.1 %collective-permute-start.12 = (bf16[4,8,1024]{2,1,0:T(8,128)(2,1)S(1)}, bf16[4,8,1024]{2,1,0:T(8,128)(2,1)S(1)}, u32[]{:S(2)}, u32[]{:S(2)}) collective-permute-start(bf16[4,8,1024]{2,1,0:T(8,128)(2,1)S(1)} %fusion.34), channel_id=1, source_target_pairs={{0,4},{1,5},{2,6},{3,7},{4,0},{5,1},{6,2},{7,3},{8,12},{9,13},{10,... | collective-permute-start | bytes 196616 | tf_op jit(solution)/shard_map/ppermute | solution.py:22
  47.4 0.2 collective-permute-start.11
  47.6 1.9 %collective-permute-done.16 = bf16[4,8,1024]{2,1,0:T(8,128)(2,1)S(1)} collective-permute-done((bf16[4,8,1024]{2,1,0:T(8,128)(2,1)S(1)}, bf16[4,8,1024]{2,1,0:T(8,128)(2,1)S(1)}, u32[]{:S(2)}, u32[]{:S(2)}) %collective-permute-start.16) | collective-permute-done | bytes 65568 | tf_op jit(solution)/shard_map/ppermute | solution.py:22
  49.5 0.2 collective-permute-start.17
  49.7 1.1 %collective-permute-done.14 = bf16[4,8,1024]{2,1,0:T(8,128)(2,1)S(1)} collective-permute-done((bf16[4,8,1024]{2,1,0:T(8,128)(2,1)S(1)}, bf16[4,8,1024]{2,1,0:T(8,128)(2,1)S(1)}, u32[]{:S(2)}, u32[]{:S(2)}) %collective-permute-start.14) | collective-permute-done | bytes 65568 | tf_op jit(solution)/shard_map/ppermute | solution.py:22
  50.8 0.9 %collective-permute-start.15 = (bf16[4,8,1024]{2,1,0:T(8,128)(2,1)S(1)}, bf16[4,8,1024]{2,1,0:T(8,128)(2,1)S(1)}, u32[]{:S(2)}, u32[]{:S(2)}) collective-permute-start(bf16[4,8,1024]{2,1,0:T(8,128)(2,1)S(1)} %collective-permute-done.14), channel_id=1, source_target_pairs={{0,2},{1,3},{2,0},{3,1},{4,6},{5,7},{6,4},{7,5},{8,10},{9,11},{10,... | collective-permute-start | bytes 196616 | tf_op jit(solution)/shard_map/ppermute | solution.py:22
  51.8 1.1 %collective-permute-start.13 = (bf16[4,8,1024]{2,1,0:T(8,128)(2,1)S(1)}, bf16[4,8,1024]{2,1,0:T(8,128)(2,1)S(1)}, u32[]{:S(2)}, u32[]{:S(2)}) collective-permute-start(bf16[4,8,1024]{2,1,0:T(8,128)(2,1)S(1)} %collective-permute-done.12), channel_id=1, source_target_pairs={{0,2},{1,3},{2,0},{3,1},{4,6},{5,7},{6,4},{7,5},{8,10},{9,11},{10,... | collective-permute-start | bytes 196616 | tf_op jit(solution)/shard_map/ppermute | solution.py:22
  52.9 1.6 %collective-permute-done.17 = bf16[4,8,1024]{2,1,0:T(8,128)(2,1)S(1)} collective-permute-done((bf16[4,8,1024]{2,1,0:T(8,128)(2,1)S(1)}, bf16[4,8,1024]{2,1,0:T(8,128)(2,1)S(1)}, u32[]{:S(2)}, u32[]{:S(2)}) %collective-permute-start.17) | collective-permute-done | bytes 65568 | tf_op jit(solution)/shard_map/ppermute | solution.py:22
  54.5 1.2 %collective-permute-done.15 = bf16[4,8,1024]{2,1,0:T(8,128)(2,1)S(1)} collective-permute-done((bf16[4,8,1024]{2,1,0:T(8,128)(2,1)S(1)}, bf16[4,8,1024]{2,1,0:T(8,128)(2,1)S(1)}, u32[]{:S(2)}, u32[]{:S(2)}) %collective-permute-start.15) | collective-permute-done | bytes 65568 | tf_op jit(solution)/shard_map/ppermute | solution.py:22
  55.7 0.7 collective-permute-done.13
  56.4 1.9 %shard_map.56 = (bf16[8,2,32,128]{3,2,1,0:T(8,128)(2,1)S(1)}, bf16[32,1024]{1,0:T(8,128)(2,1)S(1)}) custom-call(bf16[32,1024]{1,0:T(8,128)(2,1)S(1)} %bitcast.85, bf16[32,1024]{1,0:T(8,128)(2,1)S(1)} %bitcast.93, bf16[32,1024]{1,0:T(8,128)(2,1)S(1)} %bitcast.92, bf16[32,1024]{1,0:T(8,128)(2,1)S(1)} %bitcast.99, bf16[32,1024]{1,0:T(8,128)(2,1)S(1)} %bitcast.90, ...), custom_call_target="tpu_custom_call" | custom-call | flops 1073741824 | bytes 4718592 | tf_op jit(solution)/shard_map/pallas_call | solution.py:76
  58.3 9.9 %all_to_all.10 = bf16[8,2,32,128]{3,2,1,0:T(8,128)(2,1)S(1)} all-to-all(bf16[8,2,32,128]{3,2,1,0:T(8,128)(2,1)S(1)} %get-tuple-element.11), channel_id=1, replica_groups={{0,2,4,6,8,10,12,14},{1,3,5,7,9,11,13,15},{16,18,20,22,24,26,28,30},{17..., dimensions={0} | all-to-all | bytes 262144 | tf_op jit(solution)/shard_map/all_to_all | solution.py:123
  68.3 0.1 copy.11
  68.6 0.1 copy.12
  68.7 1.4 %collective-permute-start.18 = (bf16[2,8,1024]{2,1,0:T(8,128)(2,1)S(1)}, bf16[2,8,1024]{2,1,0:T(8,128)(2,1)S(1)}, u32[]{:S(2)}, u32[]{:S(2)}) collective-permute-start(bf16[2,8,1024]{2,1,0:T(8,128)(2,1)S(1)} %pad_maximum_fusion.3), channel_id=1, source_target_pairs={{0,16},{16,0},{1,17},{17,1},{2,18},{18,2},{3,19},{19,3},{4,20},{20... | collective-permute-start | bytes 98312 | tf_op jit(solution)/shard_map/ppermute | solution.py:22
  70.2 2.5 %collective-permute-done.18 = bf16[2,8,1024]{2,1,0:T(8,128)(2,1)S(1)} collective-permute-done((bf16[2,8,1024]{2,1,0:T(8,128)(2,1)S(1)}, bf16[2,8,1024]{2,1,0:T(8,128)(2,1)S(1)}, u32[]{:S(2)}, u32[]{:S(2)}) %collective-permute-start.18) | collective-permute-done | bytes 32800 | tf_op jit(solution)/shard_map/ppermute | solution.py:22
  72.7 0.2 fusion.16
  72.9 0.1 slice.156
  73.0 0.7 add_bitcast_fusion
  (50 shorter events, 0.8 us)
Async XLA Ops:
  0.0 19.4 %collective-permute-start.7 = (bf16[1024,512]{1,0:T(8,128)(2,1)}, bf16[1024,512]{1,0:T(8,128)(2,1)S(1)}, u32[]{:S(2)}, u32[]{:S(2)}) collective-permute-start(bf16[1024,512]{1,0:T(8,128)(2,1)} %refs_8_.3), channel_id=1, source_target_pairs={{0,1},{1,0},{2,3},{3,2},{4,5},{5,4},{6,7},{7,6},{8,9},{9,8},{10,11... | collective-permute-start | bytes 3145736 | tf_op jit(solution)/shard_map/ppermute | solution.py:22
  0.5 18.9 %collective-permute-start.8 = (bf16[1024,512]{1,0:T(8,128)(2,1)}, bf16[1024,512]{1,0:T(8,128)(2,1)S(1)}, u32[]{:S(2)}, u32[]{:S(2)}) collective-permute-start(bf16[1024,512]{1,0:T(8,128)(2,1)} %refs_9_.3), channel_id=1, source_target_pairs={{0,1},{1,0},{2,3},{3,2},{4,5},{5,4},{6,7},{7,6},{8,9},{9,8},{10,11... | collective-permute-start | bytes 3145736 | tf_op jit(solution)/shard_map/ppermute | solution.py:22
  1.5 7.7 %collective-permute-start.5 = (bf16[4,8,1024]{2,1,0:T(8,128)(2,1)S(1)}, bf16[4,8,1024]{2,1,0:T(8,128)(2,1)S(1)}, u32[]{:S(2)}, u32[]{:S(2)}) collective-permute-start(bf16[4,8,1024]{2,1,0:T(8,128)(2,1)S(1)} %get-tuple-element.33), channel_id=1, source_target_pairs={{0,12},{1,13},{2,14},{3,15},{4,8},{5,9},{6,10},{7,11},{8,4},{9,5},... | collective-permute-start | bytes 196616 | tf_op jit(solution)/shard_map/ppermute | solution.py:22
  6.7 5.8 %collective-permute-start.3 = (bf16[4,8,1024]{2,1,0:T(8,128)(2,1)S(1)}, bf16[4,8,1024]{2,1,0:T(8,128)(2,1)S(1)}, u32[]{:S(2)}, u32[]{:S(2)}) collective-permute-start(bf16[4,8,1024]{2,1,0:T(8,128)(2,1)S(1)} %get-tuple-element.33), channel_id=1, source_target_pairs={{0,8},{1,9},{2,10},{3,11},{4,12},{5,13},{6,14},{7,15},{8,0},{9,1},... | collective-permute-start | bytes 196616 | tf_op jit(solution)/shard_map/ppermute | solution.py:22
  6.7 7.3 %collective-permute-start.1 = (bf16[4,8,1024]{2,1,0:T(8,128)(2,1)S(1)}, bf16[4,8,1024]{2,1,0:T(8,128)(2,1)S(1)}, u32[]{:S(2)}, u32[]{:S(2)}) collective-permute-start(bf16[4,8,1024]{2,1,0:T(8,128)(2,1)S(1)} %get-tuple-element.33), channel_id=1, source_target_pairs={{0,4},{1,5},{2,6},{3,7},{4,0},{5,1},{6,2},{7,3},{8,12},{9,13},{10,... | collective-permute-start | bytes 196616 | tf_op jit(solution)/shard_map/ppermute | solution.py:22
  9.2 5.3 %collective-permute-start = (bf16[4,8,1024]{2,1,0:T(8,128)(2,1)S(1)}, bf16[4,8,1024]{2,1,0:T(8,128)(2,1)S(1)}, u32[]{:S(2)}, u32[]{:S(2)}) collective-permute-start(bf16[4,8,1024]{2,1,0:T(8,128)(2,1)S(1)} %get-tuple-element.33), channel_id=1, source_target_pairs={{0,2},{1,3},{2,0},{3,1},{4,6},{5,7},{6,4},{7,5},{8,10},{9,11},{10,... | collective-permute-start | bytes 196616 | tf_op jit(solution)/shard_map/ppermute | solution.py:22
  12.4 5.0 %collective-permute-start.6 = (bf16[4,8,1024]{2,1,0:T(8,128)(2,1)S(1)}, bf16[4,8,1024]{2,1,0:T(8,128)(2,1)S(1)}, u32[]{:S(2)}, u32[]{:S(2)}) collective-permute-start(bf16[4,8,1024]{2,1,0:T(8,128)(2,1)S(1)} %collective-permute-done.5), channel_id=1, source_target_pairs={{0,2},{1,3},{2,0},{3,1},{4,6},{5,7},{6,4},{7,5},{8,10},{9,11},{10,... | collective-permute-start | bytes 196616 | tf_op jit(solution)/shard_map/ppermute | solution.py:22
  13.9 4.8 %collective-permute-start.4 = (bf16[4,8,1024]{2,1,0:T(8,128)(2,1)S(1)}, bf16[4,8,1024]{2,1,0:T(8,128)(2,1)S(1)}, u32[]{:S(2)}, u32[]{:S(2)}) collective-permute-start(bf16[4,8,1024]{2,1,0:T(8,128)(2,1)S(1)} %collective-permute-done.3), channel_id=1, source_target_pairs={{0,2},{1,3},{2,0},{3,1},{4,6},{5,7},{6,4},{7,5},{8,10},{9,11},{10,... | collective-permute-start | bytes 196616 | tf_op jit(solution)/shard_map/ppermute | solution.py:22
  14.5 5.0 %collective-permute-start.2 = (bf16[4,8,1024]{2,1,0:T(8,128)(2,1)S(1)}, bf16[4,8,1024]{2,1,0:T(8,128)(2,1)S(1)}, u32[]{:S(2)}, u32[]{:S(2)}) collective-permute-start(bf16[4,8,1024]{2,1,0:T(8,128)(2,1)S(1)} %collective-permute-done.1), channel_id=1, source_target_pairs={{0,2},{1,3},{2,0},{3,1},{4,6},{5,7},{6,4},{7,5},{8,10},{9,11},{10,... | collective-permute-start | bytes 196616 | tf_op jit(solution)/shard_map/ppermute | solution.py:22
  19.4 1.2 %copy-start = (bf16[1024,512]{1,0:T(8,128)(2,1)S(1)}, bf16[1024,512]{1,0:T(8,128)(2,1)}, u32[]{:S(2)}) copy-start(bf16[1024,512]{1,0:T(8,128)(2,1)} %refs_8_.3) | copy-start | bytes 3145732
  20.7 1.2 %copy-start.2 = (bf16[1024,512]{1,0:T(8,128)(2,1)S(1)}, bf16[1024,512]{1,0:T(8,128)(2,1)}, u32[]{:S(2)}) copy-start(bf16[1024,512]{1,0:T(8,128)(2,1)} %refs_9_.3) | copy-start | bytes 3145732
  24.4 12.8 %all-to-all-start = ((bf16[8,2,32,128]{3,2,1,0:T(8,128)(2,1)}), bf16[8,2,32,128]{3,2,1,0:T(8,128)(2,1)S(1)}, u32[]{:S(2)}, u32[]{:S(2)}) async-start(bf16[8,2,32,128]{3,2,1,0:T(8,128)(2,1)} %get-tuple-element.9), calls=%async_computation | async-start | bytes 262144 | tf_op jit(solution)/shard_map/all_to_all | solution.py:123
  29.9 0.7 copy-start.6
  37.5 0.9 %copy-start.4 = (f32[4,1,8,1024]{3,2,1,0:T(8,128)S(1)}, f32[4,1,8,1024]{3,2,1,0:T(8,128)}, u32[]{:S(2)}) copy-start(f32[4,1,8,1024]{3,2,1,0:T(8,128)} %param.5) | copy-start | bytes 393220
  38.6 4.0 %collective-permute-start.9 = (bf16[2,8,1024]{2,1,0:T(8,128)(2,1)S(1)}, bf16[2,8,1024]{2,1,0:T(8,128)(2,1)S(1)}, u32[]{:S(2)}, u32[]{:S(2)}) collective-permute-start(bf16[2,8,1024]{2,1,0:T(8,128)(2,1)S(1)} %pad_maximum_fusion.2), channel_id=1, source_target_pairs={{0,16},{16,0},{1,17},{17,1},{2,18},{18,2},{3,19},{19,3},{4,20},{20... | collective-permute-start | bytes 98312 | tf_op jit(solution)/shard_map/ppermute | solution.py:22
  40.2 2.7 %copy-start.5 = (f32[1024]{0:T(1024)S(1)}, f32[1024]{0:T(1024)}, u32[]{:S(2)}) copy-start(f32[1024]{0:T(1024)} %param.9) | copy-start | bytes 12292
  40.3 2.4 %collective-permute-start.10 = (bf16[2,4,8,1024]{3,2,1,0:T(8,128)(2,1)S(1)}, bf16[2,4,8,1024]{3,2,1,0:T(8,128)(2,1)S(1)}, u32[]{:S(2)}, u32[]{:S(2)}) collective-permute-start(bf16[2,4,8,1024]{3,2,1,0:T(8,128)(2,1)S(1)} %pad_maximum_fusion), channel_id=1, source_target_pairs={{0,1},{1,0},{2,3},{3,2},{4,5},{5,4},{6,7},{7,6},{8,9},{9,8},{10,11... | collective-permute-start | bytes 393224 | tf_op jit(solution)/shard_map/ppermute | solution.py:22
  42.6 13.8 %copy-start.1 = (bf16[1024,512]{1,0:T(8,128)(2,1)S(1)}, bf16[1024,512]{1,0:T(8,128)(2,1)}, u32[]{:S(2)}) copy-start(bf16[1024,512]{1,0:T(8,128)(2,1)} %refs_8_.3) | copy-start | bytes 3145732
  42.6 13.8 %copy-start.3 = (bf16[1024,512]{1,0:T(8,128)(2,1)S(1)}, bf16[1024,512]{1,0:T(8,128)(2,1)}, u32[]{:S(2)}) copy-start(bf16[1024,512]{1,0:T(8,128)(2,1)} %refs_9_.3) | copy-start | bytes 3145732
  43.0 6.5 %collective-permute-start.16 = (bf16[4,8,1024]{2,1,0:T(8,128)(2,1)S(1)}, bf16[4,8,1024]{2,1,0:T(8,128)(2,1)S(1)}, u32[]{:S(2)}, u32[]{:S(2)}) collective-permute-start(bf16[4,8,1024]{2,1,0:T(8,128)(2,1)S(1)} %fusion.34), channel_id=1, source_target_pairs={{0,12},{1,13},{2,14},{3,15},{4,8},{5,9},{6,10},{7,11},{8,4},{9,5},... | collective-permute-start | bytes 196616 | tf_op jit(solution)/shard_map/ppermute | solution.py:22
  43.6 7.2 %collective-permute-start.14 = (bf16[4,8,1024]{2,1,0:T(8,128)(2,1)S(1)}, bf16[4,8,1024]{2,1,0:T(8,128)(2,1)S(1)}, u32[]{:S(2)}, u32[]{:S(2)}) collective-permute-start(bf16[4,8,1024]{2,1,0:T(8,128)(2,1)S(1)} %fusion.34), channel_id=1, source_target_pairs={{0,8},{1,9},{2,10},{3,11},{4,12},{5,13},{6,14},{7,15},{8,0},{9,1},... | collective-permute-start | bytes 196616 | tf_op jit(solution)/shard_map/ppermute | solution.py:22
  44.4 7.4 %collective-permute-start.12 = (bf16[4,8,1024]{2,1,0:T(8,128)(2,1)S(1)}, bf16[4,8,1024]{2,1,0:T(8,128)(2,1)S(1)}, u32[]{:S(2)}, u32[]{:S(2)}) collective-permute-start(bf16[4,8,1024]{2,1,0:T(8,128)(2,1)S(1)} %fusion.34), channel_id=1, source_target_pairs={{0,4},{1,5},{2,6},{3,7},{4,0},{5,1},{6,2},{7,3},{8,12},{9,13},{10,... | collective-permute-start | bytes 196616 | tf_op jit(solution)/shard_map/ppermute | solution.py:22
  47.4 5.4 %collective-permute-start.11 = (bf16[4,8,1024]{2,1,0:T(8,128)(2,1)S(1)}, bf16[4,8,1024]{2,1,0:T(8,128)(2,1)S(1)}, u32[]{:S(2)}, u32[]{:S(2)}) collective-permute-start(bf16[4,8,1024]{2,1,0:T(8,128)(2,1)S(1)} %fusion.34), channel_id=1, source_target_pairs={{0,2},{1,3},{2,0},{3,1},{4,6},{5,7},{6,4},{7,5},{8,10},{9,11},{10,... | collective-permute-start | bytes 196616 | tf_op jit(solution)/shard_map/ppermute | solution.py:22
  49.5 5.0 %collective-permute-start.17 = (bf16[4,8,1024]{2,1,0:T(8,128)(2,1)S(1)}, bf16[4,8,1024]{2,1,0:T(8,128)(2,1)S(1)}, u32[]{:S(2)}, u32[]{:S(2)}) collective-permute-start(bf16[4,8,1024]{2,1,0:T(8,128)(2,1)S(1)} %collective-permute-done.16), channel_id=1, source_target_pairs={{0,2},{1,3},{2,0},{3,1},{4,6},{5,7},{6,4},{7,5},{8,10},{9,11},{10,... | collective-permute-start | bytes 196616 | tf_op jit(solution)/shard_map/ppermute | solution.py:22
  50.8 4.9 %collective-permute-start.15 = (bf16[4,8,1024]{2,1,0:T(8,128)(2,1)S(1)}, bf16[4,8,1024]{2,1,0:T(8,128)(2,1)S(1)}, u32[]{:S(2)}, u32[]{:S(2)}) collective-permute-start(bf16[4,8,1024]{2,1,0:T(8,128)(2,1)S(1)} %collective-permute-done.14), channel_id=1, source_target_pairs={{0,2},{1,3},{2,0},{3,1},{4,6},{5,7},{6,4},{7,5},{8,10},{9,11},{10,... | collective-permute-start | bytes 196616 | tf_op jit(solution)/shard_map/ppermute | solution.py:22
  51.8 4.7 %collective-permute-start.13 = (bf16[4,8,1024]{2,1,0:T(8,128)(2,1)S(1)}, bf16[4,8,1024]{2,1,0:T(8,128)(2,1)S(1)}, u32[]{:S(2)}, u32[]{:S(2)}) collective-permute-start(bf16[4,8,1024]{2,1,0:T(8,128)(2,1)S(1)} %collective-permute-done.12), channel_id=1, source_target_pairs={{0,2},{1,3},{2,0},{3,1},{4,6},{5,7},{6,4},{7,5},{8,10},{9,11},{10,... | collective-permute-start | bytes 196616 | tf_op jit(solution)/shard_map/ppermute | solution.py:22
  68.7 4.0 %collective-permute-start.18 = (bf16[2,8,1024]{2,1,0:T(8,128)(2,1)S(1)}, bf16[2,8,1024]{2,1,0:T(8,128)(2,1)S(1)}, u32[]{:S(2)}, u32[]{:S(2)}) collective-permute-start(bf16[2,8,1024]{2,1,0:T(8,128)(2,1)S(1)} %pad_maximum_fusion.3), channel_id=1, source_target_pairs={{0,16},{16,0},{1,17},{17,1},{2,18},{18,2},{3,19},{19,3},{4,20},{20... | collective-permute-start | bytes 98312 | tf_op jit(solution)/shard_map/ppermute | solution.py:22
  70.1 2.6 %collective-permute-start.19 = (bf16[2,4,8,1024]{3,2,1,0:T(8,128)(2,1)S(1)}, bf16[2,4,8,1024]{3,2,1,0:T(8,128)(2,1)S(1)}, u32[]{:S(2)}, u32[]{:S(2)}) collective-permute-start(bf16[2,4,8,1024]{3,2,1,0:T(8,128)(2,1)S(1)} %pad_maximum_fusion.1), channel_id=1, source_target_pairs={{0,1},{1,0},{2,3},{3,2},{4,5},{5,4},{6,7},{7,6},{8,9},{9,8},{10,11... | collective-permute-start | bytes 393224 | tf_op jit(solution)/shard_map/ppermute | solution.py:22

commit v3 on v2

--- a/solution.py
+++ b/solution.py
@@ -32,9 +32,75 @@
     return [blocks[2 * at].reshape(-1, own.shape[-1]) for at in range(count // 2)]
 
 
-def collide_kernel(chips, *refs):
+def off_chip(array):
+    return pltpu.with_memory_space_constraint(array, pltpu.MemorySpace.HBM)
+
+
+def prepare_kernel(
+    state_hbm, velocity_hbm, drift_hbm, state_ref, rounded_ref, tables_ref, velocity_ref, drift_ref, sems
+):
+    copies = [
+        pltpu.make_async_copy(source, target, sems.at[at])
+        for at, (source, target) in enumerate(
+            ((state_hbm, state_ref), (velocity_hbm, velocity_ref), (drift_hbm, drift_ref))
+        )
+    ]
+    for copy in copies:
+        copy.start()
+    for copy in copies:
+        copy.wait()
+    rounded_ref[...] = state_ref[...].astype(jnp.bfloat16)
+    for dim in range(3):
+        speeds = velocity_ref[dim : dim + 1, :]
+        tables_ref[2 * dim : 2 * dim + 1, :] = jnp.maximum(speeds, 0.0)
+        tables_ref[2 * dim + 1 : 2 * dim + 2, :] = jnp.minimum(speeds, 0.0)
+    tables_ref[6:7, :] = drift_ref[...]
+    tables_ref[7:8, :] = drift_ref[...]
+
+
+def prepare(state, velocity, drift):
+    hbm = pl.BlockSpec(memory_space=pltpu.MemorySpace.HBM)
+    whole = pl.BlockSpec(memory_space=pltpu.VMEM)
+    return pl.pallas_call(
+        prepare_kernel,
+        out_shape=(
+            jax.ShapeDtypeStruct(state.shape, jnp.float32),
+            jax.ShapeDtypeStruct(state.shape, jnp.bfloat16),
+            jax.ShapeDtypeStruct((8, state.shape[-1]), jnp.float32),
+        ),
+        in_specs=[hbm] * 3,
+        out_specs=(whole,) * 3,
+        scratch_shapes=[
+            pltpu.VMEM(velocity.shape, jnp.float32),
+            pltpu.VMEM((1, drift.shape[0]), jnp.float32),
+            pltpu.SemaphoreType.DMA((3,)),
+        ],
+        compiler_params=pltpu.CompilerParams(vmem_limit_bytes=8 << 20),
+        cost_estimate=pl.CostEstimate(
+            flops=state.size, bytes_accessed=10 * state.size, transcendentals=0
+        ),
+    )(*[off_chip(each) for each in (state, velocity, drift.reshape(1, -1))])
+
+
+def collide_kernel(chips, fetch, *refs):
     blocks, factors = refs[:chips], refs[chips : chips + 4]
-    sent_ref, beside_ref = refs[chips + 4 :]
+    sent_ref, beside_ref = refs[chips + 4 : chips + 6]
+    copies = []
+    kept = factors[:2]
+    if fetch:
+        kept, sems = refs[chips + 6 : chips + 8], refs[chips + 8]
+        part = kept[0].shape[0] // sems.shape[1]
+        copies = [
+            pltpu.make_async_copy(
+                source.at[at * part : (at + 1) * part],
+                target.at[at * part : (at + 1) * part],
+                sems.at[which, at],
+            )
+            for which, (source, target) in enumerate(zip(factors[:2], kept))
+            for at in range(sems.shape[1])
+        ]
+    for copy in copies:
+        copy.start()
     me = lax.axis_index("mom")
     core, chip = me & 1, me >> 1
     rows, columns = blocks[0].shape[0], factors[0].shape[1]
@@ -42,9 +108,11 @@
     step = min(columns, 256)
     states = jnp.concatenate([block[...] for block in blocks], axis=0)
     total = jnp.zeros((chips * rows, 2 * width), jnp.float32)
-    for which in range(2):
-        a_ref, b_ref = factors[2 * which : 2 * which + 2]
-        first = (core ^ which) * width
+    for other, (a_ref, b_ref) in ((1, factors[2:]), (0, kept)):
+        if not other:
+            for copy in copies:
+                copy.wait()
+        first = (core ^ other) * width
         for at in range(0, columns, step):
             proj_a = jnp.dot(states, a_ref[:, at : at + step], preferred_element_type=jnp.float32)
             proj_b = jnp.dot(states, b_ref[:, at : at + step], preferred_element_type=jnp.float32)
@@ -69,26 +137,28 @@
             beside_ref[...] = blocks[at][...]
 
 
-def collide(blocks, factors):
+def collide(blocks, factors, fetch):
     chips, (rows, size) = len(blocks), blocks[0].shape
     columns = factors[0].shape[1]
     whole = pl.BlockSpec(memory_space=pltpu.VMEM)
+    hbm = pl.BlockSpec(memory_space=pltpu.MemorySpace.HBM)
+    factor = pltpu.VMEM((size, columns), jnp.bfloat16)
     return pl.pallas_call(
-        functools.partial(collide_kernel, chips),
-        out_shape=(
+        functools.partial(collide_kernel, chips, fetch),
+        out_shape=[
             jax.ShapeDtypeStruct((chips, 2, rows, 2 * columns // RANK), jnp.bfloat16),
             jax.ShapeDtypeStruct((rows, size), jnp.bfloat16),
-        ),
-        in_specs=[whole] * (chips + 4),
-        out_specs=(whole, whole),
+        ],
+        in_specs=[whole] * chips + [hbm if fetch else whole] * 2 + [whole] * 2,
+        out_specs=[whole] * 2,
+        scratch_shapes=[factor, factor, pltpu.SemaphoreType.DMA((2, 4))] if fetch else [],
         compiler_params=pltpu.CompilerParams(vmem_limit_bytes=16 << 20),
         cost_estimate=pl.CostEstimate(
             flops=8 * chips * rows * size * columns,
             bytes_accessed=2 * (chips * rows * size + 4 * size * columns),
             transcendentals=0,
         ),
-    )(*blocks, *factors)
-
+    )(*blocks, *[off_chip(each) if fetch else each for each in factors[:2]], *factors[2:])
 
 def x_halo(cells, axis, dtype):
     count = lax.axis_size(axis)
@@ -105,9 +175,7 @@
 
 
 def upwind(center, behind, beyond, speeds):
-    return jnp.maximum(speeds, 0.0) * (center - behind) + jnp.minimum(speeds, 0.0) * (
-        beyond - center
-    )
+    return speeds[0] * (center - behind) + speeds[1] * (beyond - center)
 
 
 def per_device(distribution, a_factor, b_factor, velocity, drift):
@@ -117,9 +185,10 @@
     odd = lax.axis_index("mom") % 2 == 1
     same = [[c + 2 * k for k in range(chips)] for c in range(2)]
     factors = (a_factor, b_factor, swap(a_factor, "mom", 1), swap(b_factor, "mom", 1))
-    state = distribution.reshape(layers, depth, size)
+    state, rounded, tables = prepare(distribution.reshape(layers, depth, size), velocity, drift)
+    drift = tables[6]
     for substep in range(ITERS):
-        sent, beside = collide(gathered(state.astype(jnp.bfloat16), "mom"), factors)
+        sent, beside = collide(gathered(rounded, "mom"), factors, substep == 0)
         got = lax.all_to_all(
             sent, "mom", split_axis=0, concat_axis=0, tiled=True, axis_index_groups=same
         )
@@ -134,15 +203,16 @@
         y_ahead = jnp.where(odd, far, near)
         x_behind = jnp.concatenate([x_behind, collided[:-1]], axis=0)
         x_ahead = jnp.concatenate([collided[1:], x_ahead], axis=0)
-        read = collided - courant * upwind(collided, x_behind, x_ahead, velocity[0])
-        read = read - courant * upwind(collided, y_behind, y_ahead, velocity[1])
+        read = collided - courant * upwind(collided, x_behind, x_ahead, tables[0:2])
+        read = read - courant * upwind(collided, y_behind, y_ahead, tables[2:4])
         read = read - courant * upwind(
-            collided, jnp.roll(collided, 1, axis=1), jnp.roll(collided, -1, axis=1), velocity[2]
+            collided, jnp.roll(collided, 1, axis=1), jnp.roll(collided, -1, axis=1), tables[4:6]
         )
         upper = jnp.concatenate(
             [read[..., NDIR:], jnp.zeros(read.shape[:2] + (NDIR,), jnp.float32)], axis=2
         )
         state = read + drift * (upper - read)
+        rounded = state.astype(jnp.bfloat16)
     return state.reshape(distribution.shape)
 
 

time: 74 us -> 71.8 us (0.970)
  local copies, waits for them, and re-layouts: 4.8 us -> 0.72 us
  Pallas kernels: 4.43 us -> 6.75 us
  other arithmetic: 2.36 us -> 1.33 us
    unnamed x14 -> x4, local copies, waits for them, and re-layouts: 4.03 us -> 0.01 us
    pallas_call x2 -> x3, Pallas kernels: 4.43 us -> 6.75 us  [the longest x2 5.8 us: collide(): pl.pallas_call(functools.partial(collide_kernel, chips, fetch), out_shape...]
    convert_element_type x2 -> x1, other arithmetic: 1.02 us -> 0.02 us  [per_device(): rounded = state.astype(jnp.bfloat16)]
  transfers between devices with their start and end apart: 21 -> 21, of which waited for: 13 -> 13; matrix products, arithmetic and copies ran while one was open for 2% -> 0% of each run, Pallas kernels for 0% -> 1%
where the time goes in v3:
time: 71.8 us; the launch traced here: 71.5 us
  starting transfers between devices  27 us (38%)
  waiting for transfers between devices  25.5 us (36%)
  blocking collectives  9.91 us (14%)
  Pallas kernels  6.75 us (9%)
  other arithmetic  1.33 us (2%)
  local copies, waits for them, and re-layouts  0.72 us (1%)
    ppermute x20, starting transfers between devices, swap(): return lax.ppermute(block, axis, [(i, i ^ bits) for i in range(count)])  21.5 us
    ppermute x20, waiting for transfers between devices, swap(): return lax.ppermute(block, axis, [(i, i ^ bits) for i in range(count)])  18.2 us
    all_to_all x1, blocking collectives, per_device(): lax.all_to_all(sent, 'mom', split_axis=0, concat_axis=0, tiled=True, axis...  9.91 us
    all_to_all x1, waiting for transfers between devices, per_device(): lax.all_to_all(sent, 'mom', split_axis=0, concat_axis=0, tiled=True, axis...  7.32 us
    pallas_call x2, Pallas kernels, collide(): pl.pallas_call(functools.partial(collide_kernel, chips, fetch), out_shape...  5.8 us
    all_to_all x1, starting transfers between devices, per_device(): lax.all_to_all(sent, 'mom', split_axis=0, concat_axis=0, tiled=True, axis...  5.5 us
  transfers between devices with their start and end apart: 21, of which 13 were waited for; matrix products, arithmetic and copies ran while one was open for 0% of the time, Pallas kernels for 1%

profile of v3, /device:TPU:0, one launch (start us, length us, event | category | flops | bytes accessed | tf_op | source)
XLA Modules:
  0.0 71.5 jit_solution(2181415202109988882)
XLA Ops:
  0.0 0.5 collective-permute-start.7
  0.5 0.0 collective-permute-start.8
  0.5 0.9 %shard_map.55 = (f32[4,8,1024]{2,1,0:T(8,128)S(1)}, bf16[4,8,1024]{2,1,0:T(8,128)(2,1)S(1)}, f32[8,1024]{1,0:T(8,128)S(1)}) custom-call(f32[4,8,1024]{2,1,0:T(8,128)} %bitcast.99, f32[3,1024]{1,0:T(4,128)} %velocity_hbm.1, f32[1,1024]{1,0:T(1,128)} %bitcast.115), custom_call_target="tpu_custom_call" | custom-call | flops 32768 | bytes 327680 | tf_op jit(solution)/shard_map/pallas_call | solution.py:64
  1.5 5.1 %collective-permute-start.5 = (bf16[4,8,1024]{2,1,0:T(8,128)(2,1)S(1)}, bf16[4,8,1024]{2,1,0:T(8,128)(2,1)S(1)}, u32[]{:S(2)}, u32[]{:S(2)}) collective-permute-start(bf16[4,8,1024]{2,1,0:T(8,128)(2,1)S(1)} %get-tuple-element.13), channel_id=1, source_target_pairs={{0,12},{1,13},{2,14},{3,15},{4,8},{5,9},{6,10},{7,11},{8,4},{9,5},... | collective-permute-start | bytes 196616 | tf_op jit(solution)/shard_map/ppermute | solution.py:22
  6.6 0.0 collective-permute-start.3
  6.6 0.6 collective-permute-start.1
  7.2 1.9 %collective-permute-done.5 = bf16[4,8,1024]{2,1,0:T(8,128)(2,1)S(1)} collective-permute-done((bf16[4,8,1024]{2,1,0:T(8,128)(2,1)S(1)}, bf16[4,8,1024]{2,1,0:T(8,128)(2,1)S(1)}, u32[]{:S(2)}, u32[]{:S(2)}) %collective-permute-start.5) | collective-permute-done | bytes 65568 | tf_op jit(solution)/shard_map/ppermute | solution.py:22
  9.1 1.7 %collective-permute-start = (bf16[4,8,1024]{2,1,0:T(8,128)(2,1)S(1)}, bf16[4,8,1024]{2,1,0:T(8,128)(2,1)S(1)}, u32[]{:S(2)}, u32[]{:S(2)}) collective-permute-start(bf16[4,8,1024]{2,1,0:T(8,128)(2,1)S(1)} %get-tuple-element.13), channel_id=1, source_target_pairs={{0,2},{1,3},{2,0},{3,1},{4,6},{5,7},{6,4},{7,5},{8,10},{9,11},{10,... | collective-permute-start | bytes 196616 | tf_op jit(solution)/shard_map/ppermute | solution.py:22
  10.9 1.5 %collective-permute-done.3 = bf16[4,8,1024]{2,1,0:T(8,128)(2,1)S(1)} collective-permute-done((bf16[4,8,1024]{2,1,0:T(8,128)(2,1)S(1)}, bf16[4,8,1024]{2,1,0:T(8,128)(2,1)S(1)}, u32[]{:S(2)}, u32[]{:S(2)}) %collective-permute-start.3) | collective-permute-done | bytes 65568 | tf_op jit(solution)/shard_map/ppermute | solution.py:22
  12.4 1.5 %collective-permute-start.6 = (bf16[4,8,1024]{2,1,0:T(8,128)(2,1)S(1)}, bf16[4,8,1024]{2,1,0:T(8,128)(2,1)S(1)}, u32[]{:S(2)}, u32[]{:S(2)}) collective-permute-start(bf16[4,8,1024]{2,1,0:T(8,128)(2,1)S(1)} %collective-permute-done.5), channel_id=1, source_target_pairs={{0,2},{1,3},{2,0},{3,1},{4,6},{5,7},{6,4},{7,5},{8,10},{9,11},{10,... | collective-permute-start | bytes 196616 | tf_op jit(solution)/shard_map/ppermute | solution.py:22
  13.9 0.5 collective-permute-start.4
  14.4 1.5 %collective-permute-start.2 = (bf16[4,8,1024]{2,1,0:T(8,128)(2,1)S(1)}, bf16[4,8,1024]{2,1,0:T(8,128)(2,1)S(1)}, u32[]{:S(2)}, u32[]{:S(2)}) collective-permute-start(bf16[4,8,1024]{2,1,0:T(8,128)(2,1)S(1)} %collective-permute-done.1), channel_id=1, source_target_pairs={{0,2},{1,3},{2,0},{3,1},{4,6},{5,7},{6,4},{7,5},{8,10},{9,11},{10,... | collective-permute-start | bytes 196616 | tf_op jit(solution)/shard_map/ppermute | solution.py:22
  15.9 1.4 %collective-permute-done.6 = bf16[4,8,1024]{2,1,0:T(8,128)(2,1)S(1)} collective-permute-done((bf16[4,8,1024]{2,1,0:T(8,128)(2,1)S(1)}, bf16[4,8,1024]{2,1,0:T(8,128)(2,1)S(1)}, u32[]{:S(2)}, u32[]{:S(2)}) %collective-permute-start.6) | collective-permute-done | bytes 65568 | tf_op jit(solution)/shard_map/ppermute | solution.py:22
  17.3 1.3 %collective-permute-done.4 = bf16[4,8,1024]{2,1,0:T(8,128)(2,1)S(1)} collective-permute-done((bf16[4,8,1024]{2,1,0:T(8,128)(2,1)S(1)}, bf16[4,8,1024]{2,1,0:T(8,128)(2,1)S(1)}, u32[]{:S(2)}, u32[]{:S(2)}) %collective-permute-start.4) | collective-permute-done | bytes 65568 | tf_op jit(solution)/shard_map/ppermute | solution.py:22
  18.7 0.7 collective-permute-done.2
  19.4 3.9 %shard_map.56 = (bf16[8,2,32,128]{3,2,1,0:T(8,128)(2,1)}, bf16[32,1024]{1,0:T(8,128)(2,1)S(1)}) custom-call(bf16[32,1024]{1,0:T(8,128)(2,1)S(1)} %bitcast.80, bf16[32,1024]{1,0:T(8,128)(2,1)S(1)} %bitcast.87, bf16[32,1024]{1,0:T(8,128)(2,1)S(1)} %bitcast.84, bf16[32,1024]{1,0:T(8,128)(2,1)S(1)} %bitcast.93, bf16[32,1024]{1,0:T(8,128)(2,1)S(1)} %bitcast.82, ...), custom_call_target="tpu_custom_call" | custom-call | flops 1073741824 | bytes 4718592 | tf_op jit(solution)/shard_map/pallas_call | solution.py:146
  23.3 5.5 %all-to-all-start = ((bf16[8,2,32,128]{3,2,1,0:T(8,128)(2,1)}), bf16[8,2,32,128]{3,2,1,0:T(8,128)(2,1)S(1)}, u32[]{:S(2)}, u32[]{:S(2)}) async-start(bf16[8,2,32,128]{3,2,1,0:T(8,128)(2,1)} %get-tuple-element.14), calls=%async_computation | async-start | bytes 262144 | tf_op jit(solution)/shard_map/all_to_all | solution.py:192
  28.8 7.3 %all-to-all-done = bf16[8,2,32,128]{3,2,1,0:T(8,128)(2,1)S(1)} async-done(((bf16[8,2,32,128]{3,2,1,0:T(8,128)(2,1)}), bf16[8,2,32,128]{3,2,1,0:T(8,128)(2,1)S(1)}, u32[]{:S(2)}, u32[]{:S(2)}) %all-to-all-start) | async-done | bytes 131104 | tf_op jit(solution)/shard_map/all_to_all | solution.py:192
  36.2 0.1 copy.7
  36.5 0.1 copy.8
  36.6 1.6 %collective-permute-start.9 = (bf16[2,8,1024]{2,1,0:T(8,128)(2,1)S(1)}, bf16[2,8,1024]{2,1,0:T(8,128)(2,1)S(1)}, u32[]{:S(2)}, u32[]{:S(2)}) collective-permute-start(bf16[2,8,1024]{2,1,0:T(8,128)(2,1)S(1)} %pad_maximum_fusion.2), channel_id=1, source_target_pairs={{0,16},{16,0},{1,17},{17,1},{2,18},{18,2},{3,19},{19,3},{4,20},{20... | collective-permute-start | bytes 98312 | tf_op jit(solution)/shard_map/ppermute | solution.py:22
  38.2 0.1 collective-permute-start.10
  38.3 2.3 %collective-permute-done.9 = bf16[2,8,1024]{2,1,0:T(8,128)(2,1)S(1)} collective-permute-done((bf16[2,8,1024]{2,1,0:T(8,128)(2,1)S(1)}, bf16[2,8,1024]{2,1,0:T(8,128)(2,1)S(1)}, u32[]{:S(2)}, u32[]{:S(2)}) %collective-permute-start.9) | collective-permute-done | bytes 32800 | tf_op jit(solution)/shard_map/ppermute | solution.py:22
  40.6 0.0 copy-start.1
  40.6 0.2 fusion.5
  40.8 0.1 slice.174
  40.9 0.6 collective-permute-start.16
  41.5 0.8 %collective-permute-start.14 = (bf16[4,8,1024]{2,1,0:T(8,128)(2,1)S(1)}, bf16[4,8,1024]{2,1,0:T(8,128)(2,1)S(1)}, u32[]{:S(2)}, u32[]{:S(2)}) collective-permute-start(bf16[4,8,1024]{2,1,0:T(8,128)(2,1)S(1)} %fusion.33), channel_id=1, source_target_pairs={{0,8},{1,9},{2,10},{3,11},{4,12},{5,13},{6,14},{7,15},{8,0},{9,1},... | collective-permute-start | bytes 196616 | tf_op jit(solution)/shard_map/ppermute | solution.py:22
  42.3 3.1 %collective-permute-start.12 = (bf16[4,8,1024]{2,1,0:T(8,128)(2,1)S(1)}, bf16[4,8,1024]{2,1,0:T(8,128)(2,1)S(1)}, u32[]{:S(2)}, u32[]{:S(2)}) collective-permute-start(bf16[4,8,1024]{2,1,0:T(8,128)(2,1)S(1)} %fusion.33), channel_id=1, source_target_pairs={{0,4},{1,5},{2,6},{3,7},{4,0},{5,1},{6,2},{7,3},{8,12},{9,13},{10,... | collective-permute-start | bytes 196616 | tf_op jit(solution)/shard_map/ppermute | solution.py:22
  45.4 0.2 collective-permute-start.11
  45.6 1.8 %collective-permute-done.16 = bf16[4,8,1024]{2,1,0:T(8,128)(2,1)S(1)} collective-permute-done((bf16[4,8,1024]{2,1,0:T(8,128)(2,1)S(1)}, bf16[4,8,1024]{2,1,0:T(8,128)(2,1)S(1)}, u32[]{:S(2)}, u32[]{:S(2)}) %collective-permute-start.16) | collective-permute-done | bytes 65568 | tf_op jit(solution)/shard_map/ppermute | solution.py:22
  47.4 0.2 collective-permute-start.17
  47.6 1.2 %collective-permute-done.14 = bf16[4,8,1024]{2,1,0:T(8,128)(2,1)S(1)} collective-permute-done((bf16[4,8,1024]{2,1,0:T(8,128)(2,1)S(1)}, bf16[4,8,1024]{2,1,0:T(8,128)(2,1)S(1)}, u32[]{:S(2)}, u32[]{:S(2)}) %collective-permute-start.14) | collective-permute-done | bytes 65568 | tf_op jit(solution)/shard_map/ppermute | solution.py:22
  48.7 0.9 %collective-permute-start.15 = (bf16[4,8,1024]{2,1,0:T(8,128)(2,1)S(1)}, bf16[4,8,1024]{2,1,0:T(8,128)(2,1)S(1)}, u32[]{:S(2)}, u32[]{:S(2)}) collective-permute-start(bf16[4,8,1024]{2,1,0:T(8,128)(2,1)S(1)} %collective-permute-done.14), channel_id=1, source_target_pairs={{0,2},{1,3},{2,0},{3,1},{4,6},{5,7},{6,4},{7,5},{8,10},{9,11},{10,... | collective-permute-start | bytes 196616 | tf_op jit(solution)/shard_map/ppermute | solution.py:22
  49.6 1.1 %collective-permute-start.13 = (bf16[4,8,1024]{2,1,0:T(8,128)(2,1)S(1)}, bf16[4,8,1024]{2,1,0:T(8,128)(2,1)S(1)}, u32[]{:S(2)}, u32[]{:S(2)}) collective-permute-start(bf16[4,8,1024]{2,1,0:T(8,128)(2,1)S(1)} %collective-permute-done.12), channel_id=1, source_target_pairs={{0,2},{1,3},{2,0},{3,1},{4,6},{5,7},{6,4},{7,5},{8,10},{9,11},{10,... | collective-permute-start | bytes 196616 | tf_op jit(solution)/shard_map/ppermute | solution.py:22
  50.8 1.6 %collective-permute-done.17 = bf16[4,8,1024]{2,1,0:T(8,128)(2,1)S(1)} collective-permute-done((bf16[4,8,1024]{2,1,0:T(8,128)(2,1)S(1)}, bf16[4,8,1024]{2,1,0:T(8,128)(2,1)S(1)}, u32[]{:S(2)}, u32[]{:S(2)}) %collective-permute-start.17) | collective-permute-done | bytes 65568 | tf_op jit(solution)/shard_map/ppermute | solution.py:22
  52.4 1.2 %collective-permute-done.15 = bf16[4,8,1024]{2,1,0:T(8,128)(2,1)S(1)} collective-permute-done((bf16[4,8,1024]{2,1,0:T(8,128)(2,1)S(1)}, bf16[4,8,1024]{2,1,0:T(8,128)(2,1)S(1)}, u32[]{:S(2)}, u32[]{:S(2)}) %collective-permute-start.15) | collective-permute-done | bytes 65568 | tf_op jit(solution)/shard_map/ppermute | solution.py:22
  53.6 0.7 collective-permute-done.13
  54.3 1.9 %shard_map.57 = (bf16[8,2,32,128]{3,2,1,0:T(8,128)(2,1)S(1)}, bf16[32,1024]{1,0:T(8,128)(2,1)S(1)}) custom-call(bf16[32,1024]{1,0:T(8,128)(2,1)S(1)} %bitcast.79, bf16[32,1024]{1,0:T(8,128)(2,1)S(1)} %bitcast.88, bf16[32,1024]{1,0:T(8,128)(2,1)S(1)} %bitcast.86, bf16[32,1024]{1,0:T(8,128)(2,1)S(1)} %bitcast.94, bf16[32,1024]{1,0:T(8,128)(2,1)S(1)} %bitcast.85, ...), custom_call_target="tpu_custom_call" | custom-call | flops 1073741824 | bytes 4718592 | tf_op jit(solution)/shard_map/pallas_call | solution.py:146
  56.2 9.9 %all_to_all.10 = bf16[8,2,32,128]{3,2,1,0:T(8,128)(2,1)S(1)} all-to-all(bf16[8,2,32,128]{3,2,1,0:T(8,128)(2,1)S(1)} %get-tuple-element.17), channel_id=1, replica_groups={{0,2,4,6,8,10,12,14},{1,3,5,7,9,11,13,15},{16,18,20,22,24,26,28,30},{17..., dimensions={0} | all-to-all | bytes 262144 | tf_op jit(solution)/shard_map/all_to_all | solution.py:192
  66.2 0.1 copy.10
  66.4 0.1 copy.11
  66.6 1.4 %collective-permute-start.18 = (bf16[2,8,1024]{2,1,0:T(8,128)(2,1)S(1)}, bf16[2,8,1024]{2,1,0:T(8,128)(2,1)S(1)}, u32[]{:S(2)}, u32[]{:S(2)}) collective-permute-start(bf16[2,8,1024]{2,1,0:T(8,128)(2,1)S(1)} %pad_maximum_fusion.3), channel_id=1, source_target_pairs={{0,16},{16,0},{1,17},{17,1},{2,18},{18,2},{3,19},{19,3},{4,20},{20... | collective-permute-start | bytes 98312 | tf_op jit(solution)/shard_map/ppermute | solution.py:22
  68.0 0.1 collective-permute-start.19
  68.1 2.4 %collective-permute-done.18 = bf16[2,8,1024]{2,1,0:T(8,128)(2,1)S(1)} collective-permute-done((bf16[2,8,1024]{2,1,0:T(8,128)(2,1)S(1)}, bf16[2,8,1024]{2,1,0:T(8,128)(2,1)S(1)}, u32[]{:S(2)}, u32[]{:S(2)}) %collective-permute-start.18) | collective-permute-done | bytes 32800 | tf_op jit(solution)/shard_map/ppermute | solution.py:22
  70.6 0.2 fusion.16
  70.7 0.1 slice.187
  70.8 0.7 add_bitcast_fusion
  (39 shorter events, 0.5 us)
Async XLA Ops:
  0.0 19.4 %collective-permute-start.7 = (bf16[1024,512]{1,0:T(8,128)(2,1)}, bf16[1024,512]{1,0:T(8,128)(2,1)S(1)}, u32[]{:S(2)}, u32[]{:S(2)}) collective-permute-start(bf16[1024,512]{1,0:T(8,128)(2,1)} %refs_8_.3), channel_id=1, source_target_pairs={{0,1},{1,0},{2,3},{3,2},{4,5},{5,4},{6,7},{7,6},{8,9},{9,8},{10,11... | collective-permute-start | bytes 3145736 | tf_op jit(solution)/shard_map/ppermute | solution.py:22
  0.5 18.9 %collective-permute-start.8 = (bf16[1024,512]{1,0:T(8,128)(2,1)}, bf16[1024,512]{1,0:T(8,128)(2,1)S(1)}, u32[]{:S(2)}, u32[]{:S(2)}) collective-permute-start(bf16[1024,512]{1,0:T(8,128)(2,1)} %refs_9_.3), channel_id=1, source_target_pairs={{0,1},{1,0},{2,3},{3,2},{4,5},{5,4},{6,7},{7,6},{8,9},{9,8},{10,11... | collective-permute-start | bytes 3145736 | tf_op jit(solution)/shard_map/ppermute | solution.py:22
  1.5 7.7 %collective-permute-start.5 = (bf16[4,8,1024]{2,1,0:T(8,128)(2,1)S(1)}, bf16[4,8,1024]{2,1,0:T(8,128)(2,1)S(1)}, u32[]{:S(2)}, u32[]{:S(2)}) collective-permute-start(bf16[4,8,1024]{2,1,0:T(8,128)(2,1)S(1)} %get-tuple-element.13), channel_id=1, source_target_pairs={{0,12},{1,13},{2,14},{3,15},{4,8},{5,9},{6,10},{7,11},{8,4},{9,5},... | collective-permute-start | bytes 196616 | tf_op jit(solution)/shard_map/ppermute | solution.py:22
  6.6 5.8 %collective-permute-start.3 = (bf16[4,8,1024]{2,1,0:T(8,128)(2,1)S(1)}, bf16[4,8,1024]{2,1,0:T(8,128)(2,1)S(1)}, u32[]{:S(2)}, u32[]{:S(2)}) collective-permute-start(bf16[4,8,1024]{2,1,0:T(8,128)(2,1)S(1)} %get-tuple-element.13), channel_id=1, source_target_pairs={{0,8},{1,9},{2,10},{3,11},{4,12},{5,13},{6,14},{7,15},{8,0},{9,1},... | collective-permute-start | bytes 196616 | tf_op jit(solution)/shard_map/ppermute | solution.py:22
  6.6 7.3 %collective-permute-start.1 = (bf16[4,8,1024]{2,1,0:T(8,128)(2,1)S(1)}, bf16[4,8,1024]{2,1,0:T(8,128)(2,1)S(1)}, u32[]{:S(2)}, u32[]{:S(2)}) collective-permute-start(bf16[4,8,1024]{2,1,0:T(8,128)(2,1)S(1)} %get-tuple-element.13), channel_id=1, source_target_pairs={{0,4},{1,5},{2,6},{3,7},{4,0},{5,1},{6,2},{7,3},{8,12},{9,13},{10,... | collective-permute-start | bytes 196616 | tf_op jit(solution)/shard_map/ppermute | solution.py:22
  9.1 5.3 %collective-permute-start = (bf16[4,8,1024]{2,1,0:T(8,128)(2,1)S(1)}, bf16[4,8,1024]{2,1,0:T(8,128)(2,1)S(1)}, u32[]{:S(2)}, u32[]{:S(2)}) collective-permute-start(bf16[4,8,1024]{2,1,0:T(8,128)(2,1)S(1)} %get-tuple-element.13), channel_id=1, source_target_pairs={{0,2},{1,3},{2,0},{3,1},{4,6},{5,7},{6,4},{7,5},{8,10},{9,11},{10,... | collective-permute-start | bytes 196616 | tf_op jit(solution)/shard_map/ppermute | solution.py:22
  12.4 5.0 %collective-permute-start.6 = (bf16[4,8,1024]{2,1,0:T(8,128)(2,1)S(1)}, bf16[4,8,1024]{2,1,0:T(8,128)(2,1)S(1)}, u32[]{:S(2)}, u32[]{:S(2)}) collective-permute-start(bf16[4,8,1024]{2,1,0:T(8,128)(2,1)S(1)} %collective-permute-done.5), channel_id=1, source_target_pairs={{0,2},{1,3},{2,0},{3,1},{4,6},{5,7},{6,4},{7,5},{8,10},{9,11},{10,... | collective-permute-start | bytes 196616 | tf_op jit(solution)/shard_map/ppermute | solution.py:22
  13.9 4.8 %collective-permute-start.4 = (bf16[4,8,1024]{2,1,0:T(8,128)(2,1)S(1)}, bf16[4,8,1024]{2,1,0:T(8,128)(2,1)S(1)}, u32[]{:S(2)}, u32[]{:S(2)}) collective-permute-start(bf16[4,8,1024]{2,1,0:T(8,128)(2,1)S(1)} %collective-permute-done.3), channel_id=1, source_target_pairs={{0,2},{1,3},{2,0},{3,1},{4,6},{5,7},{6,4},{7,5},{8,10},{9,11},{10,... | collective-permute-start | bytes 196616 | tf_op jit(solution)/shard_map/ppermute | solution.py:22
  14.4 5.0 %collective-permute-start.2 = (bf16[4,8,1024]{2,1,0:T(8,128)(2,1)S(1)}, bf16[4,8,1024]{2,1,0:T(8,128)(2,1)S(1)}, u32[]{:S(2)}, u32[]{:S(2)}) collective-permute-start(bf16[4,8,1024]{2,1,0:T(8,128)(2,1)S(1)} %collective-permute-done.1), channel_id=1, source_target_pairs={{0,2},{1,3},{2,0},{3,1},{4,6},{5,7},{6,4},{7,5},{8,10},{9,11},{10,... | collective-permute-start | bytes 196616 | tf_op jit(solution)/shard_map/ppermute | solution.py:22
  23.3 12.8 %all-to-all-start = ((bf16[8,2,32,128]{3,2,1,0:T(8,128)(2,1)}), bf16[8,2,32,128]{3,2,1,0:T(8,128)(2,1)S(1)}, u32[]{:S(2)}, u32[]{:S(2)}) async-start(bf16[8,2,32,128]{3,2,1,0:T(8,128)(2,1)} %get-tuple-element.14), calls=%async_computation | async-start | bytes 262144 | tf_op jit(solution)/shard_map/all_to_all | solution.py:192
  36.6 4.0 %collective-permute-start.9 = (bf16[2,8,1024]{2,1,0:T(8,128)(2,1)S(1)}, bf16[2,8,1024]{2,1,0:T(8,128)(2,1)S(1)}, u32[]{:S(2)}, u32[]{:S(2)}) collective-permute-start(bf16[2,8,1024]{2,1,0:T(8,128)(2,1)S(1)} %pad_maximum_fusion.2), channel_id=1, source_target_pairs={{0,16},{16,0},{1,17},{17,1},{2,18},{18,2},{3,19},{19,3},{4,20},{20... | collective-permute-start | bytes 98312 | tf_op jit(solution)/shard_map/ppermute | solution.py:22
  38.2 2.4 %collective-permute-start.10 = (bf16[2,4,8,1024]{3,2,1,0:T(8,128)(2,1)S(1)}, bf16[2,4,8,1024]{3,2,1,0:T(8,128)(2,1)S(1)}, u32[]{:S(2)}, u32[]{:S(2)}) collective-permute-start(bf16[2,4,8,1024]{3,2,1,0:T(8,128)(2,1)S(1)} %pad_maximum_fusion), channel_id=1, source_target_pairs={{0,1},{1,0},{2,3},{3,2},{4,5},{5,4},{6,7},{7,6},{8,9},{9,8},{10,11... | collective-permute-start | bytes 393224 | tf_op jit(solution)/shard_map/ppermute | solution.py:22
  40.6 13.8 %copy-start = (bf16[1024,512]{1,0:T(8,128)(2,1)S(1)}, bf16[1024,512]{1,0:T(8,128)(2,1)}, u32[]{:S(2)}) copy-start(bf16[1024,512]{1,0:T(8,128)(2,1)} %refs_8_.3) | copy-start | bytes 3145732
  40.6 13.8 %copy-start.1 = (bf16[1024,512]{1,0:T(8,128)(2,1)S(1)}, bf16[1024,512]{1,0:T(8,128)(2,1)}, u32[]{:S(2)}) copy-start(bf16[1024,512]{1,0:T(8,128)(2,1)} %refs_9_.3) | copy-start | bytes 3145732
  40.9 6.5 %collective-permute-start.16 = (bf16[4,8,1024]{2,1,0:T(8,128)(2,1)S(1)}, bf16[4,8,1024]{2,1,0:T(8,128)(2,1)S(1)}, u32[]{:S(2)}, u32[]{:S(2)}) collective-permute-start(bf16[4,8,1024]{2,1,0:T(8,128)(2,1)S(1)} %fusion.33), channel_id=1, source_target_pairs={{0,12},{1,13},{2,14},{3,15},{4,8},{5,9},{6,10},{7,11},{8,4},{9,5},... | collective-permute-start | bytes 196616 | tf_op jit(solution)/shard_map/ppermute | solution.py:22
  41.5 7.2 %collective-permute-start.14 = (bf16[4,8,1024]{2,1,0:T(8,128)(2,1)S(1)}, bf16[4,8,1024]{2,1,0:T(8,128)(2,1)S(1)}, u32[]{:S(2)}, u32[]{:S(2)}) collective-permute-start(bf16[4,8,1024]{2,1,0:T(8,128)(2,1)S(1)} %fusion.33), channel_id=1, source_target_pairs={{0,8},{1,9},{2,10},{3,11},{4,12},{5,13},{6,14},{7,15},{8,0},{9,1},... | collective-permute-start | bytes 196616 | tf_op jit(solution)/shard_map/ppermute | solution.py:22
  42.3 7.3 %collective-permute-start.12 = (bf16[4,8,1024]{2,1,0:T(8,128)(2,1)S(1)}, bf16[4,8,1024]{2,1,0:T(8,128)(2,1)S(1)}, u32[]{:S(2)}, u32[]{:S(2)}) collective-permute-start(bf16[4,8,1024]{2,1,0:T(8,128)(2,1)S(1)} %fusion.33), channel_id=1, source_target_pairs={{0,4},{1,5},{2,6},{3,7},{4,0},{5,1},{6,2},{7,3},{8,12},{9,13},{10,... | collective-permute-start | bytes 196616 | tf_op jit(solution)/shard_map/ppermute | solution.py:22
  45.4 5.4 %collective-permute-start.11 = (bf16[4,8,1024]{2,1,0:T(8,128)(2,1)S(1)}, bf16[4,8,1024]{2,1,0:T(8,128)(2,1)S(1)}, u32[]{:S(2)}, u32[]{:S(2)}) collective-permute-start(bf16[4,8,1024]{2,1,0:T(8,128)(2,1)S(1)} %fusion.33), channel_id=1, source_target_pairs={{0,2},{1,3},{2,0},{3,1},{4,6},{5,7},{6,4},{7,5},{8,10},{9,11},{10,... | collective-permute-start | bytes 196616 | tf_op jit(solution)/shard_map/ppermute | solution.py:22
  47.4 5.0 %collective-permute-start.17 = (bf16[4,8,1024]{2,1,0:T(8,128)(2,1)S(1)}, bf16[4,8,1024]{2,1,0:T(8,128)(2,1)S(1)}, u32[]{:S(2)}, u32[]{:S(2)}) collective-permute-start(bf16[4,8,1024]{2,1,0:T(8,128)(2,1)S(1)} %collective-permute-done.16), channel_id=1, source_target_pairs={{0,2},{1,3},{2,0},{3,1},{4,6},{5,7},{6,4},{7,5},{8,10},{9,11},{10,... | collective-permute-start | bytes 196616 | tf_op jit(solution)/shard_map/ppermute | solution.py:22
  48.7 4.9 %collective-permute-start.15 = (bf16[4,8,1024]{2,1,0:T(8,128)(2,1)S(1)}, bf16[4,8,1024]{2,1,0:T(8,128)(2,1)S(1)}, u32[]{:S(2)}, u32[]{:S(2)}) collective-permute-start(bf16[4,8,1024]{2,1,0:T(8,128)(2,1)S(1)} %collective-permute-done.14), channel_id=1, source_target_pairs={{0,2},{1,3},{2,0},{3,1},{4,6},{5,7},{6,4},{7,5},{8,10},{9,11},{10,... | collective-permute-start | bytes 196616 | tf_op jit(solution)/shard_map/ppermute | solution.py:22
  49.6 4.7 %collective-permute-start.13 = (bf16[4,8,1024]{2,1,0:T(8,128)(2,1)S(1)}, bf16[4,8,1024]{2,1,0:T(8,128)(2,1)S(1)}, u32[]{:S(2)}, u32[]{:S(2)}) collective-permute-start(bf16[4,8,1024]{2,1,0:T(8,128)(2,1)S(1)} %collective-permute-done.12), channel_id=1, source_target_pairs={{0,2},{1,3},{2,0},{3,1},{4,6},{5,7},{6,4},{7,5},{8,10},{9,11},{10,... | collective-permute-start | bytes 196616 | tf_op jit(solution)/shard_map/ppermute | solution.py:22
  66.6 4.0 %collective-permute-start.18 = (bf16[2,8,1024]{2,1,0:T(8,128)(2,1)S(1)}, bf16[2,8,1024]{2,1,0:T(8,128)(2,1)S(1)}, u32[]{:S(2)}, u32[]{:S(2)}) collective-permute-start(bf16[2,8,1024]{2,1,0:T(8,128)(2,1)S(1)} %pad_maximum_fusion.3), channel_id=1, source_target_pairs={{0,16},{16,0},{1,17},{17,1},{2,18},{18,2},{3,19},{19,3},{4,20},{20... | collective-permute-start | bytes 98312 | tf_op jit(solution)/shard_map/ppermute | solution.py:22
  68.0 2.5 %collective-permute-start.19 = (bf16[2,4,8,1024]{3,2,1,0:T(8,128)(2,1)S(1)}, bf16[2,4,8,1024]{3,2,1,0:T(8,128)(2,1)S(1)}, u32[]{:S(2)}, u32[]{:S(2)}) collective-permute-start(bf16[2,4,8,1024]{3,2,1,0:T(8,128)(2,1)S(1)} %pad_maximum_fusion.1), channel_id=1, source_target_pairs={{0,1},{1,0},{2,3},{3,2},{4,5},{5,4},{6,7},{7,6},{8,9},{9,8},{10,11... | collective-permute-start | bytes 393224 | tf_op jit(solution)/shard_map/ppermute | solution.py:22

commit v4 on v3

--- a/solution.py
+++ b/solution.py
@@ -29,7 +29,7 @@
         blocks[bits] = swap(own, axis, bits)
     for bits in range(0, count, 4):
         blocks[bits ^ 2] = swap(blocks[bits], axis, 2)
-    return [blocks[2 * at].reshape(-1, own.shape[-1]) for at in range(count // 2)]
+    return [blocks[2 * at] for at in range(count // 2)]
 
 
 def off_chip(array):
@@ -82,33 +82,12 @@
     )(*[off_chip(each) for each in (state, velocity, drift.reshape(1, -1))])
 
 
-def collide_kernel(chips, fetch, *refs):
-    blocks, factors = refs[:chips], refs[chips : chips + 4]
-    sent_ref, beside_ref = refs[chips + 4 : chips + 6]
-    copies = []
-    kept = factors[:2]
-    if fetch:
-        kept, sems = refs[chips + 6 : chips + 8], refs[chips + 8]
-        part = kept[0].shape[0] // sems.shape[1]
-        copies = [
-            pltpu.make_async_copy(
-                source.at[at * part : (at + 1) * part],
-                target.at[at * part : (at + 1) * part],
-                sems.at[which, at],
-            )
-            for which, (source, target) in enumerate(zip(factors[:2], kept))
-            for at in range(sems.shape[1])
-        ]
-    for copy in copies:
-        copy.start()
-    me = lax.axis_index("mom")
-    core, chip = me & 1, me >> 1
-    rows, columns = blocks[0].shape[0], factors[0].shape[1]
+def project(states, core, partner, own, copies):
+    columns = partner[0].shape[1]
     width = columns // RANK
     step = min(columns, 256)
-    states = jnp.concatenate([block[...] for block in blocks], axis=0)
-    total = jnp.zeros((chips * rows, 2 * width), jnp.float32)
-    for other, (a_ref, b_ref) in ((1, factors[2:]), (0, kept)):
+    total = jnp.zeros((states.shape[0], 2 * width), jnp.float32)
+    for other, (a_ref, b_ref) in ((1, partner), (0, own)):
         if not other:
             for copy in copies:
                 copy.wait()
@@ -124,6 +103,37 @@
             adds = jnp.where((source >> 3) + first == target, 1.0, 0.0).astype(jnp.bfloat16)
             total += jnp.dot(high, adds, preferred_element_type=jnp.float32)
             total += jnp.dot(low, adds, preferred_element_type=jnp.float32)
+    return total
+
+
+def fetches(factors, kept, sems):
+    part = kept[0].shape[0] // sems.shape[1]
+    copies = [
+        pltpu.make_async_copy(
+            source.at[at * part : (at + 1) * part],
+            target.at[at * part : (at + 1) * part],
+            sems.at[which, at],
+        )
+        for which, (source, target) in enumerate(zip(factors, kept))
+        for at in range(sems.shape[1])
+    ]
+    for copy in copies:
+        copy.start()
+    return copies
+
+
+def collide_kernel(chips, fetch, *refs):
+    blocks, factors = refs[:chips], refs[chips : chips + 4]
+    sent_ref, beside_ref = refs[chips + 4 : chips + 6]
+    copies, kept = [], factors[:2]
+    if fetch:
+        kept = refs[chips + 6 : chips + 8]
+        copies = fetches(factors[:2], kept, refs[chips + 8])
+    me = lax.axis_index("mom")
+    core, chip = me & 1, me >> 1
+    rows = blocks[0].shape[0]
+    states = jnp.concatenate([block[...] for block in blocks], axis=0)
+    total = project(states, core, factors[2:], kept, copies)
     terms = total.astype(jnp.bfloat16)
     away = 2 * core - 1
     for at in range(chips):
@@ -159,6 +169,176 @@
             transcendentals=0,
         ),
     )(*blocks, *[off_chip(each) if fetch else each for each in factors[:2]], *factors[2:])
+
+def first_kernel(chips, layers, *refs):
+    blocks, factors = refs[:chips], refs[chips : chips + 4]
+    terms_ref, edges_ref, a_kept, b_kept, sems = refs[chips + 4 :]
+    kept = (a_kept, b_kept)
+    copies = fetches(factors[:2], kept, sems)
+    me = lax.axis_index("mom")
+    core, chip = me & 1, me >> 1
+    rows = blocks[0].shape[0]
+    depth = rows // layers
+    states = jnp.concatenate([block[...] for block in blocks], axis=0)
+    total = project(states, core, factors[2:], kept, copies)
+    mine = total.shape[1]
+    columns = pl.ds(pl.multiple_of(chip * mine, 128), mine)
+    for at in range(chips):
+        here = chip ^ at
+        terms = total[at * rows : (at + 1) * rows].astype(jnp.bfloat16)
+        terms_ref[here] = terms
+        collided = blocks[at][:, columns].astype(jnp.float32)
+        collided += collide_rate * terms.astype(jnp.float32)
+        edges = jnp.concatenate([collided[rows - depth :], collided[:depth]], axis=0)
+        edges_ref[here] = edges.astype(jnp.bfloat16)
+
+
+def first_collision(blocks, factors, layers):
+    chips, (rows, size) = len(blocks), blocks[0].shape
+    columns = factors[0].shape[1]
+    mine = 2 * columns // RANK
+    whole = pl.BlockSpec(memory_space=pltpu.VMEM)
+    hbm = pl.BlockSpec(memory_space=pltpu.MemorySpace.HBM)
+    factor = pltpu.VMEM((size, columns), jnp.bfloat16)
+    return pl.pallas_call(
+        functools.partial(first_kernel, chips, layers),
+        out_shape=[
+            jax.ShapeDtypeStruct((chips, rows, mine), jnp.bfloat16),
+            jax.ShapeDtypeStruct((chips, 2 * rows // layers, mine), jnp.bfloat16),
+        ],
+        in_specs=[whole] * chips + [hbm] * 2 + [whole] * 2,
+        out_specs=[whole] * 2,
+        scratch_shapes=[factor, factor, pltpu.SemaphoreType.DMA((2, 4))],
+        compiler_params=pltpu.CompilerParams(vmem_limit_bytes=16 << 20),
+        cost_estimate=pl.CostEstimate(
+            flops=8 * chips * rows * size * columns,
+            bytes_accessed=2 * (chips * rows * size + 4 * size * columns),
+            transcendentals=0,
+        ),
+    )(*blocks, *[off_chip(each) for each in factors[:2]], *factors[2:])
+
+
+def collided_kernel(chips, rows, state_ref, *refs):
+    blocks, parts = refs[:chips], refs[chips : 2 * chips]
+    exact_ref, edges_ref, rounded_ref = refs[2 * chips :]
+    chip = lax.axis_index("mom") >> 1
+    mine = parts[0].shape[2]
+    for source in range(chips):
+        columns = pl.ds(pl.multiple_of((chip ^ source) * mine, 128), mine)
+        for at in range(chips):
+            here = chip ^ at
+            part = parts[source][here].astype(jnp.float32)
+            if at:
+                state = blocks[at][:, columns].astype(jnp.float32)
+            else:
+                state = state_ref[:, columns]
+            collided = state + collide_rate * part[:rows]
+            exact_ref[here, :, columns] = collided
+            rounded_ref[here, :, columns] = collided.astype(jnp.bfloat16)
+            edges_ref[here, :, columns] = part[rows:]
+
+
+def collided_cells(state, blocks, parts):
+    chips, (rows, size) = len(blocks), blocks[0].shape
+    edge = parts[0].shape[1] - rows
+    return pl.pallas_call(
+        functools.partial(collided_kernel, chips, rows),
+        out_shape=[
+            jax.ShapeDtypeStruct((chips, rows, size), jnp.float32),
+            jax.ShapeDtypeStruct((chips, edge, size), jnp.float32),
+            jax.ShapeDtypeStruct((chips, rows, size), jnp.bfloat16),
+        ],
+        compiler_params=pltpu.CompilerParams(vmem_limit_bytes=16 << 20),
+        cost_estimate=pl.CostEstimate(
+            flops=2 * chips * rows * size, bytes_accessed=10 * chips * rows * size, transcendentals=0
+        ),
+    )(state, *blocks, *parts)
+
+
+def second_kernel(chips, layers, exact_ref, edges_ref, other_ref, tables_ref, *refs):
+    factors = refs[:4]
+    sent_ref, own_ref, beside_ref, read_ref, states_ref = refs[4:]
+    me = lax.axis_index("mom")
+    core, chip = me & 1, me >> 1
+    away = 2 * core - 1
+    _, rows, size = exact_ref.shape
+    depth = rows // layers
+    read_ref[:, size:] = jnp.zeros((rows, read_ref.shape[1] - size), jnp.float32)
+
+    @pl.loop(0, chips)
+    def _(cell):
+        before, after = (cell - 1 + core) & (chips - 1), (cell + core) & (chips - 1)
+        for at in range(0, size, 128):
+            lanes = slice(at, at + 128)
+            center = exact_ref[cell, :, lanes]
+            edges = edges_ref[cell, :, lanes]
+            behind = jnp.concatenate([edges[:depth], center[: rows - depth]], axis=0)
+            ahead = jnp.concatenate([center[depth:], edges[depth:]], axis=0)
+            read = center - courant * upwind(center, behind, ahead, tables_ref[0:2, lanes])
+            behind = other_ref[before, :, lanes].astype(jnp.float32)
+            ahead = other_ref[after, :, lanes].astype(jnp.float32)
+            read = read - courant * upwind(center, behind, ahead, tables_ref[2:4, lanes])
+            levels = center.reshape(layers, depth, 128)
+            behind = pltpu.roll(levels, 1, 1).reshape(rows, 128)
+            ahead = pltpu.roll(levels, depth - 1, 1).reshape(rows, 128)
+            read = read - courant * upwind(center, behind, ahead, tables_ref[4:6, lanes])
+            read_ref[:, lanes] = read
+        for at in range(0, size, 128):
+            lanes = slice(at, at + 128)
+            read = read_ref[:, lanes]
+            upper = read_ref[:, at + NDIR : at + NDIR + 128]
+            state = read + tables_ref[6:7, lanes] * (upper - read)
+            states_ref[cell, :, lanes] = state.astype(jnp.bfloat16)
+
+            @pl.when(cell == chip)
+            def _():
+                own_ref[:, lanes] = state
+
+            @pl.when(cell == ((chip - away) & (chips - 1)))
+            def _():
+                beside_ref[:, lanes] = state
+
+    states = states_ref[...].reshape(chips * rows, size)
+    terms = project(states, core, factors[2:], factors[:2], []).astype(jnp.bfloat16)
+    for here in range(chips):
+        part = terms[here * rows : (here + 1) * rows]
+        sent_ref[here, 0] = part
+        sent_ref[(here + away) & (chips - 1), 1] = part
+
+
+def second_collision(exact, edges, other, tables, factors, layers):
+    chips, rows, size = exact.shape
+    columns = factors[0].shape[1]
+    return pl.pallas_call(
+        functools.partial(second_kernel, chips, layers),
+        out_shape=[
+            jax.ShapeDtypeStruct((chips, 2, rows, 2 * columns // RANK), jnp.bfloat16),
+            jax.ShapeDtypeStruct((rows, size), jnp.float32),
+            jax.ShapeDtypeStruct((rows, size), jnp.float32),
+        ],
+        scratch_shapes=[
+            pltpu.VMEM((rows, size + 128), jnp.float32),
+            pltpu.VMEM((chips, rows, size), jnp.bfloat16),
+        ],
+        compiler_params=pltpu.CompilerParams(vmem_limit_bytes=16 << 20),
+        cost_estimate=pl.CostEstimate(
+            flops=8 * chips * rows * size * columns,
+            bytes_accessed=2 * (chips * rows * size + 4 * size * columns),
+            transcendentals=0,
+        ),
+    )(exact, edges, other, tables, *factors)
+
+
+def edge_layers(edges, axis):
+    count = lax.axis_size(axis)
+    if count == 2:
+        return swap(edges, axis, 1)
+    depth = edges.shape[1] // 2
+    last, first = edges[:, :depth], edges[:, depth:]
+    behind = lax.ppermute(last, axis, [(i, (i + 1) % count) for i in range(count)])
+    ahead = lax.ppermute(first, axis, [((i + 1) % count, i) for i in range(count)])
+    return jnp.concatenate([behind, ahead], axis=1)
+
 
 def x_halo(cells, axis, dtype):
     count = lax.axis_size(axis)
@@ -175,45 +355,62 @@
 
 
 def upwind(center, behind, beyond, speeds):
-    return speeds[0] * (center - behind) + speeds[1] * (beyond - center)
+    return speeds[0:1] * (center - behind) + speeds[1:2] * (beyond - center)
 
 
 def per_device(distribution, a_factor, b_factor, velocity, drift):
     layers, owned, depth, size = distribution.shape
     assert owned == 1
     chips = lax.axis_size("mom") // 2
+    factors = (a_factor, b_factor, swap(a_factor, "mom", 1), swap(b_factor, "mom", 1))
+    state, rounded, tables = prepare(distribution.reshape(layers * depth, size), velocity, drift)
+    if 2 * (a_factor.shape[1] // RANK) % 128:
+        for substep in range(ITERS):
+            sent, beside = collide(gathered(rounded, "mom"), factors, substep == 0)
+            state = settle(state, sent, beside.astype(jnp.float32), tables, layers)
+            rounded = state.astype(jnp.bfloat16)
+        return state.reshape(distribution.shape)
+    for substep in range(0, ITERS, 2):
+        blocks = gathered(rounded, "mom")
+        terms, edges = first_collision(blocks, factors, layers)
+        parts = gathered(jnp.concatenate([terms, edge_layers(edges, "space")], axis=1), "mom")
+        exact, edges, cells = collided_cells(state, blocks, parts)
+        other = swap(cells, "mom", 1)
+        sent, state, beside = second_collision(exact, edges, other, tables, factors, layers)
+        state = settle(state, sent, beside, tables, layers)
+        rounded = state.astype(jnp.bfloat16)
+    return state.reshape(distribution.shape)
+
+
+def settle(state, sent, beside, tables, layers):
+    rows, size = state.shape
+    shape = (layers, rows // layers, size)
+    chips = sent.shape[0]
     odd = lax.axis_index("mom") % 2 == 1
     same = [[c + 2 * k for k in range(chips)] for c in range(2)]
-    factors = (a_factor, b_factor, swap(a_factor, "mom", 1), swap(b_factor, "mom", 1))
-    state, rounded, tables = prepare(distribution.reshape(layers, depth, size), velocity, drift)
-    drift = tables[6]
-    for substep in range(ITERS):
-        sent, beside = collide(gathered(rounded, "mom"), factors, substep == 0)
-        got = lax.all_to_all(
-            sent, "mom", split_axis=0, concat_axis=0, tiled=True, axis_index_groups=same
-        )
-        got = jnp.moveaxis(got, 0, 2).reshape(2, layers, depth, size).astype(jnp.float32)
-        collided = state + collide_rate * got[0]
-        beside = beside.astype(jnp.float32).reshape(state.shape) + collide_rate * got[1]
-        x_behind, x_ahead = x_halo(collided, "space", jnp.bfloat16)
-        near, far = swap(jnp.stack([collided, beside]).astype(jnp.bfloat16), "mom", 1).astype(
-            jnp.float32
-        )
-        y_behind = jnp.where(odd, near, far)
-        y_ahead = jnp.where(odd, far, near)
-        x_behind = jnp.concatenate([x_behind, collided[:-1]], axis=0)
-        x_ahead = jnp.concatenate([collided[1:], x_ahead], axis=0)
-        read = collided - courant * upwind(collided, x_behind, x_ahead, tables[0:2])
-        read = read - courant * upwind(collided, y_behind, y_ahead, tables[2:4])
-        read = read - courant * upwind(
-            collided, jnp.roll(collided, 1, axis=1), jnp.roll(collided, -1, axis=1), tables[4:6]
-        )
-        upper = jnp.concatenate(
-            [read[..., NDIR:], jnp.zeros(read.shape[:2] + (NDIR,), jnp.float32)], axis=2
-        )
-        state = read + drift * (upper - read)
-        rounded = state.astype(jnp.bfloat16)
-    return state.reshape(distribution.shape)
+    got = lax.all_to_all(
+        sent, "mom", split_axis=0, concat_axis=0, tiled=True, axis_index_groups=same
+    )
+    got = jnp.moveaxis(got, 0, 2).reshape((2,) + shape).astype(jnp.float32)
+    collided = state.reshape(shape) + collide_rate * got[0]
+    beside = beside.reshape(shape) + collide_rate * got[1]
+    x_behind, x_ahead = x_halo(collided, "space", jnp.bfloat16)
+    near, far = swap(jnp.stack([collided, beside]).astype(jnp.bfloat16), "mom", 1).astype(
+        jnp.float32
+    )
+    y_behind = jnp.where(odd, near, far)
+    y_ahead = jnp.where(odd, far, near)
+    x_behind = jnp.concatenate([x_behind, collided[:-1]], axis=0)
+    x_ahead = jnp.concatenate([collided[1:], x_ahead], axis=0)
+    read = collided - courant * upwind(collided, x_behind, x_ahead, tables[0:2])
+    read = read - courant * upwind(collided, y_behind, y_ahead, tables[2:4])
+    read = read - courant * upwind(
+        collided, jnp.roll(collided, 1, axis=1), jnp.roll(collided, -1, axis=1), tables[4:6]
+    )
+    upper = jnp.concatenate(
+        [read[..., NDIR:], jnp.zeros(read.shape[:2] + (NDIR,), jnp.float32)], axis=2
+    )
+    return (read + tables[6] * (upper - read)).reshape(rows, size)
 
 
 def solution(mesh):

time: 71.8 us -> 72.2 us (level)
  Pallas kernels: 6.75 us -> 17.3 us
  blocking collectives: 9.91 us -> 0 us
    pallas_call x2 -> x3, Pallas kernels: 5.8 us -> 16.3 us  [the longest x1 12.6 us: second_collision(): pl.pallas_call(functools.partial(second_kernel, chips, layers), out_shape...]
    all_to_all x1 -> x0, blocking collectives: 9.91 us -> none  [per_device(): lax.all_to_all(sent, 'mom', split_axis=0, concat_axis=0, tiled=True, axis...]
    all_to_all x1, starting transfers between devices: 5.5 us -> 3.37 us  [settle(): lax.all_to_all(sent, 'mom', split_axis=0, concat_axis=0, tiled=True, axis...]
    ppermute x20, starting transfers between devices: 21.5 us -> 23.5 us  [swap(): return lax.ppermute(block, axis, [(i, i ^ bits) for i in range(count)])]
  transfers between devices with their start and end apart: 21 -> 21, of which waited for: 13 -> 12; matrix products, arithmetic and copies ran while one was open for 0% -> 0% of each run, Pallas kernels for 1% -> 1%
where the time goes in v4:
time: 72.2 us; the launch traced here: 72 us
  starting transfers between devices  26.8 us (37%)
  waiting for transfers between devices  26.1 us (36%)
  Pallas kernels  17.3 us (24%)
  other arithmetic  1.02 us (1%)
    ppermute x20, starting transfers between devices, swap(): return lax.ppermute(block, axis, [(i, i ^ bits) for i in range(count)])  23.5 us
    ppermute x20, waiting for transfers between devices, swap(): return lax.ppermute(block, axis, [(i, i ^ bits) for i in range(count)])  18.7 us
    pallas_call x1, Pallas kernels, second_collision(): pl.pallas_call(functools.partial(second_kernel, chips, layers), out_shape...  12.6 us
    all_to_all x1, waiting for transfers between devices, settle(): lax.all_to_all(sent, 'mom', split_axis=0, concat_axis=0, tiled=True, axis...  7.45 us
    all_to_all x1, starting transfers between devices, settle(): lax.all_to_all(sent, 'mom', split_axis=0, concat_axis=0, tiled=True, axis...  3.37 us
    pallas_call x1, Pallas kernels, first_collision(): pl.pallas_call(functools.partial(first_kernel, chips, layers), out_shape=...  3.23 us
  transfers between devices with their start and end apart: 21, of which 12 were waited for; matrix products, arithmetic and copies ran while one was open for 0% of the time, Pallas kernels for 1%

profile of v4, /device:TPU:0, one launch (start us, length us, event | category | flops | bytes accessed | tf_op | source)
XLA Modules:
  0.0 72.0 jit_solution(17734041574664170932)
XLA Ops:
  0.0 0.5 collective-permute-start.7
  0.5 0.0 collective-permute-start.8
  0.5 0.9 %shard_map.55 = (f32[32,1024]{1,0:T(8,128)S(1)}, bf16[32,1024]{1,0:T(8,128)(2,1)S(1)}, f32[8,1024]{1,0:T(8,128)S(1)}) custom-call(f32[32,1024]{1,0:T(8,128)} %bitcast.48, f32[3,1024]{1,0:T(4,128)} %velocity_hbm.1, f32[1,1024]{1,0:T(1,128)} %bitcast.56), custom_call_target="tpu_custom_call" | custom-call | flops 32768 | bytes 327680 | tf_op jit(solution)/shard_map/pallas_call | solution.py:64
  1.5 3.1 %collective-permute-start.1 = (bf16[32,1024]{1,0:T(8,128)(2,1)S(1)}, bf16[32,1024]{1,0:T(8,128)(2,1)S(1)}, u32[]{:S(2)}, u32[]{:S(2)}) collective-permute-start(bf16[32,1024]{1,0:T(8,128)(2,1)S(1)} %get-tuple-element.17.refs_0_), channel_id=1, source_target_pairs={{0,4},{1,5},{2,6},{3,7},{4,0},{5,1},{6,2},{7,3},{8,12},{9,13},{10,... | collective-permute-start | bytes 196616 | tf_op jit(solution)/shard_map/ppermute | solution.py:22
  4.6 2.6 %collective-permute-start.3 = (bf16[32,1024]{1,0:T(8,128)(2,1)S(1)}, bf16[32,1024]{1,0:T(8,128)(2,1)S(1)}, u32[]{:S(2)}, u32[]{:S(2)}) collective-permute-start(bf16[32,1024]{1,0:T(8,128)(2,1)S(1)} %get-tuple-element.17.refs_0_), channel_id=1, source_target_pairs={{0,8},{1,9},{2,10},{3,11},{4,12},{5,13},{6,14},{7,15},{8,0},{9,1},... | collective-permute-start | bytes 196616 | tf_op jit(solution)/shard_map/ppermute | solution.py:22
  7.2 0.0 collective-permute-start.5
  7.2 0.0 collective-permute-done.1.refs_2_
  7.2 1.7 %collective-permute-start = (bf16[32,1024]{1,0:T(8,128)(2,1)S(1)}, bf16[32,1024]{1,0:T(8,128)(2,1)S(1)}, u32[]{:S(2)}, u32[]{:S(2)}) collective-permute-start(bf16[32,1024]{1,0:T(8,128)(2,1)S(1)} %get-tuple-element.17.refs_0_), channel_id=1, source_target_pairs={{0,2},{1,3},{2,0},{3,1},{4,6},{5,7},{6,4},{7,5},{8,10},{9,11},{10,... | collective-permute-start | bytes 196616 | tf_op jit(solution)/shard_map/ppermute | solution.py:22
  8.9 3.1 %collective-permute-done.3.refs_4_ = bf16[32,1024]{1,0:T(8,128)(2,1)S(1)} collective-permute-done((bf16[32,1024]{1,0:T(8,128)(2,1)S(1)}, bf16[32,1024]{1,0:T(8,128)(2,1)S(1)}, u32[]{:S(2)}, u32[]{:S(2)}) %collective-permute-start.3) | collective-permute-done | bytes 65568 | tf_op jit(solution)/shard_map/ppermute | solution.py:22
  12.0 1.5 %collective-permute-start.2 = (bf16[32,1024]{1,0:T(8,128)(2,1)S(1)}, bf16[32,1024]{1,0:T(8,128)(2,1)S(1)}, u32[]{:S(2)}, u32[]{:S(2)}) collective-permute-start(bf16[32,1024]{1,0:T(8,128)(2,1)S(1)} %collective-permute-done.1.refs_2_), channel_id=1, source_target_pairs={{0,2},{1,3},{2,0},{3,1},{4,6},{5,7},{6,4},{7,5},{8,10},{9,11},{10,... | collective-permute-start | bytes 196616 | tf_op jit(solution)/shard_map/ppermute | solution.py:22
  13.6 0.0 collective-permute-done.5.refs_6_
  13.6 1.3 %collective-permute-start.4 = (bf16[32,1024]{1,0:T(8,128)(2,1)S(1)}, bf16[32,1024]{1,0:T(8,128)(2,1)S(1)}, u32[]{:S(2)}, u32[]{:S(2)}) collective-permute-start(bf16[32,1024]{1,0:T(8,128)(2,1)S(1)} %collective-permute-done.3.refs_4_), channel_id=1, source_target_pairs={{0,2},{1,3},{2,0},{3,1},{4,6},{5,7},{6,4},{7,5},{8,10},{9,11},{10,... | collective-permute-start | bytes 196616 | tf_op jit(solution)/shard_map/ppermute | solution.py:22
  14.9 0.0 collective-permute-done.refs_1_
  14.9 0.7 %collective-permute-start.6 = (bf16[32,1024]{1,0:T(8,128)(2,1)S(1)}, bf16[32,1024]{1,0:T(8,128)(2,1)S(1)}, u32[]{:S(2)}, u32[]{:S(2)}) collective-permute-start(bf16[32,1024]{1,0:T(8,128)(2,1)S(1)} %collective-permute-done.5.refs_6_), channel_id=1, source_target_pairs={{0,2},{1,3},{2,0},{3,1},{4,6},{5,7},{6,4},{7,5},{8,10},{9,11},{10,... | collective-permute-start | bytes 196616 | tf_op jit(solution)/shard_map/ppermute | solution.py:22
  15.6 1.3 %collective-permute-done.2.refs_3_ = bf16[32,1024]{1,0:T(8,128)(2,1)S(1)} collective-permute-done((bf16[32,1024]{1,0:T(8,128)(2,1)S(1)}, bf16[32,1024]{1,0:T(8,128)(2,1)S(1)}, u32[]{:S(2)}, u32[]{:S(2)}) %collective-permute-start.2) | collective-permute-done | bytes 65568 | tf_op jit(solution)/shard_map/ppermute | solution.py:22
  16.9 1.0 %collective-permute-done.4.refs_5_ = bf16[32,1024]{1,0:T(8,128)(2,1)S(1)} collective-permute-done((bf16[32,1024]{1,0:T(8,128)(2,1)S(1)}, bf16[32,1024]{1,0:T(8,128)(2,1)S(1)}, u32[]{:S(2)}, u32[]{:S(2)}) %collective-permute-start.4) | collective-permute-done | bytes 65568 | tf_op jit(solution)/shard_map/ppermute | solution.py:22
  17.8 1.3 %collective-permute-done.6.refs_7_ = bf16[32,1024]{1,0:T(8,128)(2,1)S(1)} collective-permute-done((bf16[32,1024]{1,0:T(8,128)(2,1)S(1)}, bf16[32,1024]{1,0:T(8,128)(2,1)S(1)}, u32[]{:S(2)}, u32[]{:S(2)}) %collective-permute-start.6) | collective-permute-done | bytes 65568 | tf_op jit(solution)/shard_map/ppermute | solution.py:22
  19.1 3.2 %shard_map.56 = (bf16[8,32,128]{2,1,0:T(8,128)(2,1)S(1)}, bf16[8,16,128]{2,1,0:T(8,128)(2,1)S(1)}) custom-call(bf16[32,1024]{1,0:T(8,128)(2,1)S(1)} %get-tuple-element.17.refs_0_, bf16[32,1024]{1,0:T(8,128)(2,1)S(1)} %collective-permute-done.refs_1_, bf16[32,1024]{1,0:T(8,128)(2,1)S(1)} %collective-permute-done.1.refs_2_, ...), custom_call_target="tpu_custom_call" | custom-call | flops 1073741824 | bytes 4718592 | tf_op jit(solution)/shard_map/pallas_call | solution.py:203
  22.4 0.0 copy-start
  22.4 1.6 %collective-permute-start.9 = (bf16[8,16,128]{2,1,0:T(8,128)(2,1)S(1)}, bf16[8,16,128]{2,1,0:T(8,128)(2,1)S(1)}, u32[]{:S(2)}, u32[]{:S(2)}) collective-permute-start(bf16[8,16,128]{2,1,0:T(8,128)(2,1)S(1)} %get-tuple-element.19), channel_id=1, source_target_pairs={{0,16},{16,0},{1,17},{17,1},{2,18},{18,2},{3,19},{19,3},{4,20},{20... | collective-permute-start | bytes 98312 | tf_op jit(solution)/shard_map/ppermute | solution.py:22
  24.0 2.4 %collective-permute-done.9 = bf16[8,16,128]{2,1,0:T(8,128)(2,1)S(1)} collective-permute-done((bf16[8,16,128]{2,1,0:T(8,128)(2,1)S(1)}, bf16[8,16,128]{2,1,0:T(8,128)(2,1)S(1)}, u32[]{:S(2)}, u32[]{:S(2)}) %collective-permute-start.9) | collective-permute-done | bytes 32800 | tf_op jit(solution)/shard_map/ppermute | solution.py:22
  26.4 0.7 collective-permute-start.11
  27.1 2.4 %collective-permute-start.13 = (bf16[8,48,128]{2,1,0:T(8,128)(2,1)S(1)}, bf16[8,48,128]{2,1,0:T(8,128)(2,1)S(1)}, u32[]{:S(2)}, u32[]{:S(2)}) collective-permute-start(bf16[8,48,128]{2,1,0:T(8,128)(2,1)S(1)} %constant_dynamic-update-slice_fusion.refs_8_), channel_id=1, source_target_pairs={{0,8},{1,9},{2,10},{3,11},{4,12},{5,13},{6,14},{7,15},{8,0},{9,1},... | collective-permute-start | bytes 294920 | tf_op jit(solution)/shard_map/ppermute | solution.py:22
  29.5 1.3 %collective-permute-start.15 = (bf16[8,48,128]{2,1,0:T(8,128)(2,1)S(1)}, bf16[8,48,128]{2,1,0:T(8,128)(2,1)S(1)}, u32[]{:S(2)}, u32[]{:S(2)}) collective-permute-start(bf16[8,48,128]{2,1,0:T(8,128)(2,1)S(1)} %constant_dynamic-update-slice_fusion.refs_8_), channel_id=1, source_target_pairs={{0,12},{1,13},{2,14},{3,15},{4,8},{5,9},{6,10},{7,11},{8,4},{9,5},... | collective-permute-start | bytes 294920 | tf_op jit(solution)/shard_map/ppermute | solution.py:22
  30.8 0.7 %collective-permute-start.10 = (bf16[8,48,128]{2,1,0:T(8,128)(2,1)S(1)}, bf16[8,48,128]{2,1,0:T(8,128)(2,1)S(1)}, u32[]{:S(2)}, u32[]{:S(2)}) collective-permute-start(bf16[8,48,128]{2,1,0:T(8,128)(2,1)S(1)} %constant_dynamic-update-slice_fusion.refs_8_), channel_id=1, source_target_pairs={{0,2},{1,3},{2,0},{3,1},{4,6},{5,7},{6,4},{7,5},{8,10},{9,11},{10,... | collective-permute-start | bytes 294920 | tf_op jit(solution)/shard_map/ppermute | solution.py:22
  31.5 1.3 %collective-permute-start.12 = (bf16[8,48,128]{2,1,0:T(8,128)(2,1)S(1)}, bf16[8,48,128]{2,1,0:T(8,128)(2,1)S(1)}, u32[]{:S(2)}, u32[]{:S(2)}) collective-permute-start(bf16[8,48,128]{2,1,0:T(8,128)(2,1)S(1)} %collective-permute-done.11.refs_10_), channel_id=1, source_target_pairs={{0,2},{1,3},{2,0},{3,1},{4,6},{5,7},{6,4},{7,5},{8,10},{9,11},{10,... | collective-permute-start | bytes 294920 | tf_op jit(solution)/shard_map/ppermute | solution.py:22
  32.8 0.8 %collective-permute-done.13.refs_12_ = bf16[8,48,128]{2,1,0:T(8,128)(2,1)S(1)} collective-permute-done((bf16[8,48,128]{2,1,0:T(8,128)(2,1)S(1)}, bf16[8,48,128]{2,1,0:T(8,128)(2,1)S(1)}, u32[]{:S(2)}, u32[]{:S(2)}) %collective-permute-start.13) | collective-permute-done | bytes 98336 | tf_op jit(solution)/shard_map/ppermute | solution.py:22
  33.6 1.0 %collective-permute-start.14 = (bf16[8,48,128]{2,1,0:T(8,128)(2,1)S(1)}, bf16[8,48,128]{2,1,0:T(8,128)(2,1)S(1)}, u32[]{:S(2)}, u32[]{:S(2)}) collective-permute-start(bf16[8,48,128]{2,1,0:T(8,128)(2,1)S(1)} %collective-permute-done.13.refs_12_), channel_id=1, source_target_pairs={{0,2},{1,3},{2,0},{3,1},{4,6},{5,7},{6,4},{7,5},{8,10},{9,11},{10,... | collective-permute-start | bytes 294920 | tf_op jit(solution)/shard_map/ppermute | solution.py:22
  34.6 1.3 %collective-permute-done.15.refs_14_ = bf16[8,48,128]{2,1,0:T(8,128)(2,1)S(1)} collective-permute-done((bf16[8,48,128]{2,1,0:T(8,128)(2,1)S(1)}, bf16[8,48,128]{2,1,0:T(8,128)(2,1)S(1)}, u32[]{:S(2)}, u32[]{:S(2)}) %collective-permute-start.15) | collective-permute-done | bytes 98336 | tf_op jit(solution)/shard_map/ppermute | solution.py:22
  35.9 1.3 %collective-permute-start.16 = (bf16[8,48,128]{2,1,0:T(8,128)(2,1)S(1)}, bf16[8,48,128]{2,1,0:T(8,128)(2,1)S(1)}, u32[]{:S(2)}, u32[]{:S(2)}) collective-permute-start(bf16[8,48,128]{2,1,0:T(8,128)(2,1)S(1)} %collective-permute-done.15.refs_14_), channel_id=1, source_target_pairs={{0,2},{1,3},{2,0},{3,1},{4,6},{5,7},{6,4},{7,5},{8,10},{9,11},{10,... | collective-permute-start | bytes 294920 | tf_op jit(solution)/shard_map/ppermute | solution.py:22
  37.2 1.0 %collective-permute-done.14.refs_13_ = bf16[8,48,128]{2,1,0:T(8,128)(2,1)S(1)} collective-permute-done((bf16[8,48,128]{2,1,0:T(8,128)(2,1)S(1)}, bf16[8,48,128]{2,1,0:T(8,128)(2,1)S(1)}, u32[]{:S(2)}, u32[]{:S(2)}) %collective-permute-start.14) | collective-permute-done | bytes 98336 | tf_op jit(solution)/shard_map/ppermute | solution.py:22
  38.3 2.3 %collective-permute-done.16.refs_15_ = bf16[8,48,128]{2,1,0:T(8,128)(2,1)S(1)} collective-permute-done((bf16[8,48,128]{2,1,0:T(8,128)(2,1)S(1)}, bf16[8,48,128]{2,1,0:T(8,128)(2,1)S(1)}, u32[]{:S(2)}, u32[]{:S(2)}) %collective-permute-start.16) | collective-permute-done | bytes 98336 | tf_op jit(solution)/shard_map/ppermute | solution.py:22
  40.5 0.5 shard_map.57
  41.0 0.1 collective-permute-start.17
  41.1 1.9 %collective-permute-done.17.other_ref = bf16[8,32,1024]{2,1,0:T(8,128)(2,1)S(1)} collective-permute-done((bf16[8,32,1024]{2,1,0:T(8,128)(2,1)S(1)}, bf16[8,32,1024]{2,1,0:T(8,128)(2,1)S(1)}, u32[]{:S(2)}, u32[]{:S(2)}) %collective-permute-start.17) | collective-permute-done | bytes 524320 | tf_op jit(solution)/shard_map/ppermute | solution.py:22
  43.0 12.6 %shard_map.58 = (bf16[8,2,32,128]{3,2,1,0:T(8,128)(2,1)}, f32[32,1024]{1,0:T(8,128)S(1)}, f32[32,1024]{1,0:T(8,128)S(1)}) custom-call(f32[8,32,1024]{2,1,0:T(8,128)S(1)} %get-tuple-element.20.exact_ref, f32[8,16,1024]{2,1,0:T(8,128)S(1)} %get-tuple-element.21.edges_ref, bf16[8,32,1024]{2,1,0:T(8,128)(2,1)S(1)} %collective-permute-done.17.other_ref, ...), custom_call_target="tpu_custom_call" | custom-call | flops 1073741824 | bytes 4718592 | tf_op jit(solution)/shard_map/pallas_call | solution.py:312
  55.6 3.4 %all-to-all-start = ((bf16[8,2,32,128]{3,2,1,0:T(8,128)(2,1)}), bf16[8,2,32,128]{3,2,1,0:T(8,128)(2,1)S(1)}, u32[]{:S(2)}, u32[]{:S(2)}) async-start(bf16[8,2,32,128]{3,2,1,0:T(8,128)(2,1)} %get-tuple-element.25), calls=%async_computation | async-start | bytes 262144 | tf_op jit(solution)/shard_map/all_to_all | solution.py:391
  59.0 7.5 %all-to-all-done = bf16[8,2,32,128]{3,2,1,0:T(8,128)(2,1)S(1)} async-done(((bf16[8,2,32,128]{3,2,1,0:T(8,128)(2,1)}), bf16[8,2,32,128]{3,2,1,0:T(8,128)(2,1)S(1)}, u32[]{:S(2)}, u32[]{:S(2)}) %all-to-all-start) | async-done | bytes 131104 | tf_op jit(solution)/shard_map/all_to_all | solution.py:391
  66.6 0.1 copy.7
  66.6 0.1 copy.6
  66.9 0.1 copy.9
  67.0 1.6 %collective-permute-start.18 = (bf16[2,8,1024]{2,1,0:T(8,128)(2,1)S(1)}, bf16[2,8,1024]{2,1,0:T(8,128)(2,1)S(1)}, u32[]{:S(2)}, u32[]{:S(2)}) collective-permute-start(bf16[2,8,1024]{2,1,0:T(8,128)(2,1)S(1)} %pad_maximum_fusion.1), channel_id=1, source_target_pairs={{0,16},{16,0},{1,17},{17,1},{2,18},{18,2},{3,19},{19,3},{4,20},{20... | collective-permute-start | bytes 98312 | tf_op jit(solution)/shard_map/ppermute | solution.py:22
  68.5 0.1 fusion.15
  68.6 0.1 collective-permute-start.19
  68.7 2.3 %collective-permute-done.18 = bf16[2,8,1024]{2,1,0:T(8,128)(2,1)S(1)} collective-permute-done((bf16[2,8,1024]{2,1,0:T(8,128)(2,1)S(1)}, bf16[2,8,1024]{2,1,0:T(8,128)(2,1)S(1)}, u32[]{:S(2)}, u32[]{:S(2)}) %collective-permute-start.18) | collective-permute-done | bytes 32800 | tf_op jit(solution)/shard_map/ppermute | solution.py:22
  71.0 0.2 fusion.5
  71.2 0.1 slice.109
  71.3 0.7 add_bitcast_fusion
  (24 shorter events, 0.3 us)
Async XLA Ops:
  0.0 19.1 %collective-permute-start.7 = (bf16[1024,512]{1,0:T(8,128)(2,1)}, bf16[1024,512]{1,0:T(8,128)(2,1)S(1)}, u32[]{:S(2)}, u32[]{:S(2)}) collective-permute-start(bf16[1024,512]{1,0:T(8,128)(2,1)} %refs_0_.1), channel_id=1, source_target_pairs={{0,1},{1,0},{2,3},{3,2},{4,5},{5,4},{6,7},{7,6},{8,9},{9,8},{10,11... | collective-permute-start | bytes 3145736 | tf_op jit(solution)/shard_map/ppermute | solution.py:22
  0.5 18.6 %collective-permute-start.8 = (bf16[1024,512]{1,0:T(8,128)(2,1)}, bf16[1024,512]{1,0:T(8,128)(2,1)S(1)}, u32[]{:S(2)}, u32[]{:S(2)}) collective-permute-start(bf16[1024,512]{1,0:T(8,128)(2,1)} %refs_1_.1), channel_id=1, source_target_pairs={{0,1},{1,0},{2,3},{3,2},{4,5},{5,4},{6,7},{7,6},{8,9},{9,8},{10,11... | collective-permute-start | bytes 3145736 | tf_op jit(solution)/shard_map/ppermute | solution.py:22
  1.5 5.7 %collective-permute-start.1 = (bf16[32,1024]{1,0:T(8,128)(2,1)S(1)}, bf16[32,1024]{1,0:T(8,128)(2,1)S(1)}, u32[]{:S(2)}, u32[]{:S(2)}) collective-permute-start(bf16[32,1024]{1,0:T(8,128)(2,1)S(1)} %get-tuple-element.17.refs_0_), channel_id=1, source_target_pairs={{0,4},{1,5},{2,6},{3,7},{4,0},{5,1},{6,2},{7,3},{8,12},{9,13},{10,... | collective-permute-start | bytes 196616 | tf_op jit(solution)/shard_map/ppermute | solution.py:22
  4.6 7.5 %collective-permute-start.3 = (bf16[32,1024]{1,0:T(8,128)(2,1)S(1)}, bf16[32,1024]{1,0:T(8,128)(2,1)S(1)}, u32[]{:S(2)}, u32[]{:S(2)}) collective-permute-start(bf16[32,1024]{1,0:T(8,128)(2,1)S(1)} %get-tuple-element.17.refs_0_), channel_id=1, source_target_pairs={{0,8},{1,9},{2,10},{3,11},{4,12},{5,13},{6,14},{7,15},{8,0},{9,1},... | collective-permute-start | bytes 196616 | tf_op jit(solution)/shard_map/ppermute | solution.py:22
  7.2 6.4 %collective-permute-start.5 = (bf16[32,1024]{1,0:T(8,128)(2,1)S(1)}, bf16[32,1024]{1,0:T(8,128)(2,1)S(1)}, u32[]{:S(2)}, u32[]{:S(2)}) collective-permute-start(bf16[32,1024]{1,0:T(8,128)(2,1)S(1)} %get-tuple-element.17.refs_0_), channel_id=1, source_target_pairs={{0,12},{1,13},{2,14},{3,15},{4,8},{5,9},{6,10},{7,11},{8,4},{9,5},... | collective-permute-start | bytes 196616 | tf_op jit(solution)/shard_map/ppermute | solution.py:22
  7.2 7.7 %collective-permute-start = (bf16[32,1024]{1,0:T(8,128)(2,1)S(1)}, bf16[32,1024]{1,0:T(8,128)(2,1)S(1)}, u32[]{:S(2)}, u32[]{:S(2)}) collective-permute-start(bf16[32,1024]{1,0:T(8,128)(2,1)S(1)} %get-tuple-element.17.refs_0_), channel_id=1, source_target_pairs={{0,2},{1,3},{2,0},{3,1},{4,6},{5,7},{6,4},{7,5},{8,10},{9,11},{10,... | collective-permute-start | bytes 196616 | tf_op jit(solution)/shard_map/ppermute | solution.py:22
  12.0 4.8 %collective-permute-start.2 = (bf16[32,1024]{1,0:T(8,128)(2,1)S(1)}, bf16[32,1024]{1,0:T(8,128)(2,1)S(1)}, u32[]{:S(2)}, u32[]{:S(2)}) collective-permute-start(bf16[32,1024]{1,0:T(8,128)(2,1)S(1)} %collective-permute-done.1.refs_2_), channel_id=1, source_target_pairs={{0,2},{1,3},{2,0},{3,1},{4,6},{5,7},{6,4},{7,5},{8,10},{9,11},{10,... | collective-permute-start | bytes 196616 | tf_op jit(solution)/shard_map/ppermute | solution.py:22
  13.6 4.3 %collective-permute-start.4 = (bf16[32,1024]{1,0:T(8,128)(2,1)S(1)}, bf16[32,1024]{1,0:T(8,128)(2,1)S(1)}, u32[]{:S(2)}, u32[]{:S(2)}) collective-permute-start(bf16[32,1024]{1,0:T(8,128)(2,1)S(1)} %collective-permute-done.3.refs_4_), channel_id=1, source_target_pairs={{0,2},{1,3},{2,0},{3,1},{4,6},{5,7},{6,4},{7,5},{8,10},{9,11},{10,... | collective-permute-start | bytes 196616 | tf_op jit(solution)/shard_map/ppermute | solution.py:22
  14.9 4.3 %collective-permute-start.6 = (bf16[32,1024]{1,0:T(8,128)(2,1)S(1)}, bf16[32,1024]{1,0:T(8,128)(2,1)S(1)}, u32[]{:S(2)}, u32[]{:S(2)}) collective-permute-start(bf16[32,1024]{1,0:T(8,128)(2,1)S(1)} %collective-permute-done.5.refs_6_), channel_id=1, source_target_pairs={{0,2},{1,3},{2,0},{3,1},{4,6},{5,7},{6,4},{7,5},{8,10},{9,11},{10,... | collective-permute-start | bytes 196616 | tf_op jit(solution)/shard_map/ppermute | solution.py:22
  19.1 23.9 %copy-start.1 = (bf16[1024,512]{1,0:T(8,128)(2,1)S(1)}, bf16[1024,512]{1,0:T(8,128)(2,1)}, u32[]{:S(2)}) copy-start(bf16[1024,512]{1,0:T(8,128)(2,1)} %refs_1_.1) | copy-start | bytes 3145732
  22.4 20.6 %copy-start = (bf16[1024,512]{1,0:T(8,128)(2,1)S(1)}, bf16[1024,512]{1,0:T(8,128)(2,1)}, u32[]{:S(2)}) copy-start(bf16[1024,512]{1,0:T(8,128)(2,1)} %refs_0_.1) | copy-start | bytes 3145732
  22.4 4.0 %collective-permute-start.9 = (bf16[8,16,128]{2,1,0:T(8,128)(2,1)S(1)}, bf16[8,16,128]{2,1,0:T(8,128)(2,1)S(1)}, u32[]{:S(2)}, u32[]{:S(2)}) collective-permute-start(bf16[8,16,128]{2,1,0:T(8,128)(2,1)S(1)} %get-tuple-element.19), channel_id=1, source_target_pairs={{0,16},{16,0},{1,17},{17,1},{2,18},{18,2},{3,19},{19,3},{4,20},{20... | collective-permute-start | bytes 98312 | tf_op jit(solution)/shard_map/ppermute | solution.py:22
  26.4 5.1 %collective-permute-start.11 = (bf16[8,48,128]{2,1,0:T(8,128)(2,1)S(1)}, bf16[8,48,128]{2,1,0:T(8,128)(2,1)S(1)}, u32[]{:S(2)}, u32[]{:S(2)}) collective-permute-start(bf16[8,48,128]{2,1,0:T(8,128)(2,1)S(1)} %constant_dynamic-update-slice_fusion.refs_8_), channel_id=1, source_target_pairs={{0,4},{1,5},{2,6},{3,7},{4,0},{5,1},{6,2},{7,3},{8,12},{9,13},{10,... | collective-permute-start | bytes 294920 | tf_op jit(solution)/shard_map/ppermute | solution.py:22
  27.1 6.6 %collective-permute-start.13 = (bf16[8,48,128]{2,1,0:T(8,128)(2,1)S(1)}, bf16[8,48,128]{2,1,0:T(8,128)(2,1)S(1)}, u32[]{:S(2)}, u32[]{:S(2)}) collective-permute-start(bf16[8,48,128]{2,1,0:T(8,128)(2,1)S(1)} %constant_dynamic-update-slice_fusion.refs_8_), channel_id=1, source_target_pairs={{0,8},{1,9},{2,10},{3,11},{4,12},{5,13},{6,14},{7,15},{8,0},{9,1},... | collective-permute-start | bytes 294920 | tf_op jit(solution)/shard_map/ppermute | solution.py:22
  29.5 6.4 %collective-permute-start.15 = (bf16[8,48,128]{2,1,0:T(8,128)(2,1)S(1)}, bf16[8,48,128]{2,1,0:T(8,128)(2,1)S(1)}, u32[]{:S(2)}, u32[]{:S(2)}) collective-permute-start(bf16[8,48,128]{2,1,0:T(8,128)(2,1)S(1)} %constant_dynamic-update-slice_fusion.refs_8_), channel_id=1, source_target_pairs={{0,12},{1,13},{2,14},{3,15},{4,8},{5,9},{6,10},{7,11},{8,4},{9,5},... | collective-permute-start | bytes 294920 | tf_op jit(solution)/shard_map/ppermute | solution.py:22
  30.8 6.5 %collective-permute-start.10 = (bf16[8,48,128]{2,1,0:T(8,128)(2,1)S(1)}, bf16[8,48,128]{2,1,0:T(8,128)(2,1)S(1)}, u32[]{:S(2)}, u32[]{:S(2)}) collective-permute-start(bf16[8,48,128]{2,1,0:T(8,128)(2,1)S(1)} %constant_dynamic-update-slice_fusion.refs_8_), channel_id=1, source_target_pairs={{0,2},{1,3},{2,0},{3,1},{4,6},{5,7},{6,4},{7,5},{8,10},{9,11},{10,... | collective-permute-start | bytes 294920 | tf_op jit(solution)/shard_map/ppermute | solution.py:22
  31.5 5.7 %collective-permute-start.12 = (bf16[8,48,128]{2,1,0:T(8,128)(2,1)S(1)}, bf16[8,48,128]{2,1,0:T(8,128)(2,1)S(1)}, u32[]{:S(2)}, u32[]{:S(2)}) collective-permute-start(bf16[8,48,128]{2,1,0:T(8,128)(2,1)S(1)} %collective-permute-done.11.refs_10_), channel_id=1, source_target_pairs={{0,2},{1,3},{2,0},{3,1},{4,6},{5,7},{6,4},{7,5},{8,10},{9,11},{10,... | collective-permute-start | bytes 294920 | tf_op jit(solution)/shard_map/ppermute | solution.py:22
  33.6 4.6 %collective-permute-start.14 = (bf16[8,48,128]{2,1,0:T(8,128)(2,1)S(1)}, bf16[8,48,128]{2,1,0:T(8,128)(2,1)S(1)}, u32[]{:S(2)}, u32[]{:S(2)}) collective-permute-start(bf16[8,48,128]{2,1,0:T(8,128)(2,1)S(1)} %collective-permute-done.13.refs_12_), channel_id=1, source_target_pairs={{0,2},{1,3},{2,0},{3,1},{4,6},{5,7},{6,4},{7,5},{8,10},{9,11},{10,... | collective-permute-start | bytes 294920 | tf_op jit(solution)/shard_map/ppermute | solution.py:22
  35.9 4.6 %collective-permute-start.16 = (bf16[8,48,128]{2,1,0:T(8,128)(2,1)S(1)}, bf16[8,48,128]{2,1,0:T(8,128)(2,1)S(1)}, u32[]{:S(2)}, u32[]{:S(2)}) collective-permute-start(bf16[8,48,128]{2,1,0:T(8,128)(2,1)S(1)} %collective-permute-done.15.refs_14_), channel_id=1, source_target_pairs={{0,2},{1,3},{2,0},{3,1},{4,6},{5,7},{6,4},{7,5},{8,10},{9,11},{10,... | collective-permute-start | bytes 294920 | tf_op jit(solution)/shard_map/ppermute | solution.py:22
  41.0 2.0 %collective-permute-start.17 = (bf16[8,32,1024]{2,1,0:T(8,128)(2,1)S(1)}, bf16[8,32,1024]{2,1,0:T(8,128)(2,1)S(1)}, u32[]{:S(2)}, u32[]{:S(2)}) collective-permute-start(bf16[8,32,1024]{2,1,0:T(8,128)(2,1)S(1)} %get-tuple-element.22), channel_id=1, source_target_pairs={{0,1},{1,0},{2,3},{3,2},{4,5},{5,4},{6,7},{7,6},{8,9},{9,8},{10,11... | collective-permute-start | bytes 1572872 | tf_op jit(solution)/shard_map/ppermute | solution.py:22
  55.6 10.9 %all-to-all-start = ((bf16[8,2,32,128]{3,2,1,0:T(8,128)(2,1)}), bf16[8,2,32,128]{3,2,1,0:T(8,128)(2,1)S(1)}, u32[]{:S(2)}, u32[]{:S(2)}) async-start(bf16[8,2,32,128]{3,2,1,0:T(8,128)(2,1)} %get-tuple-element.25), calls=%async_computation | async-start | bytes 262144 | tf_op jit(solution)/shard_map/all_to_all | solution.py:391
  67.0 4.0 %collective-permute-start.18 = (bf16[2,8,1024]{2,1,0:T(8,128)(2,1)S(1)}, bf16[2,8,1024]{2,1,0:T(8,128)(2,1)S(1)}, u32[]{:S(2)}, u32[]{:S(2)}) collective-permute-start(bf16[2,8,1024]{2,1,0:T(8,128)(2,1)S(1)} %pad_maximum_fusion.1), channel_id=1, source_target_pairs={{0,16},{16,0},{1,17},{17,1},{2,18},{18,2},{3,19},{19,3},{4,20},{20... | collective-permute-start | bytes 98312 | tf_op jit(solution)/shard_map/ppermute | solution.py:22
  68.6 2.4 %collective-permute-start.19 = (bf16[2,4,8,1024]{3,2,1,0:T(8,128)(2,1)S(1)}, bf16[2,4,8,1024]{3,2,1,0:T(8,128)(2,1)S(1)}, u32[]{:S(2)}, u32[]{:S(2)}) collective-permute-start(bf16[2,4,8,1024]{3,2,1,0:T(8,128)(2,1)S(1)} %pad_maximum_fusion), channel_id=1, source_target_pairs={{0,1},{1,0},{2,3},{3,2},{4,5},{5,4},{6,7},{7,6},{8,9},{9,8},{10,11... | collective-permute-start | bytes 393224 | tf_op jit(solution)/shard_map/ppermute | solution.py:22

commit v5 on v4

--- a/solution.py
+++ b/solution.py
@@ -257,7 +257,7 @@
 
 def second_kernel(chips, layers, exact_ref, edges_ref, other_ref, tables_ref, *refs):
     factors = refs[:4]
-    sent_ref, own_ref, beside_ref, read_ref, states_ref = refs[4:]
+    sent_ref, own_ref, beside_ref, read_ref, states_ref, updated_ref = refs[4:]
     me = lax.axis_index("mom")
     core, chip = me & 1, me >> 1
     away = 2 * core - 1
@@ -289,15 +289,10 @@
             upper = read_ref[:, at + NDIR : at + NDIR + 128]
             state = read + tables_ref[6:7, lanes] * (upper - read)
             states_ref[cell, :, lanes] = state.astype(jnp.bfloat16)
-
-            @pl.when(cell == chip)
-            def _():
-                own_ref[:, lanes] = state
-
-            @pl.when(cell == ((chip - away) & (chips - 1)))
-            def _():
-                beside_ref[:, lanes] = state
-
+            updated_ref[cell, :, lanes] = state
+
+    own_ref[...] = updated_ref[chip]
+    beside_ref[...] = updated_ref[(chip - away) & (chips - 1)]
     states = states_ref[...].reshape(chips * rows, size)
     terms = project(states, core, factors[2:], factors[:2], []).astype(jnp.bfloat16)
     for here in range(chips):
@@ -319,6 +314,7 @@
         scratch_shapes=[
             pltpu.VMEM((rows, size + 128), jnp.float32),
             pltpu.VMEM((chips, rows, size), jnp.bfloat16),
+            pltpu.VMEM((chips, rows, size), jnp.float32),
         ],
         compiler_params=pltpu.CompilerParams(vmem_limit_bytes=16 << 20),
         cost_estimate=pl.CostEstimate(

time: 72.2 us -> 64.1 us (0.89)
  Pallas kernels: 17.3 us -> 9.16 us
    pallas_call x1, Pallas kernels: 12.6 us -> 4.51 us  [second_collision(): pl.pallas_call(functools.partial(second_kernel, chips, layers), out_shape...]
where the time goes in v5:
time: 64.1 us; the launch traced here: 63.8 us
  starting transfers between devices  26.8 us (42%)
  waiting for transfers between devices  26.1 us (41%)
  Pallas kernels  9.16 us (14%)
  other arithmetic  1.02 us (2%)
    ppermute x20, starting transfers between devices, swap(): return lax.ppermute(block, axis, [(i, i ^ bits) for i in range(count)])  23.5 us
    ppermute x20, waiting for transfers between devices, swap(): return lax.ppermute(block, axis, [(i, i ^ bits) for i in range(count)])  18.7 us
    all_to_all x1, waiting for transfers between devices, settle(): lax.all_to_all(sent, 'mom', split_axis=0, concat_axis=0, tiled=True, axis...  7.45 us
    pallas_call x1, Pallas kernels, second_collision(): pl.pallas_call(functools.partial(second_kernel, chips, layers), out_shape...  4.51 us
    all_to_all x1, starting transfers between devices, settle(): lax.all_to_all(sent, 'mom', split_axis=0, concat_axis=0, tiled=True, axis...  3.37 us
    pallas_call x1, Pallas kernels, first_collision(): pl.pallas_call(functools.partial(first_kernel, chips, layers), out_shape=...  3.23 us
  transfers between devices with their start and end apart: 21, of which 12 were waited for; matrix products, arithmetic and copies ran while one was open for 0% of the time, Pallas kernels for 1%

profile of v5, /device:TPU:0, one launch (start us, length us, event | category | flops | bytes accessed | tf_op | source)
XLA Modules:
  0.0 63.8 jit_solution(1379443081316748881)
XLA Ops:
  0.0 0.5 collective-permute-start.7
  0.5 0.0 collective-permute-start.8
  0.5 0.9 %shard_map.55 = (f32[32,1024]{1,0:T(8,128)S(1)}, bf16[32,1024]{1,0:T(8,128)(2,1)S(1)}, f32[8,1024]{1,0:T(8,128)S(1)}) custom-call(f32[32,1024]{1,0:T(8,128)} %bitcast.48, f32[3,1024]{1,0:T(4,128)} %velocity_hbm.1, f32[1,1024]{1,0:T(1,128)} %bitcast.56), custom_call_target="tpu_custom_call" | custom-call | flops 32768 | bytes 327680 | tf_op jit(solution)/shard_map/pallas_call | solution.py:64
  1.5 3.1 %collective-permute-start.1 = (bf16[32,1024]{1,0:T(8,128)(2,1)S(1)}, bf16[32,1024]{1,0:T(8,128)(2,1)S(1)}, u32[]{:S(2)}, u32[]{:S(2)}) collective-permute-start(bf16[32,1024]{1,0:T(8,128)(2,1)S(1)} %get-tuple-element.17.refs_0_), channel_id=1, source_target_pairs={{0,4},{1,5},{2,6},{3,7},{4,0},{5,1},{6,2},{7,3},{8,12},{9,13},{10,... | collective-permute-start | bytes 196616 | tf_op jit(solution)/shard_map/ppermute | solution.py:22
  4.6 2.6 %collective-permute-start.3 = (bf16[32,1024]{1,0:T(8,128)(2,1)S(1)}, bf16[32,1024]{1,0:T(8,128)(2,1)S(1)}, u32[]{:S(2)}, u32[]{:S(2)}) collective-permute-start(bf16[32,1024]{1,0:T(8,128)(2,1)S(1)} %get-tuple-element.17.refs_0_), channel_id=1, source_target_pairs={{0,8},{1,9},{2,10},{3,11},{4,12},{5,13},{6,14},{7,15},{8,0},{9,1},... | collective-permute-start | bytes 196616 | tf_op jit(solution)/shard_map/ppermute | solution.py:22
  7.2 0.0 collective-permute-start.5
  7.2 0.0 collective-permute-done.1.refs_2_
  7.2 1.7 %collective-permute-start = (bf16[32,1024]{1,0:T(8,128)(2,1)S(1)}, bf16[32,1024]{1,0:T(8,128)(2,1)S(1)}, u32[]{:S(2)}, u32[]{:S(2)}) collective-permute-start(bf16[32,1024]{1,0:T(8,128)(2,1)S(1)} %get-tuple-element.17.refs_0_), channel_id=1, source_target_pairs={{0,2},{1,3},{2,0},{3,1},{4,6},{5,7},{6,4},{7,5},{8,10},{9,11},{10,... | collective-permute-start | bytes 196616 | tf_op jit(solution)/shard_map/ppermute | solution.py:22
  8.9 3.1 %collective-permute-done.3.refs_4_ = bf16[32,1024]{1,0:T(8,128)(2,1)S(1)} collective-permute-done((bf16[32,1024]{1,0:T(8,128)(2,1)S(1)}, bf16[32,1024]{1,0:T(8,128)(2,1)S(1)}, u32[]{:S(2)}, u32[]{:S(2)}) %collective-permute-start.3) | collective-permute-done | bytes 65568 | tf_op jit(solution)/shard_map/ppermute | solution.py:22
  12.0 1.5 %collective-permute-start.2 = (bf16[32,1024]{1,0:T(8,128)(2,1)S(1)}, bf16[32,1024]{1,0:T(8,128)(2,1)S(1)}, u32[]{:S(2)}, u32[]{:S(2)}) collective-permute-start(bf16[32,1024]{1,0:T(8,128)(2,1)S(1)} %collective-permute-done.1.refs_2_), channel_id=1, source_target_pairs={{0,2},{1,3},{2,0},{3,1},{4,6},{5,7},{6,4},{7,5},{8,10},{9,11},{10,... | collective-permute-start | bytes 196616 | tf_op jit(solution)/shard_map/ppermute | solution.py:22
  13.6 0.0 collective-permute-done.5.refs_6_
  13.6 1.3 %collective-permute-start.4 = (bf16[32,1024]{1,0:T(8,128)(2,1)S(1)}, bf16[32,1024]{1,0:T(8,128)(2,1)S(1)}, u32[]{:S(2)}, u32[]{:S(2)}) collective-permute-start(bf16[32,1024]{1,0:T(8,128)(2,1)S(1)} %collective-permute-done.3.refs_4_), channel_id=1, source_target_pairs={{0,2},{1,3},{2,0},{3,1},{4,6},{5,7},{6,4},{7,5},{8,10},{9,11},{10,... | collective-permute-start | bytes 196616 | tf_op jit(solution)/shard_map/ppermute | solution.py:22
  14.9 0.7 %collective-permute-start.6 = (bf16[32,1024]{1,0:T(8,128)(2,1)S(1)}, bf16[32,1024]{1,0:T(8,128)(2,1)S(1)}, u32[]{:S(2)}, u32[]{:S(2)}) collective-permute-start(bf16[32,1024]{1,0:T(8,128)(2,1)S(1)} %collective-permute-done.5.refs_6_), channel_id=1, source_target_pairs={{0,2},{1,3},{2,0},{3,1},{4,6},{5,7},{6,4},{7,5},{8,10},{9,11},{10,... | collective-permute-start | bytes 196616 | tf_op jit(solution)/shard_map/ppermute | solution.py:22
  15.6 1.3 %collective-permute-done.2.refs_3_ = bf16[32,1024]{1,0:T(8,128)(2,1)S(1)} collective-permute-done((bf16[32,1024]{1,0:T(8,128)(2,1)S(1)}, bf16[32,1024]{1,0:T(8,128)(2,1)S(1)}, u32[]{:S(2)}, u32[]{:S(2)}) %collective-permute-start.2) | collective-permute-done | bytes 65568 | tf_op jit(solution)/shard_map/ppermute | solution.py:22
  16.9 1.0 %collective-permute-done.4.refs_5_ = bf16[32,1024]{1,0:T(8,128)(2,1)S(1)} collective-permute-done((bf16[32,1024]{1,0:T(8,128)(2,1)S(1)}, bf16[32,1024]{1,0:T(8,128)(2,1)S(1)}, u32[]{:S(2)}, u32[]{:S(2)}) %collective-permute-start.4) | collective-permute-done | bytes 65568 | tf_op jit(solution)/shard_map/ppermute | solution.py:22
  17.8 1.3 %collective-permute-done.6.refs_7_ = bf16[32,1024]{1,0:T(8,128)(2,1)S(1)} collective-permute-done((bf16[32,1024]{1,0:T(8,128)(2,1)S(1)}, bf16[32,1024]{1,0:T(8,128)(2,1)S(1)}, u32[]{:S(2)}, u32[]{:S(2)}) %collective-permute-start.6) | collective-permute-done | bytes 65568 | tf_op jit(solution)/shard_map/ppermute | solution.py:22
  19.1 3.2 %shard_map.56 = (bf16[8,32,128]{2,1,0:T(8,128)(2,1)S(1)}, bf16[8,16,128]{2,1,0:T(8,128)(2,1)S(1)}) custom-call(bf16[32,1024]{1,0:T(8,128)(2,1)S(1)} %get-tuple-element.17.refs_0_, bf16[32,1024]{1,0:T(8,128)(2,1)S(1)} %collective-permute-done.refs_1_, bf16[32,1024]{1,0:T(8,128)(2,1)S(1)} %collective-permute-done.1.refs_2_, ...), custom_call_target="tpu_custom_call" | custom-call | flops 1073741824 | bytes 4718592 | tf_op jit(solution)/shard_map/pallas_call | solution.py:203
  22.4 0.0 copy-start
  22.4 1.6 %collective-permute-start.9 = (bf16[8,16,128]{2,1,0:T(8,128)(2,1)S(1)}, bf16[8,16,128]{2,1,0:T(8,128)(2,1)S(1)}, u32[]{:S(2)}, u32[]{:S(2)}) collective-permute-start(bf16[8,16,128]{2,1,0:T(8,128)(2,1)S(1)} %get-tuple-element.19), channel_id=1, source_target_pairs={{0,16},{16,0},{1,17},{17,1},{2,18},{18,2},{3,19},{19,3},{4,20},{20... | collective-permute-start | bytes 98312 | tf_op jit(solution)/shard_map/ppermute | solution.py:22
  24.0 2.4 %collective-permute-done.9 = bf16[8,16,128]{2,1,0:T(8,128)(2,1)S(1)} collective-permute-done((bf16[8,16,128]{2,1,0:T(8,128)(2,1)S(1)}, bf16[8,16,128]{2,1,0:T(8,128)(2,1)S(1)}, u32[]{:S(2)}, u32[]{:S(2)}) %collective-permute-start.9) | collective-permute-done | bytes 32800 | tf_op jit(solution)/shard_map/ppermute | solution.py:22
  26.4 0.7 %collective-permute-start.11 = (bf16[8,48,128]{2,1,0:T(8,128)(2,1)S(1)}, bf16[8,48,128]{2,1,0:T(8,128)(2,1)S(1)}, u32[]{:S(2)}, u32[]{:S(2)}) collective-permute-start(bf16[8,48,128]{2,1,0:T(8,128)(2,1)S(1)} %constant_dynamic-update-slice_fusion.refs_8_), channel_id=1, source_target_pairs={{0,4},{1,5},{2,6},{3,7},{4,0},{5,1},{6,2},{7,3},{8,12},{9,13},{10,... | collective-permute-start | bytes 294920 | tf_op jit(solution)/shard_map/ppermute | solution.py:22
  27.1 2.4 %collective-permute-start.13 = (bf16[8,48,128]{2,1,0:T(8,128)(2,1)S(1)}, bf16[8,48,128]{2,1,0:T(8,128)(2,1)S(1)}, u32[]{:S(2)}, u32[]{:S(2)}) collective-permute-start(bf16[8,48,128]{2,1,0:T(8,128)(2,1)S(1)} %constant_dynamic-update-slice_fusion.refs_8_), channel_id=1, source_target_pairs={{0,8},{1,9},{2,10},{3,11},{4,12},{5,13},{6,14},{7,15},{8,0},{9,1},... | collective-permute-start | bytes 294920 | tf_op jit(solution)/shard_map/ppermute | solution.py:22
  29.5 1.3 %collective-permute-start.15 = (bf16[8,48,128]{2,1,0:T(8,128)(2,1)S(1)}, bf16[8,48,128]{2,1,0:T(8,128)(2,1)S(1)}, u32[]{:S(2)}, u32[]{:S(2)}) collective-permute-start(bf16[8,48,128]{2,1,0:T(8,128)(2,1)S(1)} %constant_dynamic-update-slice_fusion.refs_8_), channel_id=1, source_target_pairs={{0,12},{1,13},{2,14},{3,15},{4,8},{5,9},{6,10},{7,11},{8,4},{9,5},... | collective-permute-start | bytes 294920 | tf_op jit(solution)/shard_map/ppermute | solution.py:22
  30.8 0.7 %collective-permute-start.10 = (bf16[8,48,128]{2,1,0:T(8,128)(2,1)S(1)}, bf16[8,48,128]{2,1,0:T(8,128)(2,1)S(1)}, u32[]{:S(2)}, u32[]{:S(2)}) collective-permute-start(bf16[8,48,128]{2,1,0:T(8,128)(2,1)S(1)} %constant_dynamic-update-slice_fusion.refs_8_), channel_id=1, source_target_pairs={{0,2},{1,3},{2,0},{3,1},{4,6},{5,7},{6,4},{7,5},{8,10},{9,11},{10,... | collective-permute-start | bytes 294920 | tf_op jit(solution)/shard_map/ppermute | solution.py:22
  31.5 1.3 %collective-permute-start.12 = (bf16[8,48,128]{2,1,0:T(8,128)(2,1)S(1)}, bf16[8,48,128]{2,1,0:T(8,128)(2,1)S(1)}, u32[]{:S(2)}, u32[]{:S(2)}) collective-permute-start(bf16[8,48,128]{2,1,0:T(8,128)(2,1)S(1)} %collective-permute-done.11.refs_10_), channel_id=1, source_target_pairs={{0,2},{1,3},{2,0},{3,1},{4,6},{5,7},{6,4},{7,5},{8,10},{9,11},{10,... | collective-permute-start | bytes 294920 | tf_op jit(solution)/shard_map/ppermute | solution.py:22
  32.8 0.8 %collective-permute-done.13.refs_12_ = bf16[8,48,128]{2,1,0:T(8,128)(2,1)S(1)} collective-permute-done((bf16[8,48,128]{2,1,0:T(8,128)(2,1)S(1)}, bf16[8,48,128]{2,1,0:T(8,128)(2,1)S(1)}, u32[]{:S(2)}, u32[]{:S(2)}) %collective-permute-start.13) | collective-permute-done | bytes 98336 | tf_op jit(solution)/shard_map/ppermute | solution.py:22
  33.6 1.0 %collective-permute-start.14 = (bf16[8,48,128]{2,1,0:T(8,128)(2,1)S(1)}, bf16[8,48,128]{2,1,0:T(8,128)(2,1)S(1)}, u32[]{:S(2)}, u32[]{:S(2)}) collective-permute-start(bf16[8,48,128]{2,1,0:T(8,128)(2,1)S(1)} %collective-permute-done.13.refs_12_), channel_id=1, source_target_pairs={{0,2},{1,3},{2,0},{3,1},{4,6},{5,7},{6,4},{7,5},{8,10},{9,11},{10,... | collective-permute-start | bytes 294920 | tf_op jit(solution)/shard_map/ppermute | solution.py:22
  34.6 1.3 %collective-permute-done.15.refs_14_ = bf16[8,48,128]{2,1,0:T(8,128)(2,1)S(1)} collective-permute-done((bf16[8,48,128]{2,1,0:T(8,128)(2,1)S(1)}, bf16[8,48,128]{2,1,0:T(8,128)(2,1)S(1)}, u32[]{:S(2)}, u32[]{:S(2)}) %collective-permute-start.15) | collective-permute-done | bytes 98336 | tf_op jit(solution)/shard_map/ppermute | solution.py:22
  35.9 1.3 %collective-permute-start.16 = (bf16[8,48,128]{2,1,0:T(8,128)(2,1)S(1)}, bf16[8,48,128]{2,1,0:T(8,128)(2,1)S(1)}, u32[]{:S(2)}, u32[]{:S(2)}) collective-permute-start(bf16[8,48,128]{2,1,0:T(8,128)(2,1)S(1)} %collective-permute-done.15.refs_14_), channel_id=1, source_target_pairs={{0,2},{1,3},{2,0},{3,1},{4,6},{5,7},{6,4},{7,5},{8,10},{9,11},{10,... | collective-permute-start | bytes 294920 | tf_op jit(solution)/shard_map/ppermute | solution.py:22
  37.2 1.0 %collective-permute-done.14.refs_13_ = bf16[8,48,128]{2,1,0:T(8,128)(2,1)S(1)} collective-permute-done((bf16[8,48,128]{2,1,0:T(8,128)(2,1)S(1)}, bf16[8,48,128]{2,1,0:T(8,128)(2,1)S(1)}, u32[]{:S(2)}, u32[]{:S(2)}) %collective-permute-start.14) | collective-permute-done | bytes 98336 | tf_op jit(solution)/shard_map/ppermute | solution.py:22
  38.3 2.3 %collective-permute-done.16.refs_15_ = bf16[8,48,128]{2,1,0:T(8,128)(2,1)S(1)} collective-permute-done((bf16[8,48,128]{2,1,0:T(8,128)(2,1)S(1)}, bf16[8,48,128]{2,1,0:T(8,128)(2,1)S(1)}, u32[]{:S(2)}, u32[]{:S(2)}) %collective-permute-start.16) | collective-permute-done | bytes 98336 | tf_op jit(solution)/shard_map/ppermute | solution.py:22
  40.5 0.5 shard_map.57
  41.0 0.1 collective-permute-start.17
  41.1 1.9 %collective-permute-done.17.other_ref = bf16[8,32,1024]{2,1,0:T(8,128)(2,1)S(1)} collective-permute-done((bf16[8,32,1024]{2,1,0:T(8,128)(2,1)S(1)}, bf16[8,32,1024]{2,1,0:T(8,128)(2,1)S(1)}, u32[]{:S(2)}, u32[]{:S(2)}) %collective-permute-start.17) | collective-permute-done | bytes 524320 | tf_op jit(solution)/shard_map/ppermute | solution.py:22
  43.0 4.5 %shard_map.58 = (bf16[8,2,32,128]{3,2,1,0:T(8,128)(2,1)}, f32[32,1024]{1,0:T(8,128)S(1)}, f32[32,1024]{1,0:T(8,128)S(1)}) custom-call(f32[8,32,1024]{2,1,0:T(8,128)S(1)} %get-tuple-element.20.exact_ref, f32[8,16,1024]{2,1,0:T(8,128)S(1)} %get-tuple-element.21.edges_ref, bf16[8,32,1024]{2,1,0:T(8,128)(2,1)S(1)} %collective-permute-done.17.other_ref, ...), custom_call_target="tpu_custom_call" | custom-call | flops 1073741824 | bytes 4718592 | tf_op jit(solution)/shard_map/pallas_call | solution.py:307
  47.5 3.4 %all-to-all-start = ((bf16[8,2,32,128]{3,2,1,0:T(8,128)(2,1)}), bf16[8,2,32,128]{3,2,1,0:T(8,128)(2,1)S(1)}, u32[]{:S(2)}, u32[]{:S(2)}) async-start(bf16[8,2,32,128]{3,2,1,0:T(8,128)(2,1)} %get-tuple-element.25), calls=%async_computation | async-start | bytes 262144 | tf_op jit(solution)/shard_map/all_to_all | solution.py:387
  50.9 7.5 %all-to-all-done = bf16[8,2,32,128]{3,2,1,0:T(8,128)(2,1)S(1)} async-done(((bf16[8,2,32,128]{3,2,1,0:T(8,128)(2,1)}), bf16[8,2,32,128]{3,2,1,0:T(8,128)(2,1)S(1)}, u32[]{:S(2)}, u32[]{:S(2)}) %all-to-all-start) | async-done | bytes 131104 | tf_op jit(solution)/shard_map/all_to_all | solution.py:387
  58.4 0.1 copy.7
  58.5 0.1 copy.6
  58.8 0.1 copy.9
  58.9 1.6 %collective-permute-start.18 = (bf16[2,8,1024]{2,1,0:T(8,128)(2,1)S(1)}, bf16[2,8,1024]{2,1,0:T(8,128)(2,1)S(1)}, u32[]{:S(2)}, u32[]{:S(2)}) collective-permute-start(bf16[2,8,1024]{2,1,0:T(8,128)(2,1)S(1)} %pad_maximum_fusion.1), channel_id=1, source_target_pairs={{0,16},{16,0},{1,17},{17,1},{2,18},{18,2},{3,19},{19,3},{4,20},{20... | collective-permute-start | bytes 98312 | tf_op jit(solution)/shard_map/ppermute | solution.py:22
  60.4 0.1 fusion.15
  60.5 0.1 collective-permute-start.19
  60.6 2.3 %collective-permute-done.18 = bf16[2,8,1024]{2,1,0:T(8,128)(2,1)S(1)} collective-permute-done((bf16[2,8,1024]{2,1,0:T(8,128)(2,1)S(1)}, bf16[2,8,1024]{2,1,0:T(8,128)(2,1)S(1)}, u32[]{:S(2)}, u32[]{:S(2)}) %collective-permute-start.18) | collective-permute-done | bytes 32800 | tf_op jit(solution)/shard_map/ppermute | solution.py:22
  62.9 0.0 collective-permute-done.19
  62.9 0.2 fusion.5
  63.1 0.1 slice.109
  63.2 0.7 %add_bitcast_fusion = f32[4,1,8,1024]{3,2,1,0:T(8,128)} fusion(f32[4,8,1024]{2,1,0:T(8,128)S(1)} %fusion.5, f32[4,8,1008]{2,1,0:T(8,128)S(1)} %slice.109, f32[1024]{0:T(1024)S(1)} %bitcast.49), kind=kLoop, calls=%fused_computation.30 | loop fusion | flops 98304 | bytes 395264 | tf_op jit(solution)/shard_map/reshape;reshape | solution.py:378
  (24 shorter events, 0.3 us)
Async XLA Ops:
  0.0 19.1 %collective-permute-start.7 = (bf16[1024,512]{1,0:T(8,128)(2,1)}, bf16[1024,512]{1,0:T(8,128)(2,1)S(1)}, u32[]{:S(2)}, u32[]{:S(2)}) collective-permute-start(bf16[1024,512]{1,0:T(8,128)(2,1)} %refs_0_.1), channel_id=1, source_target_pairs={{0,1},{1,0},{2,3},{3,2},{4,5},{5,4},{6,7},{7,6},{8,9},{9,8},{10,11... | collective-permute-start | bytes 3145736 | tf_op jit(solution)/shard_map/ppermute | solution.py:22
  0.5 18.6 %collective-permute-start.8 = (bf16[1024,512]{1,0:T(8,128)(2,1)}, bf16[1024,512]{1,0:T(8,128)(2,1)S(1)}, u32[]{:S(2)}, u32[]{:S(2)}) collective-permute-start(bf16[1024,512]{1,0:T(8,128)(2,1)} %refs_1_.1), channel_id=1, source_target_pairs={{0,1},{1,0},{2,3},{3,2},{4,5},{5,4},{6,7},{7,6},{8,9},{9,8},{10,11... | collective-permute-start | bytes 3145736 | tf_op jit(solution)/shard_map/ppermute | solution.py:22
  1.5 5.7 %collective-permute-start.1 = (bf16[32,1024]{1,0:T(8,128)(2,1)S(1)}, bf16[32,1024]{1,0:T(8,128)(2,1)S(1)}, u32[]{:S(2)}, u32[]{:S(2)}) collective-permute-start(bf16[32,1024]{1,0:T(8,128)(2,1)S(1)} %get-tuple-element.17.refs_0_), channel_id=1, source_target_pairs={{0,4},{1,5},{2,6},{3,7},{4,0},{5,1},{6,2},{7,3},{8,12},{9,13},{10,... | collective-permute-start | bytes 196616 | tf_op jit(solution)/shard_map/ppermute | solution.py:22
  4.6 7.5 %collective-permute-start.3 = (bf16[32,1024]{1,0:T(8,128)(2,1)S(1)}, bf16[32,1024]{1,0:T(8,128)(2,1)S(1)}, u32[]{:S(2)}, u32[]{:S(2)}) collective-permute-start(bf16[32,1024]{1,0:T(8,128)(2,1)S(1)} %get-tuple-element.17.refs_0_), channel_id=1, source_target_pairs={{0,8},{1,9},{2,10},{3,11},{4,12},{5,13},{6,14},{7,15},{8,0},{9,1},... | collective-permute-start | bytes 196616 | tf_op jit(solution)/shard_map/ppermute | solution.py:22
  7.2 6.4 %collective-permute-start.5 = (bf16[32,1024]{1,0:T(8,128)(2,1)S(1)}, bf16[32,1024]{1,0:T(8,128)(2,1)S(1)}, u32[]{:S(2)}, u32[]{:S(2)}) collective-permute-start(bf16[32,1024]{1,0:T(8,128)(2,1)S(1)} %get-tuple-element.17.refs_0_), channel_id=1, source_target_pairs={{0,12},{1,13},{2,14},{3,15},{4,8},{5,9},{6,10},{7,11},{8,4},{9,5},... | collective-permute-start | bytes 196616 | tf_op jit(solution)/shard_map/ppermute | solution.py:22
  7.2 7.7 %collective-permute-start = (bf16[32,1024]{1,0:T(8,128)(2,1)S(1)}, bf16[32,1024]{1,0:T(8,128)(2,1)S(1)}, u32[]{:S(2)}, u32[]{:S(2)}) collective-permute-start(bf16[32,1024]{1,0:T(8,128)(2,1)S(1)} %get-tuple-element.17.refs_0_), channel_id=1, source_target_pairs={{0,2},{1,3},{2,0},{3,1},{4,6},{5,7},{6,4},{7,5},{8,10},{9,11},{10,... | collective-permute-start | bytes 196616 | tf_op jit(solution)/shard_map/ppermute | solution.py:22
  12.0 4.8 %collective-permute-start.2 = (bf16[32,1024]{1,0:T(8,128)(2,1)S(1)}, bf16[32,1024]{1,0:T(8,128)(2,1)S(1)}, u32[]{:S(2)}, u32[]{:S(2)}) collective-permute-start(bf16[32,1024]{1,0:T(8,128)(2,1)S(1)} %collective-permute-done.1.refs_2_), channel_id=1, source_target_pairs={{0,2},{1,3},{2,0},{3,1},{4,6},{5,7},{6,4},{7,5},{8,10},{9,11},{10,... | collective-permute-start | bytes 196616 | tf_op jit(solution)/shard_map/ppermute | solution.py:22
  13.6 4.3 %collective-permute-start.4 = (bf16[32,1024]{1,0:T(8,128)(2,1)S(1)}, bf16[32,1024]{1,0:T(8,128)(2,1)S(1)}, u32[]{:S(2)}, u32[]{:S(2)}) collective-permute-start(bf16[32,1024]{1,0:T(8,128)(2,1)S(1)} %collective-permute-done.3.refs_4_), channel_id=1, source_target_pairs={{0,2},{1,3},{2,0},{3,1},{4,6},{5,7},{6,4},{7,5},{8,10},{9,11},{10,... | collective-permute-start | bytes 196616 | tf_op jit(solution)/shard_map/ppermute | solution.py:22
  14.9 4.3 %collective-permute-start.6 = (bf16[32,1024]{1,0:T(8,128)(2,1)S(1)}, bf16[32,1024]{1,0:T(8,128)(2,1)S(1)}, u32[]{:S(2)}, u32[]{:S(2)}) collective-permute-start(bf16[32,1024]{1,0:T(8,128)(2,1)S(1)} %collective-permute-done.5.refs_6_), channel_id=1, source_target_pairs={{0,2},{1,3},{2,0},{3,1},{4,6},{5,7},{6,4},{7,5},{8,10},{9,11},{10,... | collective-permute-start | bytes 196616 | tf_op jit(solution)/shard_map/ppermute | solution.py:22
  19.1 23.9 %copy-start.1 = (bf16[1024,512]{1,0:T(8,128)(2,1)S(1)}, bf16[1024,512]{1,0:T(8,128)(2,1)}, u32[]{:S(2)}) copy-start(bf16[1024,512]{1,0:T(8,128)(2,1)} %refs_1_.1) | copy-start | bytes 3145732
  22.4 20.6 %copy-start = (bf16[1024,512]{1,0:T(8,128)(2,1)S(1)}, bf16[1024,512]{1,0:T(8,128)(2,1)}, u32[]{:S(2)}) copy-start(bf16[1024,512]{1,0:T(8,128)(2,1)} %refs_0_.1) | copy-start | bytes 3145732
  22.4 4.0 %collective-permute-start.9 = (bf16[8,16,128]{2,1,0:T(8,128)(2,1)S(1)}, bf16[8,16,128]{2,1,0:T(8,128)(2,1)S(1)}, u32[]{:S(2)}, u32[]{:S(2)}) collective-permute-start(bf16[8,16,128]{2,1,0:T(8,128)(2,1)S(1)} %get-tuple-element.19), channel_id=1, source_target_pairs={{0,16},{16,0},{1,17},{17,1},{2,18},{18,2},{3,19},{19,3},{4,20},{20... | collective-permute-start | bytes 98312 | tf_op jit(solution)/shard_map/ppermute | solution.py:22
  26.4 5.1 %collective-permute-start.11 = (bf16[8,48,128]{2,1,0:T(8,128)(2,1)S(1)}, bf16[8,48,128]{2,1,0:T(8,128)(2,1)S(1)}, u32[]{:S(2)}, u32[]{:S(2)}) collective-permute-start(bf16[8,48,128]{2,1,0:T(8,128)(2,1)S(1)} %constant_dynamic-update-slice_fusion.refs_8_), channel_id=1, source_target_pairs={{0,4},{1,5},{2,6},{3,7},{4,0},{5,1},{6,2},{7,3},{8,12},{9,13},{10,... | collective-permute-start | bytes 294920 | tf_op jit(solution)/shard_map/ppermute | solution.py:22
  27.1 6.6 %collective-permute-start.13 = (bf16[8,48,128]{2,1,0:T(8,128)(2,1)S(1)}, bf16[8,48,128]{2,1,0:T(8,128)(2,1)S(1)}, u32[]{:S(2)}, u32[]{:S(2)}) collective-permute-start(bf16[8,48,128]{2,1,0:T(8,128)(2,1)S(1)} %constant_dynamic-update-slice_fusion.refs_8_), channel_id=1, source_target_pairs={{0,8},{1,9},{2,10},{3,11},{4,12},{5,13},{6,14},{7,15},{8,0},{9,1},... | collective-permute-start | bytes 294920 | tf_op jit(solution)/shard_map/ppermute | solution.py:22
  29.5 6.4 %collective-permute-start.15 = (bf16[8,48,128]{2,1,0:T(8,128)(2,1)S(1)}, bf16[8,48,128]{2,1,0:T(8,128)(2,1)S(1)}, u32[]{:S(2)}, u32[]{:S(2)}) collective-permute-start(bf16[8,48,128]{2,1,0:T(8,128)(2,1)S(1)} %constant_dynamic-update-slice_fusion.refs_8_), channel_id=1, source_target_pairs={{0,12},{1,13},{2,14},{3,15},{4,8},{5,9},{6,10},{7,11},{8,4},{9,5},... | collective-permute-start | bytes 294920 | tf_op jit(solution)/shard_map/ppermute | solution.py:22
  30.8 6.5 %collective-permute-start.10 = (bf16[8,48,128]{2,1,0:T(8,128)(2,1)S(1)}, bf16[8,48,128]{2,1,0:T(8,128)(2,1)S(1)}, u32[]{:S(2)}, u32[]{:S(2)}) collective-permute-start(bf16[8,48,128]{2,1,0:T(8,128)(2,1)S(1)} %constant_dynamic-update-slice_fusion.refs_8_), channel_id=1, source_target_pairs={{0,2},{1,3},{2,0},{3,1},{4,6},{5,7},{6,4},{7,5},{8,10},{9,11},{10,... | collective-permute-start | bytes 294920 | tf_op jit(solution)/shard_map/ppermute | solution.py:22
  31.5 5.7 %collective-permute-start.12 = (bf16[8,48,128]{2,1,0:T(8,128)(2,1)S(1)}, bf16[8,48,128]{2,1,0:T(8,128)(2,1)S(1)}, u32[]{:S(2)}, u32[]{:S(2)}) collective-permute-start(bf16[8,48,128]{2,1,0:T(8,128)(2,1)S(1)} %collective-permute-done.11.refs_10_), channel_id=1, source_target_pairs={{0,2},{1,3},{2,0},{3,1},{4,6},{5,7},{6,4},{7,5},{8,10},{9,11},{10,... | collective-permute-start | bytes 294920 | tf_op jit(solution)/shard_map/ppermute | solution.py:22
  33.6 4.6 %collective-permute-start.14 = (bf16[8,48,128]{2,1,0:T(8,128)(2,1)S(1)}, bf16[8,48,128]{2,1,0:T(8,128)(2,1)S(1)}, u32[]{:S(2)}, u32[]{:S(2)}) collective-permute-start(bf16[8,48,128]{2,1,0:T(8,128)(2,1)S(1)} %collective-permute-done.13.refs_12_), channel_id=1, source_target_pairs={{0,2},{1,3},{2,0},{3,1},{4,6},{5,7},{6,4},{7,5},{8,10},{9,11},{10,... | collective-permute-start | bytes 294920 | tf_op jit(solution)/shard_map/ppermute | solution.py:22
  35.9 4.6 %collective-permute-start.16 = (bf16[8,48,128]{2,1,0:T(8,128)(2,1)S(1)}, bf16[8,48,128]{2,1,0:T(8,128)(2,1)S(1)}, u32[]{:S(2)}, u32[]{:S(2)}) collective-permute-start(bf16[8,48,128]{2,1,0:T(8,128)(2,1)S(1)} %collective-permute-done.15.refs_14_), channel_id=1, source_target_pairs={{0,2},{1,3},{2,0},{3,1},{4,6},{5,7},{6,4},{7,5},{8,10},{9,11},{10,... | collective-permute-start | bytes 294920 | tf_op jit(solution)/shard_map/ppermute | solution.py:22
  41.0 2.0 %collective-permute-start.17 = (bf16[8,32,1024]{2,1,0:T(8,128)(2,1)S(1)}, bf16[8,32,1024]{2,1,0:T(8,128)(2,1)S(1)}, u32[]{:S(2)}, u32[]{:S(2)}) collective-permute-start(bf16[8,32,1024]{2,1,0:T(8,128)(2,1)S(1)} %get-tuple-element.22), channel_id=1, source_target_pairs={{0,1},{1,0},{2,3},{3,2},{4,5},{5,4},{6,7},{7,6},{8,9},{9,8},{10,11... | collective-permute-start | bytes 1572872 | tf_op jit(solution)/shard_map/ppermute | solution.py:22
  47.5 10.9 %all-to-all-start = ((bf16[8,2,32,128]{3,2,1,0:T(8,128)(2,1)}), bf16[8,2,32,128]{3,2,1,0:T(8,128)(2,1)S(1)}, u32[]{:S(2)}, u32[]{:S(2)}) async-start(bf16[8,2,32,128]{3,2,1,0:T(8,128)(2,1)} %get-tuple-element.25), calls=%async_computation | async-start | bytes 262144 | tf_op jit(solution)/shard_map/all_to_all | solution.py:387
  58.9 4.0 %collective-permute-start.18 = (bf16[2,8,1024]{2,1,0:T(8,128)(2,1)S(1)}, bf16[2,8,1024]{2,1,0:T(8,128)(2,1)S(1)}, u32[]{:S(2)}, u32[]{:S(2)}) collective-permute-start(bf16[2,8,1024]{2,1,0:T(8,128)(2,1)S(1)} %pad_maximum_fusion.1), channel_id=1, source_target_pairs={{0,16},{16,0},{1,17},{17,1},{2,18},{18,2},{3,19},{19,3},{4,20},{20... | collective-permute-start | bytes 98312 | tf_op jit(solution)/shard_map/ppermute | solution.py:22
  60.5 2.4 %collective-permute-start.19 = (bf16[2,4,8,1024]{3,2,1,0:T(8,128)(2,1)S(1)}, bf16[2,4,8,1024]{3,2,1,0:T(8,128)(2,1)S(1)}, u32[]{:S(2)}, u32[]{:S(2)}) collective-permute-start(bf16[2,4,8,1024]{3,2,1,0:T(8,128)(2,1)S(1)} %pad_maximum_fusion), channel_id=1, source_target_pairs={{0,1},{1,0},{2,3},{3,2},{4,5},{5,4},{6,7},{7,6},{8,9},{9,8},{10,11... | collective-permute-start | bytes 393224 | tf_op jit(solution)/shard_map/ppermute | solution.py:22

commit v6 on v5

--- a/solution.py
+++ b/solution.py
@@ -7,7 +7,7 @@
 from jax.experimental.pallas import tpu as pltpu
 from jax.sharding import PartitionSpec as P
 
-P_SIZE = 1024
+
 RANK = 8
 NDIR = 16
 ITERS = 2
@@ -170,6 +170,7 @@
         ),
     )(*blocks, *[off_chip(each) if fetch else each for each in factors[:2]], *factors[2:])
 
+
 def first_kernel(chips, layers, *refs):
     blocks, factors = refs[:chips], refs[chips : chips + 4]
     terms_ref, edges_ref, a_kept, b_kept, sems = refs[chips + 4 :]
@@ -255,19 +256,12 @@
     )(state, *blocks, *parts)
 
 
-def second_kernel(chips, layers, exact_ref, edges_ref, other_ref, tables_ref, *refs):
-    factors = refs[:4]
-    sent_ref, own_ref, beside_ref, read_ref, states_ref, updated_ref = refs[4:]
-    me = lax.axis_index("mom")
-    core, chip = me & 1, me >> 1
-    away = 2 * core - 1
-    _, rows, size = exact_ref.shape
+def inner_kernel(layers, exact_ref, edges_ref, tables_ref, read_ref):
+    chips, rows, size = exact_ref.shape
     depth = rows // layers
-    read_ref[:, size:] = jnp.zeros((rows, read_ref.shape[1] - size), jnp.float32)
 
     @pl.loop(0, chips)
     def _(cell):
-        before, after = (cell - 1 + core) & (chips - 1), (cell + core) & (chips - 1)
         for at in range(0, size, 128):
             lanes = slice(at, at + 128)
             center = exact_ref[cell, :, lanes]
@@ -275,19 +269,51 @@
             behind = jnp.concatenate([edges[:depth], center[: rows - depth]], axis=0)
             ahead = jnp.concatenate([center[depth:], edges[depth:]], axis=0)
             read = center - courant * upwind(center, behind, ahead, tables_ref[0:2, lanes])
-            behind = other_ref[before, :, lanes].astype(jnp.float32)
-            ahead = other_ref[after, :, lanes].astype(jnp.float32)
-            read = read - courant * upwind(center, behind, ahead, tables_ref[2:4, lanes])
             levels = center.reshape(layers, depth, 128)
             behind = pltpu.roll(levels, 1, 1).reshape(rows, 128)
             ahead = pltpu.roll(levels, depth - 1, 1).reshape(rows, 128)
             read = read - courant * upwind(center, behind, ahead, tables_ref[4:6, lanes])
-            read_ref[:, lanes] = read
-        for at in range(0, size, 128):
+            speeds = tables_ref[2:3, lanes] - tables_ref[3:4, lanes]
+            read_ref[cell, :, lanes] = read - courant * speeds * center
+
+
+def inner_update(exact, edges, tables, layers):
+    return pl.pallas_call(
+        functools.partial(inner_kernel, layers),
+        out_shape=jax.ShapeDtypeStruct(exact.shape, jnp.float32),
+        compiler_params=pltpu.CompilerParams(vmem_limit_bytes=8 << 20),
+        cost_estimate=pl.CostEstimate(
+            flops=20 * exact.size, bytes_accessed=8 * exact.size, transcendentals=0
+        ),
+    )(exact, edges, tables)
+
+
+def drifted(read, after, drift):
+    rolled = pltpu.roll(read, 128 - NDIR, 1)
+    inside = lax.broadcasted_iota(jnp.int32, read.shape, 1) < 128 - NDIR
+    upper = jnp.where(inside, rolled, 0.0 if after is None else after)
+    return read + drift * (upper - read), rolled
+
+
+def second_kernel(chips, inner_ref, other_ref, tables_ref, *refs):
+    factors = refs[:4]
+    sent_ref, own_ref, beside_ref, states_ref, updated_ref = refs[4:]
+    me = lax.axis_index("mom")
+    core, chip = me & 1, me >> 1
+    away = 2 * core - 1
+    _, rows, size = inner_ref.shape
+
+    @pl.loop(0, chips)
+    def _(cell):
+        before, after = (cell - 1 + core) & (chips - 1), (cell + core) & (chips - 1)
+        rolled = None
+        for at in reversed(range(0, size, 128)):
             lanes = slice(at, at + 128)
-            read = read_ref[:, lanes]
-            upper = read_ref[:, at + NDIR : at + NDIR + 128]
-            state = read + tables_ref[6:7, lanes] * (upper - read)
+            speeds = courant * tables_ref[2:4, lanes]
+            read = inner_ref[cell, :, lanes]
+            read += speeds[0:1] * other_ref[before, :, lanes].astype(jnp.float32)
+            read -= speeds[1:2] * other_ref[after, :, lanes].astype(jnp.float32)
+            state, rolled = drifted(read, rolled, tables_ref[6:7, lanes])
             states_ref[cell, :, lanes] = state.astype(jnp.bfloat16)
             updated_ref[cell, :, lanes] = state
 
@@ -301,18 +327,17 @@
         sent_ref[(here + away) & (chips - 1), 1] = part
 
 
-def second_collision(exact, edges, other, tables, factors, layers):
-    chips, rows, size = exact.shape
+def second_collision(inner, other, tables, factors):
+    chips, rows, size = inner.shape
     columns = factors[0].shape[1]
     return pl.pallas_call(
-        functools.partial(second_kernel, chips, layers),
+        functools.partial(second_kernel, chips),
         out_shape=[
             jax.ShapeDtypeStruct((chips, 2, rows, 2 * columns // RANK), jnp.bfloat16),
             jax.ShapeDtypeStruct((rows, size), jnp.float32),
             jax.ShapeDtypeStruct((rows, size), jnp.float32),
         ],
         scratch_shapes=[
-            pltpu.VMEM((rows, size + 128), jnp.float32),
             pltpu.VMEM((chips, rows, size), jnp.bfloat16),
             pltpu.VMEM((chips, rows, size), jnp.float32),
         ],
@@ -322,7 +347,72 @@
             bytes_accessed=2 * (chips * rows * size + 4 * size * columns),
             transcendentals=0,
         ),
-    )(exact, edges, other, tables, *factors)
+    )(inner, other, tables, *factors)
+
+
+def arrive_kernel(layers, got_ref, own_ref, beside_ref, exact_ref, edges_ref, cells_ref):
+    chips, _, rows, mine = got_ref.shape
+    depth = rows // layers
+    for source in range(chips):
+        lanes = slice(source * mine, (source + 1) * mine)
+        collided = own_ref[:, lanes] + collide_rate * got_ref[source, 0].astype(jnp.float32)
+        beyond = beside_ref[:, lanes] + collide_rate * got_ref[source, 1].astype(jnp.float32)
+        exact_ref[:, lanes] = collided
+        edges = jnp.concatenate([collided[rows - depth :], collided[:depth]], axis=0)
+        edges_ref[0, :, lanes] = edges.astype(jnp.bfloat16)
+        cells_ref[0, :, lanes] = collided.astype(jnp.bfloat16)
+        cells_ref[1, :, lanes] = beyond.astype(jnp.bfloat16)
+
+
+def last_kernel(layers, exact_ref, edges_ref, cells_ref, tables_ref, out_ref):
+    core = lax.axis_index("mom") & 1
+    rows, size = exact_ref.shape
+    depth = rows // layers
+    rolled = None
+    for at in reversed(range(0, size, 128)):
+        lanes = slice(at, at + 128)
+        center = exact_ref[:, lanes]
+        edges = edges_ref[0, :, lanes].astype(jnp.float32)
+        behind = jnp.concatenate([edges[:depth], center[: rows - depth]], axis=0)
+        ahead = jnp.concatenate([center[depth:], edges[depth:]], axis=0)
+        read = center - courant * upwind(center, behind, ahead, tables_ref[0:2, lanes])
+        behind = cells_ref[1 - core, :, lanes].astype(jnp.float32)
+        ahead = cells_ref[core, :, lanes].astype(jnp.float32)
+        read = read - courant * upwind(center, behind, ahead, tables_ref[2:4, lanes])
+        levels = center.reshape(layers, depth, 128)
+        behind = pltpu.roll(levels, 1, 1).reshape(rows, 128)
+        ahead = pltpu.roll(levels, depth - 1, 1).reshape(rows, 128)
+        read = read - courant * upwind(center, behind, ahead, tables_ref[4:6, lanes])
+        out_ref[:, lanes], rolled = drifted(read, rolled, tables_ref[6:7, lanes])
+
+
+def settled(state, sent, beside, tables, layers):
+    rows, size = state.shape
+    chips = sent.shape[0]
+    same = [[c + 2 * k for k in range(chips)] for c in range(2)]
+    got = lax.all_to_all(
+        sent, "mom", split_axis=0, concat_axis=0, tiled=True, axis_index_groups=same
+    )
+    params = pltpu.CompilerParams(vmem_limit_bytes=4 << 20)
+    cost = pl.CostEstimate(flops=20 * state.size, bytes_accessed=12 * state.size, transcendentals=0)
+    exact, edges, cells = pl.pallas_call(
+        functools.partial(arrive_kernel, layers),
+        out_shape=[
+            jax.ShapeDtypeStruct((rows, size), jnp.float32),
+            jax.ShapeDtypeStruct((1, 2 * rows // layers, size), jnp.bfloat16),
+            jax.ShapeDtypeStruct((2, rows, size), jnp.bfloat16),
+        ],
+        compiler_params=params,
+        cost_estimate=cost,
+    )(got, state, beside)
+    edges = edge_layers(edges, "space")
+    cells = swap(cells, "mom", 1)
+    return pl.pallas_call(
+        functools.partial(last_kernel, layers),
+        out_shape=jax.ShapeDtypeStruct((rows, size), jnp.float32),
+        compiler_params=params,
+        cost_estimate=cost,
+    )(exact, edges, cells, tables)
 
 
 def edge_layers(edges, axis):
@@ -357,7 +447,6 @@
 def per_device(distribution, a_factor, b_factor, velocity, drift):
     layers, owned, depth, size = distribution.shape
     assert owned == 1
-    chips = lax.axis_size("mom") // 2
     factors = (a_factor, b_factor, swap(a_factor, "mom", 1), swap(b_factor, "mom", 1))
     state, rounded, tables = prepare(distribution.reshape(layers * depth, size), velocity, drift)
     if 2 * (a_factor.shape[1] // RANK) % 128:
@@ -366,14 +455,15 @@
             state = settle(state, sent, beside.astype(jnp.float32), tables, layers)
             rounded = state.astype(jnp.bfloat16)
         return state.reshape(distribution.shape)
-    for substep in range(0, ITERS, 2):
+    for _ in range(0, ITERS, 2):
         blocks = gathered(rounded, "mom")
         terms, edges = first_collision(blocks, factors, layers)
         parts = gathered(jnp.concatenate([terms, edge_layers(edges, "space")], axis=1), "mom")
         exact, edges, cells = collided_cells(state, blocks, parts)
         other = swap(cells, "mom", 1)
-        sent, state, beside = second_collision(exact, edges, other, tables, factors, layers)
-        state = settle(state, sent, beside, tables, layers)
+        inner = inner_update(exact, edges, tables, layers)
+        sent, state, beside = second_collision(inner, other, tables, factors)
+        state = settled(state, sent, beside, tables, layers)
         rounded = state.astype(jnp.bfloat16)
     return state.reshape(distribution.shape)
 
@@ -412,6 +502,5 @@
 def solution(mesh):
     in_specs = (P("space", "mom", None, None), P(None, "mom"), P(None, "mom"), P(), P())
     out_specs = P("space", "mom", None, None)
-    return jax.shard_map(
-        per_device, mesh=mesh, in_specs=in_specs, out_specs=out_specs, check_vma=False
-    )
+
+    return jax.shard_map(per_device, mesh=mesh, in_specs=in_specs, out_specs=out_specs, check_vma=False)

time: 64.1 us -> 63.6 us (level)
  blocking collectives: 0 us -> 10.9 us
  waiting for transfers between devices: 26.1 us -> 19.8 us
  starting transfers between devices: 26.8 us -> 23.6 us
  other arithmetic: 1.02 us -> 0 us
    all_to_all x0 -> x1, blocking collectives: none -> 10.9 us  [settled(): lax.all_to_all(sent, 'mom', split_axis=0, concat_axis=0, tiled=True, axis...]
    all_to_all x1 -> x0, waiting for transfers between devices: 7.45 us -> none  [settle(): lax.all_to_all(sent, 'mom', split_axis=0, concat_axis=0, tiled=True, axis...]
    all_to_all x1 -> x0, starting transfers between devices: 3.37 us -> none  [settle(): lax.all_to_all(sent, 'mom', split_axis=0, concat_axis=0, tiled=True, axis...]
    ppermute x20, waiting for transfers between devices: 18.7 us -> 19.8 us  [swap(): return lax.ppermute(block, axis, [(i, i ^ bits) for i in range(count)])]
    another operation x4 -> x0, other arithmetic: 0.77 us -> none  [the longest x1 0.68 us: per_device(): return state.reshape(distribution.shape)]
    pallas_call x1 -> x4, Pallas kernels: 4.51 us -> 4.3 us  [the longest x1 2.77 us: second_collision(): pl.pallas_call(functools.partial(second_kernel, chips), out_shape=[jax.Sh...]
  transfers between devices with their start and end apart: 21 -> 20, of which waited for: 12 -> 12; matrix products, arithmetic and copies ran while one was open for 0% -> 0% of each run, Pallas kernels for 1% -> 3%
where the time goes in v6:
time: 63.6 us; the launch traced here: 63.4 us
  starting transfers between devices  23.6 us (37%)
  waiting for transfers between devices  19.8 us (31%)
  blocking collectives  10.9 us (17%)
  Pallas kernels  8.95 us (14%)
    ppermute x20, starting transfers between devices, swap(): return lax.ppermute(block, axis, [(i, i ^ bits) for i in range(count)])  23.6 us
    ppermute x20, waiting for transfers between devices, swap(): return lax.ppermute(block, axis, [(i, i ^ bits) for i in range(count)])  19.8 us
    all_to_all x1, blocking collectives, settled(): lax.all_to_all(sent, 'mom', split_axis=0, concat_axis=0, tiled=True, axis...  10.9 us
    pallas_call x1, Pallas kernels, first_collision(): pl.pallas_call(functools.partial(first_kernel, chips, layers), out_shape=...  3.23 us
    pallas_call x1, Pallas kernels, second_collision(): pl.pallas_call(functools.partial(second_kernel, chips), out_shape=[jax.Sh...  2.77 us
  transfers between devices with their start and end apart: 20, of which 12 were waited for; matrix products, arithmetic and copies ran while one was open for 0% of the time, Pallas kernels for 3%

profile of v6, /device:TPU:0, one launch (start us, length us, event | category | flops | bytes accessed | tf_op | source)
XLA Modules:
  0.0 63.4 jit_solution(12092968013999845373)
XLA Ops:
  0.0 0.5 collective-permute-start.7
  0.5 0.0 collective-permute-start.8
  0.5 0.9 %shard_map.55 = (f32[32,1024]{1,0:T(8,128)S(1)}, bf16[32,1024]{1,0:T(8,128)(2,1)S(1)}, f32[8,1024]{1,0:T(8,128)S(1)}) custom-call(f32[32,1024]{1,0:T(8,128)} %bitcast.5, f32[3,1024]{1,0:T(4,128)} %velocity_hbm.1, f32[1,1024]{1,0:T(1,128)} %bitcast.6), custom_call_target="tpu_custom_call" | custom-call | flops 32768 | bytes 327680 | tf_op jit(solution)/shard_map/pallas_call | solution.py:64
  1.5 5.1 %collective-permute-start.5 = (bf16[32,1024]{1,0:T(8,128)(2,1)S(1)}, bf16[32,1024]{1,0:T(8,128)(2,1)S(1)}, u32[]{:S(2)}, u32[]{:S(2)}) collective-permute-start(bf16[32,1024]{1,0:T(8,128)(2,1)S(1)} %get-tuple-element.20.refs_0_), channel_id=1, source_target_pairs={{0,12},{1,13},{2,14},{3,15},{4,8},{5,9},{6,10},{7,11},{8,4},{9,5},... | collective-permute-start | bytes 196616 | tf_op jit(solution)/shard_map/ppermute | solution.py:22
  6.6 0.0 collective-permute-start.3
  6.6 0.6 %collective-permute-start.1 = (bf16[32,1024]{1,0:T(8,128)(2,1)S(1)}, bf16[32,1024]{1,0:T(8,128)(2,1)S(1)}, u32[]{:S(2)}, u32[]{:S(2)}) collective-permute-start(bf16[32,1024]{1,0:T(8,128)(2,1)S(1)} %get-tuple-element.20.refs_0_), channel_id=1, source_target_pairs={{0,4},{1,5},{2,6},{3,7},{4,0},{5,1},{6,2},{7,3},{8,12},{9,13},{10,... | collective-permute-start | bytes 196616 | tf_op jit(solution)/shard_map/ppermute | solution.py:22
  7.2 1.9 %collective-permute-done.5.refs_6_ = bf16[32,1024]{1,0:T(8,128)(2,1)S(1)} collective-permute-done((bf16[32,1024]{1,0:T(8,128)(2,1)S(1)}, bf16[32,1024]{1,0:T(8,128)(2,1)S(1)}, u32[]{:S(2)}, u32[]{:S(2)}) %collective-permute-start.5) | collective-permute-done | bytes 65568 | tf_op jit(solution)/shard_map/ppermute | solution.py:22
  9.1 1.7 %collective-permute-start = (bf16[32,1024]{1,0:T(8,128)(2,1)S(1)}, bf16[32,1024]{1,0:T(8,128)(2,1)S(1)}, u32[]{:S(2)}, u32[]{:S(2)}) collective-permute-start(bf16[32,1024]{1,0:T(8,128)(2,1)S(1)} %get-tuple-element.20.refs_0_), channel_id=1, source_target_pairs={{0,2},{1,3},{2,0},{3,1},{4,6},{5,7},{6,4},{7,5},{8,10},{9,11},{10,... | collective-permute-start | bytes 196616 | tf_op jit(solution)/shard_map/ppermute | solution.py:22
  10.9 1.5 %collective-permute-done.3.refs_4_ = bf16[32,1024]{1,0:T(8,128)(2,1)S(1)} collective-permute-done((bf16[32,1024]{1,0:T(8,128)(2,1)S(1)}, bf16[32,1024]{1,0:T(8,128)(2,1)S(1)}, u32[]{:S(2)}, u32[]{:S(2)}) %collective-permute-start.3) | collective-permute-done | bytes 65568 | tf_op jit(solution)/shard_map/ppermute | solution.py:22
  12.4 1.5 %collective-permute-start.6 = (bf16[32,1024]{1,0:T(8,128)(2,1)S(1)}, bf16[32,1024]{1,0:T(8,128)(2,1)S(1)}, u32[]{:S(2)}, u32[]{:S(2)}) collective-permute-start(bf16[32,1024]{1,0:T(8,128)(2,1)S(1)} %collective-permute-done.5.refs_6_), channel_id=1, source_target_pairs={{0,2},{1,3},{2,0},{3,1},{4,6},{5,7},{6,4},{7,5},{8,10},{9,11},{10,... | collective-permute-start | bytes 196616 | tf_op jit(solution)/shard_map/ppermute | solution.py:22
  13.9 0.0 collective-permute-done.1.refs_2_
  13.9 0.5 collective-permute-start.4
  14.4 0.0 collective-permute-done.refs_1_
  14.4 1.5 %collective-permute-start.2 = (bf16[32,1024]{1,0:T(8,128)(2,1)S(1)}, bf16[32,1024]{1,0:T(8,128)(2,1)S(1)}, u32[]{:S(2)}, u32[]{:S(2)}) collective-permute-start(bf16[32,1024]{1,0:T(8,128)(2,1)S(1)} %collective-permute-done.1.refs_2_), channel_id=1, source_target_pairs={{0,2},{1,3},{2,0},{3,1},{4,6},{5,7},{6,4},{7,5},{8,10},{9,11},{10,... | collective-permute-start | bytes 196616 | tf_op jit(solution)/shard_map/ppermute | solution.py:22
  15.9 1.4 %collective-permute-done.6.refs_7_ = bf16[32,1024]{1,0:T(8,128)(2,1)S(1)} collective-permute-done((bf16[32,1024]{1,0:T(8,128)(2,1)S(1)}, bf16[32,1024]{1,0:T(8,128)(2,1)S(1)}, u32[]{:S(2)}, u32[]{:S(2)}) %collective-permute-start.6) | collective-permute-done | bytes 65568 | tf_op jit(solution)/shard_map/ppermute | solution.py:22
  17.3 1.3 %collective-permute-done.4.refs_5_ = bf16[32,1024]{1,0:T(8,128)(2,1)S(1)} collective-permute-done((bf16[32,1024]{1,0:T(8,128)(2,1)S(1)}, bf16[32,1024]{1,0:T(8,128)(2,1)S(1)}, u32[]{:S(2)}, u32[]{:S(2)}) %collective-permute-start.4) | collective-permute-done | bytes 65568 | tf_op jit(solution)/shard_map/ppermute | solution.py:22
  18.7 0.7 %collective-permute-done.2.refs_3_ = bf16[32,1024]{1,0:T(8,128)(2,1)S(1)} collective-permute-done((bf16[32,1024]{1,0:T(8,128)(2,1)S(1)}, bf16[32,1024]{1,0:T(8,128)(2,1)S(1)}, u32[]{:S(2)}, u32[]{:S(2)}) %collective-permute-start.2) | collective-permute-done | bytes 65568 | tf_op jit(solution)/shard_map/ppermute | solution.py:22
  19.4 0.0 collective-permute-done.7.refs_10_.refs_2_
  19.4 0.0 collective-permute-done.8.refs_11_.refs_3_
  19.4 3.2 %shard_map.56 = (bf16[8,32,128]{2,1,0:T(8,128)(2,1)S(1)}, bf16[8,16,128]{2,1,0:T(8,128)(2,1)S(1)}) custom-call(bf16[32,1024]{1,0:T(8,128)(2,1)S(1)} %get-tuple-element.20.refs_0_, bf16[32,1024]{1,0:T(8,128)(2,1)S(1)} %collective-permute-done.refs_1_, bf16[32,1024]{1,0:T(8,128)(2,1)S(1)} %collective-permute-done.1.refs_2_, ...), custom_call_target="tpu_custom_call" | custom-call | flops 1073741824 | bytes 4718592 | tf_op jit(solution)/shard_map/pallas_call | solution.py:204
  22.6 1.6 %collective-permute-start.9 = (bf16[8,16,128]{2,1,0:T(8,128)(2,1)S(1)}, bf16[8,16,128]{2,1,0:T(8,128)(2,1)S(1)}, u32[]{:S(2)}, u32[]{:S(2)}) collective-permute-start(bf16[8,16,128]{2,1,0:T(8,128)(2,1)S(1)} %get-tuple-element.22), channel_id=1, source_target_pairs={{0,16},{16,0},{1,17},{17,1},{2,18},{18,2},{3,19},{19,3},{4,20},{20... | collective-permute-start | bytes 98312 | tf_op jit(solution)/shard_map/ppermute | solution.py:22
  24.2 2.4 %collective-permute-done.9 = bf16[8,16,128]{2,1,0:T(8,128)(2,1)S(1)} collective-permute-done((bf16[8,16,128]{2,1,0:T(8,128)(2,1)S(1)}, bf16[8,16,128]{2,1,0:T(8,128)(2,1)S(1)}, u32[]{:S(2)}, u32[]{:S(2)}) %collective-permute-start.9) | collective-permute-done | bytes 32800 | tf_op jit(solution)/shard_map/ppermute | solution.py:22
  26.6 3.1 %collective-permute-start.15 = (bf16[8,48,128]{2,1,0:T(8,128)(2,1)S(1)}, bf16[8,48,128]{2,1,0:T(8,128)(2,1)S(1)}, u32[]{:S(2)}, u32[]{:S(2)}) collective-permute-start(bf16[8,48,128]{2,1,0:T(8,128)(2,1)S(1)} %constant_dynamic-update-slice_fusion.refs_8_), channel_id=1, source_target_pairs={{0,12},{1,13},{2,14},{3,15},{4,8},{5,9},{6,10},{7,11},{8,4},{9,5},... | collective-permute-start | bytes 294920 | tf_op jit(solution)/shard_map/ppermute | solution.py:22
  29.7 0.0 collective-permute-start.13
  29.7 1.3 %collective-permute-start.11 = (bf16[8,48,128]{2,1,0:T(8,128)(2,1)S(1)}, bf16[8,48,128]{2,1,0:T(8,128)(2,1)S(1)}, u32[]{:S(2)}, u32[]{:S(2)}) collective-permute-start(bf16[8,48,128]{2,1,0:T(8,128)(2,1)S(1)} %constant_dynamic-update-slice_fusion.refs_8_), channel_id=1, source_target_pairs={{0,4},{1,5},{2,6},{3,7},{4,0},{5,1},{6,2},{7,3},{8,12},{9,13},{10,... | collective-permute-start | bytes 294920 | tf_op jit(solution)/shard_map/ppermute | solution.py:22
  31.0 1.0 %collective-permute-start.10 = (bf16[8,48,128]{2,1,0:T(8,128)(2,1)S(1)}, bf16[8,48,128]{2,1,0:T(8,128)(2,1)S(1)}, u32[]{:S(2)}, u32[]{:S(2)}) collective-permute-start(bf16[8,48,128]{2,1,0:T(8,128)(2,1)S(1)} %constant_dynamic-update-slice_fusion.refs_8_), channel_id=1, source_target_pairs={{0,2},{1,3},{2,0},{3,1},{4,6},{5,7},{6,4},{7,5},{8,10},{9,11},{10,... | collective-permute-start | bytes 294920 | tf_op jit(solution)/shard_map/ppermute | solution.py:22
  32.0 1.4 %collective-permute-done.15.refs_14_ = bf16[8,48,128]{2,1,0:T(8,128)(2,1)S(1)} collective-permute-done((bf16[8,48,128]{2,1,0:T(8,128)(2,1)S(1)}, bf16[8,48,128]{2,1,0:T(8,128)(2,1)S(1)}, u32[]{:S(2)}, u32[]{:S(2)}) %collective-permute-start.15) | collective-permute-done | bytes 98336 | tf_op jit(solution)/shard_map/ppermute | solution.py:22
  33.4 1.3 %collective-permute-start.16 = (bf16[8,48,128]{2,1,0:T(8,128)(2,1)S(1)}, bf16[8,48,128]{2,1,0:T(8,128)(2,1)S(1)}, u32[]{:S(2)}, u32[]{:S(2)}) collective-permute-start(bf16[8,48,128]{2,1,0:T(8,128)(2,1)S(1)} %collective-permute-done.15.refs_14_), channel_id=1, source_target_pairs={{0,2},{1,3},{2,0},{3,1},{4,6},{5,7},{6,4},{7,5},{8,10},{9,11},{10,... | collective-permute-start | bytes 294920 | tf_op jit(solution)/shard_map/ppermute | solution.py:22
  34.7 1.7 %collective-permute-done.13.refs_12_ = bf16[8,48,128]{2,1,0:T(8,128)(2,1)S(1)} collective-permute-done((bf16[8,48,128]{2,1,0:T(8,128)(2,1)S(1)}, bf16[8,48,128]{2,1,0:T(8,128)(2,1)S(1)}, u32[]{:S(2)}, u32[]{:S(2)}) %collective-permute-start.13) | collective-permute-done | bytes 98336 | tf_op jit(solution)/shard_map/ppermute | solution.py:22
  36.5 0.7 %collective-permute-start.14 = (bf16[8,48,128]{2,1,0:T(8,128)(2,1)S(1)}, bf16[8,48,128]{2,1,0:T(8,128)(2,1)S(1)}, u32[]{:S(2)}, u32[]{:S(2)}) collective-permute-start(bf16[8,48,128]{2,1,0:T(8,128)(2,1)S(1)} %collective-permute-done.13.refs_12_), channel_id=1, source_target_pairs={{0,2},{1,3},{2,0},{3,1},{4,6},{5,7},{6,4},{7,5},{8,10},{9,11},{10,... | collective-permute-start | bytes 294920 | tf_op jit(solution)/shard_map/ppermute | solution.py:22
  37.2 1.3 %collective-permute-start.12 = (bf16[8,48,128]{2,1,0:T(8,128)(2,1)S(1)}, bf16[8,48,128]{2,1,0:T(8,128)(2,1)S(1)}, u32[]{:S(2)}, u32[]{:S(2)}) collective-permute-start(bf16[8,48,128]{2,1,0:T(8,128)(2,1)S(1)} %collective-permute-done.11.refs_10_), channel_id=1, source_target_pairs={{0,2},{1,3},{2,0},{3,1},{4,6},{5,7},{6,4},{7,5},{8,10},{9,11},{10,... | collective-permute-start | bytes 294920 | tf_op jit(solution)/shard_map/ppermute | solution.py:22
  38.5 0.0 collective-permute-done.10.refs_9_
  38.5 0.0 collective-permute-done.16.refs_15_
  38.5 2.7 %collective-permute-done.14.refs_13_ = bf16[8,48,128]{2,1,0:T(8,128)(2,1)S(1)} collective-permute-done((bf16[8,48,128]{2,1,0:T(8,128)(2,1)S(1)}, bf16[8,48,128]{2,1,0:T(8,128)(2,1)S(1)}, u32[]{:S(2)}, u32[]{:S(2)}) %collective-permute-start.14) | collective-permute-done | bytes 98336 | tf_op jit(solution)/shard_map/ppermute | solution.py:22
  41.2 1.1 %collective-permute-done.12.refs_11_ = bf16[8,48,128]{2,1,0:T(8,128)(2,1)S(1)} collective-permute-done((bf16[8,48,128]{2,1,0:T(8,128)(2,1)S(1)}, bf16[8,48,128]{2,1,0:T(8,128)(2,1)S(1)}, u32[]{:S(2)}, u32[]{:S(2)}) %collective-permute-start.12) | collective-permute-done | bytes 98336 | tf_op jit(solution)/shard_map/ppermute | solution.py:22
  42.2 0.5 shard_map.57
  42.7 0.1 collective-permute-start.17
  42.8 0.0 copy-start
  42.8 0.0 copy-start.1
  42.8 0.7 %shard_map.58.inner_ref = f32[8,32,1024]{2,1,0:T(8,128)S(1)} custom-call(f32[8,32,1024]{2,1,0:T(8,128)S(1)} %get-tuple-element.23.exact_ref, f32[8,16,1024]{2,1,0:T(8,128)S(1)} %get-tuple-element.24.edges_ref, f32[8,1024]{1,0:T(8,128)S(1)} %get-tuple-element.25.tables_ref), custom_call_target="tpu_custom_call" | custom-call | flops 5242880 | bytes 2097152 | tf_op jit(solution)/shard_map/pallas_call | solution.py:281
  43.5 1.2 %collective-permute-done.17.other_ref = bf16[8,32,1024]{2,1,0:T(8,128)(2,1)S(1)} collective-permute-done((bf16[8,32,1024]{2,1,0:T(8,128)(2,1)S(1)}, bf16[8,32,1024]{2,1,0:T(8,128)(2,1)S(1)}, u32[]{:S(2)}, u32[]{:S(2)}) %collective-permute-start.17) | collective-permute-done | bytes 524320 | tf_op jit(solution)/shard_map/ppermute | solution.py:22
  44.7 2.8 %shard_map.59 = (bf16[8,2,32,128]{3,2,1,0:T(8,128)(2,1)S(1)}, f32[32,1024]{1,0:T(8,128)S(1)}, f32[32,1024]{1,0:T(8,128)S(1)}) custom-call(f32[8,32,1024]{2,1,0:T(8,128)S(1)} %shard_map.58.inner_ref, bf16[8,32,1024]{2,1,0:T(8,128)(2,1)S(1)} %collective-permute-done.17.other_ref, f32[8,1024]{1,0:T(8,128)S(1)} %get-tuple-element.25.tables_ref, ...), custom_call_target="tpu_custom_call" | custom-call | flops 1073741824 | bytes 4718592 | tf_op jit(solution)/shard_map/pallas_call | solution.py:333
  47.5 10.9 %all_to_all.5.got_ref = bf16[8,2,32,128]{3,2,1,0:T(8,128)(2,1)S(1)} all-to-all(bf16[8,2,32,128]{3,2,1,0:T(8,128)(2,1)S(1)} %get-tuple-element.27), channel_id=1, replica_groups={{0,2,4,6,8,10,12,14},{1,3,5,7,9,11,13,15},{16,18,20,22,24,26,28,30},{17..., dimensions={0} | all-to-all | bytes 262144 | tf_op jit(solution)/shard_map/all_to_all | solution.py:393
  58.5 0.1 collective-permute-start.19
  58.6 1.6 %collective-permute-start.18 = (bf16[1,16,1024]{2,1,0:T(8,128)(2,1)S(1)}, bf16[1,16,1024]{2,1,0:T(8,128)(2,1)S(1)}, u32[]{:S(2)}, u32[]{:S(2)}) collective-permute-start(bf16[1,16,1024]{2,1,0:T(8,128)(2,1)S(1)} %get-tuple-element.31), channel_id=1, source_target_pairs={{0,16},{16,0},{1,17},{17,1},{2,18},{18,2},{3,19},{19,3},{4,20},{20... | collective-permute-start | bytes 98312 | tf_op jit(solution)/shard_map/ppermute | solution.py:22
  60.1 2.4 %collective-permute-done.18.edges_ref = bf16[1,16,1024]{2,1,0:T(8,128)(2,1)S(1)} collective-permute-done((bf16[1,16,1024]{2,1,0:T(8,128)(2,1)S(1)}, bf16[1,16,1024]{2,1,0:T(8,128)(2,1)S(1)}, u32[]{:S(2)}, u32[]{:S(2)}) %collective-permute-start.18) | collective-permute-done | bytes 32800 | tf_op jit(solution)/shard_map/ppermute | solution.py:22
  62.5 0.0 collective-permute-done.19.cells_ref
  62.6 0.8 %shard_map.61 = f32[32,1024]{1,0:T(8,128)} custom-call(f32[32,1024]{1,0:T(8,128)S(1)} %get-tuple-element.30.exact_ref, bf16[1,16,1024]{2,1,0:T(8,128)(2,1)S(1)} %collective-permute-done.18.edges_ref, bf16[2,32,1024]{2,1,0:T(8,128)(2,1)S(1)} %collective-permute-done.19.cells_ref, f32[8,1024]{1,0:T(8,128)S(1)} %get-tuple-element.25.tables_ref), custom_call_target="tpu_custom_call" | custom-call | flops 655360 | bytes 393216 | tf_op jit(solution)/shard_map/pallas_call | solution.py:410
  (6 shorter events, 0.1 us)
Async XLA Ops:
  0.0 19.4 %collective-permute-start.7 = (bf16[1024,512]{1,0:T(8,128)(2,1)}, bf16[1024,512]{1,0:T(8,128)(2,1)S(1)}, u32[]{:S(2)}, u32[]{:S(2)}) collective-permute-start(bf16[1024,512]{1,0:T(8,128)(2,1)} %refs_0_.1), channel_id=1, source_target_pairs={{0,1},{1,0},{2,3},{3,2},{4,5},{5,4},{6,7},{7,6},{8,9},{9,8},{10,11... | collective-permute-start | bytes 3145736 | tf_op jit(solution)/shard_map/ppermute | solution.py:22
  0.5 18.9 %collective-permute-start.8 = (bf16[1024,512]{1,0:T(8,128)(2,1)}, bf16[1024,512]{1,0:T(8,128)(2,1)S(1)}, u32[]{:S(2)}, u32[]{:S(2)}) collective-permute-start(bf16[1024,512]{1,0:T(8,128)(2,1)} %refs_1_.1), channel_id=1, source_target_pairs={{0,1},{1,0},{2,3},{3,2},{4,5},{5,4},{6,7},{7,6},{8,9},{9,8},{10,11... | collective-permute-start | bytes 3145736 | tf_op jit(solution)/shard_map/ppermute | solution.py:22
  1.5 7.7 %collective-permute-start.5 = (bf16[32,1024]{1,0:T(8,128)(2,1)S(1)}, bf16[32,1024]{1,0:T(8,128)(2,1)S(1)}, u32[]{:S(2)}, u32[]{:S(2)}) collective-permute-start(bf16[32,1024]{1,0:T(8,128)(2,1)S(1)} %get-tuple-element.20.refs_0_), channel_id=1, source_target_pairs={{0,12},{1,13},{2,14},{3,15},{4,8},{5,9},{6,10},{7,11},{8,4},{9,5},... | collective-permute-start | bytes 196616 | tf_op jit(solution)/shard_map/ppermute | solution.py:22
  6.6 5.8 %collective-permute-start.3 = (bf16[32,1024]{1,0:T(8,128)(2,1)S(1)}, bf16[32,1024]{1,0:T(8,128)(2,1)S(1)}, u32[]{:S(2)}, u32[]{:S(2)}) collective-permute-start(bf16[32,1024]{1,0:T(8,128)(2,1)S(1)} %get-tuple-element.20.refs_0_), channel_id=1, source_target_pairs={{0,8},{1,9},{2,10},{3,11},{4,12},{5,13},{6,14},{7,15},{8,0},{9,1},... | collective-permute-start | bytes 196616 | tf_op jit(solution)/shard_map/ppermute | solution.py:22
  6.6 7.3 %collective-permute-start.1 = (bf16[32,1024]{1,0:T(8,128)(2,1)S(1)}, bf16[32,1024]{1,0:T(8,128)(2,1)S(1)}, u32[]{:S(2)}, u32[]{:S(2)}) collective-permute-start(bf16[32,1024]{1,0:T(8,128)(2,1)S(1)} %get-tuple-element.20.refs_0_), channel_id=1, source_target_pairs={{0,4},{1,5},{2,6},{3,7},{4,0},{5,1},{6,2},{7,3},{8,12},{9,13},{10,... | collective-permute-start | bytes 196616 | tf_op jit(solution)/shard_map/ppermute | solution.py:22
  9.1 5.3 %collective-permute-start = (bf16[32,1024]{1,0:T(8,128)(2,1)S(1)}, bf16[32,1024]{1,0:T(8,128)(2,1)S(1)}, u32[]{:S(2)}, u32[]{:S(2)}) collective-permute-start(bf16[32,1024]{1,0:T(8,128)(2,1)S(1)} %get-tuple-element.20.refs_0_), channel_id=1, source_target_pairs={{0,2},{1,3},{2,0},{3,1},{4,6},{5,7},{6,4},{7,5},{8,10},{9,11},{10,... | collective-permute-start | bytes 196616 | tf_op jit(solution)/shard_map/ppermute | solution.py:22
  12.4 5.0 %collective-permute-start.6 = (bf16[32,1024]{1,0:T(8,128)(2,1)S(1)}, bf16[32,1024]{1,0:T(8,128)(2,1)S(1)}, u32[]{:S(2)}, u32[]{:S(2)}) collective-permute-start(bf16[32,1024]{1,0:T(8,128)(2,1)S(1)} %collective-permute-done.5.refs_6_), channel_id=1, source_target_pairs={{0,2},{1,3},{2,0},{3,1},{4,6},{5,7},{6,4},{7,5},{8,10},{9,11},{10,... | collective-permute-start | bytes 196616 | tf_op jit(solution)/shard_map/ppermute | solution.py:22
  13.9 4.8 %collective-permute-start.4 = (bf16[32,1024]{1,0:T(8,128)(2,1)S(1)}, bf16[32,1024]{1,0:T(8,128)(2,1)S(1)}, u32[]{:S(2)}, u32[]{:S(2)}) collective-permute-start(bf16[32,1024]{1,0:T(8,128)(2,1)S(1)} %collective-permute-done.3.refs_4_), channel_id=1, source_target_pairs={{0,2},{1,3},{2,0},{3,1},{4,6},{5,7},{6,4},{7,5},{8,10},{9,11},{10,... | collective-permute-start | bytes 196616 | tf_op jit(solution)/shard_map/ppermute | solution.py:22
  14.4 5.0 %collective-permute-start.2 = (bf16[32,1024]{1,0:T(8,128)(2,1)S(1)}, bf16[32,1024]{1,0:T(8,128)(2,1)S(1)}, u32[]{:S(2)}, u32[]{:S(2)}) collective-permute-start(bf16[32,1024]{1,0:T(8,128)(2,1)S(1)} %collective-permute-done.1.refs_2_), channel_id=1, source_target_pairs={{0,2},{1,3},{2,0},{3,1},{4,6},{5,7},{6,4},{7,5},{8,10},{9,11},{10,... | collective-permute-start | bytes 196616 | tf_op jit(solution)/shard_map/ppermute | solution.py:22
  22.6 4.0 %collective-permute-start.9 = (bf16[8,16,128]{2,1,0:T(8,128)(2,1)S(1)}, bf16[8,16,128]{2,1,0:T(8,128)(2,1)S(1)}, u32[]{:S(2)}, u32[]{:S(2)}) collective-permute-start(bf16[8,16,128]{2,1,0:T(8,128)(2,1)S(1)} %get-tuple-element.22), channel_id=1, source_target_pairs={{0,16},{16,0},{1,17},{17,1},{2,18},{18,2},{3,19},{19,3},{4,20},{20... | collective-permute-start | bytes 98312 | tf_op jit(solution)/shard_map/ppermute | solution.py:22
  26.6 6.8 %collective-permute-start.15 = (bf16[8,48,128]{2,1,0:T(8,128)(2,1)S(1)}, bf16[8,48,128]{2,1,0:T(8,128)(2,1)S(1)}, u32[]{:S(2)}, u32[]{:S(2)}) collective-permute-start(bf16[8,48,128]{2,1,0:T(8,128)(2,1)S(1)} %constant_dynamic-update-slice_fusion.refs_8_), channel_id=1, source_target_pairs={{0,12},{1,13},{2,14},{3,15},{4,8},{5,9},{6,10},{7,11},{8,4},{9,5},... | collective-permute-start | bytes 294920 | tf_op jit(solution)/shard_map/ppermute | solution.py:22
  29.7 6.7 %collective-permute-start.13 = (bf16[8,48,128]{2,1,0:T(8,128)(2,1)S(1)}, bf16[8,48,128]{2,1,0:T(8,128)(2,1)S(1)}, u32[]{:S(2)}, u32[]{:S(2)}) collective-permute-start(bf16[8,48,128]{2,1,0:T(8,128)(2,1)S(1)} %constant_dynamic-update-slice_fusion.refs_8_), channel_id=1, source_target_pairs={{0,8},{1,9},{2,10},{3,11},{4,12},{5,13},{6,14},{7,15},{8,0},{9,1},... | collective-permute-start | bytes 294920 | tf_op jit(solution)/shard_map/ppermute | solution.py:22
  29.7 7.5 %collective-permute-start.11 = (bf16[8,48,128]{2,1,0:T(8,128)(2,1)S(1)}, bf16[8,48,128]{2,1,0:T(8,128)(2,1)S(1)}, u32[]{:S(2)}, u32[]{:S(2)}) collective-permute-start(bf16[8,48,128]{2,1,0:T(8,128)(2,1)S(1)} %constant_dynamic-update-slice_fusion.refs_8_), channel_id=1, source_target_pairs={{0,4},{1,5},{2,6},{3,7},{4,0},{5,1},{6,2},{7,3},{8,12},{9,13},{10,... | collective-permute-start | bytes 294920 | tf_op jit(solution)/shard_map/ppermute | solution.py:22
  31.0 7.5 %collective-permute-start.10 = (bf16[8,48,128]{2,1,0:T(8,128)(2,1)S(1)}, bf16[8,48,128]{2,1,0:T(8,128)(2,1)S(1)}, u32[]{:S(2)}, u32[]{:S(2)}) collective-permute-start(bf16[8,48,128]{2,1,0:T(8,128)(2,1)S(1)} %constant_dynamic-update-slice_fusion.refs_8_), channel_id=1, source_target_pairs={{0,2},{1,3},{2,0},{3,1},{4,6},{5,7},{6,4},{7,5},{8,10},{9,11},{10,... | collective-permute-start | bytes 294920 | tf_op jit(solution)/shard_map/ppermute | solution.py:22
  33.4 5.1 %collective-permute-start.16 = (bf16[8,48,128]{2,1,0:T(8,128)(2,1)S(1)}, bf16[8,48,128]{2,1,0:T(8,128)(2,1)S(1)}, u32[]{:S(2)}, u32[]{:S(2)}) collective-permute-start(bf16[8,48,128]{2,1,0:T(8,128)(2,1)S(1)} %collective-permute-done.15.refs_14_), channel_id=1, source_target_pairs={{0,2},{1,3},{2,0},{3,1},{4,6},{5,7},{6,4},{7,5},{8,10},{9,11},{10,... | collective-permute-start | bytes 294920 | tf_op jit(solution)/shard_map/ppermute | solution.py:22
  36.5 4.7 %collective-permute-start.14 = (bf16[8,48,128]{2,1,0:T(8,128)(2,1)S(1)}, bf16[8,48,128]{2,1,0:T(8,128)(2,1)S(1)}, u32[]{:S(2)}, u32[]{:S(2)}) collective-permute-start(bf16[8,48,128]{2,1,0:T(8,128)(2,1)S(1)} %collective-permute-done.13.refs_12_), channel_id=1, source_target_pairs={{0,2},{1,3},{2,0},{3,1},{4,6},{5,7},{6,4},{7,5},{8,10},{9,11},{10,... | collective-permute-start | bytes 294920 | tf_op jit(solution)/shard_map/ppermute | solution.py:22
  37.2 5.1 %collective-permute-start.12 = (bf16[8,48,128]{2,1,0:T(8,128)(2,1)S(1)}, bf16[8,48,128]{2,1,0:T(8,128)(2,1)S(1)}, u32[]{:S(2)}, u32[]{:S(2)}) collective-permute-start(bf16[8,48,128]{2,1,0:T(8,128)(2,1)S(1)} %collective-permute-done.11.refs_10_), channel_id=1, source_target_pairs={{0,2},{1,3},{2,0},{3,1},{4,6},{5,7},{6,4},{7,5},{8,10},{9,11},{10,... | collective-permute-start | bytes 294920 | tf_op jit(solution)/shard_map/ppermute | solution.py:22
  42.7 2.0 %collective-permute-start.17 = (bf16[8,32,1024]{2,1,0:T(8,128)(2,1)S(1)}, bf16[8,32,1024]{2,1,0:T(8,128)(2,1)S(1)}, u32[]{:S(2)}, u32[]{:S(2)}) collective-permute-start(bf16[8,32,1024]{2,1,0:T(8,128)(2,1)S(1)} %get-tuple-element.26), channel_id=1, source_target_pairs={{0,1},{1,0},{2,3},{3,2},{4,5},{5,4},{6,7},{7,6},{8,9},{9,8},{10,11... | collective-permute-start | bytes 1572872 | tf_op jit(solution)/shard_map/ppermute | solution.py:22
  42.8 1.9 %copy-start = (bf16[1024,512]{1,0:T(8,128)(2,1)S(1)}, bf16[1024,512]{1,0:T(8,128)(2,1)}, u32[]{:S(2)}) copy-start(bf16[1024,512]{1,0:T(8,128)(2,1)} %refs_0_.1) | copy-start | bytes 3145732
  42.8 1.9 %copy-start.1 = (bf16[1024,512]{1,0:T(8,128)(2,1)S(1)}, bf16[1024,512]{1,0:T(8,128)(2,1)}, u32[]{:S(2)}) copy-start(bf16[1024,512]{1,0:T(8,128)(2,1)} %refs_1_.1) | copy-start | bytes 3145732
  58.5 4.1 %collective-permute-start.19 = (bf16[2,32,1024]{2,1,0:T(8,128)(2,1)S(1)}, bf16[2,32,1024]{2,1,0:T(8,128)(2,1)S(1)}, u32[]{:S(2)}, u32[]{:S(2)}) collective-permute-start(bf16[2,32,1024]{2,1,0:T(8,128)(2,1)S(1)} %get-tuple-element.32), channel_id=1, source_target_pairs={{0,1},{1,0},{2,3},{3,2},{4,5},{5,4},{6,7},{7,6},{8,9},{9,8},{10,11... | collective-permute-start | bytes 393224 | tf_op jit(solution)/shard_map/ppermute | solution.py:22
  58.6 4.0 %collective-permute-start.18 = (bf16[1,16,1024]{2,1,0:T(8,128)(2,1)S(1)}, bf16[1,16,1024]{2,1,0:T(8,128)(2,1)S(1)}, u32[]{:S(2)}, u32[]{:S(2)}) collective-permute-start(bf16[1,16,1024]{2,1,0:T(8,128)(2,1)S(1)} %get-tuple-element.31), channel_id=1, source_target_pairs={{0,16},{16,0},{1,17},{17,1},{2,18},{18,2},{3,19},{19,3},{4,20},{20... | collective-permute-start | bytes 98312 | tf_op jit(solution)/shard_map/ppermute | solution.py:22

commit v7 on v6

--- a/solution.py
+++ b/solution.py
@@ -171,17 +171,35 @@
     )(*blocks, *[off_chip(each) if fetch else each for each in factors[:2]], *factors[2:])
 
 
+def keep_kernel(a_hbm, b_hbm, a_ref, b_ref, sems):
+    for copy in fetches((a_hbm, b_hbm), (a_ref, b_ref), sems):
+        copy.wait()
+
+
+def keep(factors):
+    hbm = pl.BlockSpec(memory_space=pltpu.MemorySpace.HBM)
+    return pl.pallas_call(
+        keep_kernel,
+        out_shape=[jax.ShapeDtypeStruct(each.shape, each.dtype) for each in factors],
+        in_specs=[hbm] * 2,
+        out_specs=[pl.BlockSpec(memory_space=pltpu.VMEM)] * 2,
+        scratch_shapes=[pltpu.SemaphoreType.DMA((2, 4))],
+        compiler_params=pltpu.CompilerParams(vmem_limit_bytes=4 << 20),
+        cost_estimate=pl.CostEstimate(
+            flops=0, bytes_accessed=8 * factors[0].size, transcendentals=0
+        ),
+    )(*[off_chip(each) for each in factors])
+
+
 def first_kernel(chips, layers, *refs):
     blocks, factors = refs[:chips], refs[chips : chips + 4]
-    terms_ref, edges_ref, a_kept, b_kept, sems = refs[chips + 4 :]
-    kept = (a_kept, b_kept)
-    copies = fetches(factors[:2], kept, sems)
+    terms_ref, edges_ref = refs[chips + 4 :]
     me = lax.axis_index("mom")
     core, chip = me & 1, me >> 1
     rows = blocks[0].shape[0]
     depth = rows // layers
     states = jnp.concatenate([block[...] for block in blocks], axis=0)
-    total = project(states, core, factors[2:], kept, copies)
+    total = project(states, core, factors[2:], factors[:2], [])
     mine = total.shape[1]
     columns = pl.ds(pl.multiple_of(chip * mine, 128), mine)
     for at in range(chips):
@@ -198,25 +216,19 @@
     chips, (rows, size) = len(blocks), blocks[0].shape
     columns = factors[0].shape[1]
     mine = 2 * columns // RANK
-    whole = pl.BlockSpec(memory_space=pltpu.VMEM)
-    hbm = pl.BlockSpec(memory_space=pltpu.MemorySpace.HBM)
-    factor = pltpu.VMEM((size, columns), jnp.bfloat16)
     return pl.pallas_call(
         functools.partial(first_kernel, chips, layers),
         out_shape=[
             jax.ShapeDtypeStruct((chips, rows, mine), jnp.bfloat16),
             jax.ShapeDtypeStruct((chips, 2 * rows // layers, mine), jnp.bfloat16),
         ],
-        in_specs=[whole] * chips + [hbm] * 2 + [whole] * 2,
-        out_specs=[whole] * 2,
-        scratch_shapes=[factor, factor, pltpu.SemaphoreType.DMA((2, 4))],
         compiler_params=pltpu.CompilerParams(vmem_limit_bytes=16 << 20),
         cost_estimate=pl.CostEstimate(
             flops=8 * chips * rows * size * columns,
             bytes_accessed=2 * (chips * rows * size + 4 * size * columns),
             transcendentals=0,
         ),
-    )(*blocks, *[off_chip(each) for each in factors[:2]], *factors[2:])
+    )(*blocks, *factors)
 
 
 def collided_kernel(chips, rows, state_ref, *refs):
@@ -447,7 +459,8 @@
 def per_device(distribution, a_factor, b_factor, velocity, drift):
     layers, owned, depth, size = distribution.shape
     assert owned == 1
-    factors = (a_factor, b_factor, swap(a_factor, "mom", 1), swap(b_factor, "mom", 1))
+    partner = (swap(a_factor, "mom", 1), swap(b_factor, "mom", 1))
+    factors = (a_factor, b_factor, *partner)
     state, rounded, tables = prepare(distribution.reshape(layers * depth, size), velocity, drift)
     if 2 * (a_factor.shape[1] // RANK) % 128:
         for substep in range(ITERS):
@@ -455,6 +468,7 @@
             state = settle(state, sent, beside.astype(jnp.float32), tables, layers)
             rounded = state.astype(jnp.bfloat16)
         return state.reshape(distribution.shape)
+    factors = (*keep((a_factor, b_factor)), *partner)
     for _ in range(0, ITERS, 2):
         blocks = gathered(rounded, "mom")
         terms, edges = first_collision(blocks, factors, layers)

time: 63.6 us -> 62.2 us (0.978)
  waiting for transfers between devices: 19.8 us -> 18.3 us
    pallas_call x0 -> x1, Pallas kernels: none -> 1.57 us  [keep(): pl.pallas_call(keep_kernel, out_shape=[jax.ShapeDtypeStruct(each.shape, e...]
    ppermute x20, waiting for transfers between devices: 19.8 us -> 18.3 us  [swap(): return lax.ppermute(block, axis, [(i, i ^ bits) for i in range(count)])]
    pallas_call x1, Pallas kernels: 3.23 us -> 1.85 us  [first_collision(): pl.pallas_call(functools.partial(first_kernel, chips, layers), out_shape=...]
  transfers between devices with their start and end apart: 20 -> 20, of which waited for: 12 -> 11; matrix products, arithmetic and copies ran while one was open for 0% -> 0% of each run, Pallas kernels for 3% -> 5%
where the time goes in v7:
time: 62.2 us; the launch traced here: 62 us
  starting transfers between devices  23.6 us (38%)
  waiting for transfers between devices  18.3 us (29%)
  blocking collectives  11 us (18%)
  Pallas kernels  9.14 us (15%)
    ppermute x20, starting transfers between devices, swap(): return lax.ppermute(block, axis, [(i, i ^ bits) for i in range(count)])  23.6 us
    ppermute x20, waiting for transfers between devices, swap(): return lax.ppermute(block, axis, [(i, i ^ bits) for i in range(count)])  18.3 us
    all_to_all x1, blocking collectives, settled(): lax.all_to_all(sent, 'mom', split_axis=0, concat_axis=0, tiled=True, axis...  11 us
    pallas_call x1, Pallas kernels, second_collision(): pl.pallas_call(functools.partial(second_kernel, chips), out_shape=[jax.Sh...  2.77 us
    pallas_call x1, Pallas kernels, first_collision(): pl.pallas_call(functools.partial(first_kernel, chips, layers), out_shape=...  1.85 us
    pallas_call x1, Pallas kernels, keep(): pl.pallas_call(keep_kernel, out_shape=[jax.ShapeDtypeStruct(each.shape, e...  1.57 us
  transfers between devices with their start and end apart: 20, of which 11 were waited for; matrix products, arithmetic and copies ran while one was open for 0% of the time, Pallas kernels for 5%

profile of v7, /device:TPU:0, one launch (start us, length us, event | category | flops | bytes accessed | tf_op | source)
XLA Modules:
  0.0 62.0 jit_solution(18250710397662544179)
XLA Ops:
  0.0 0.5 collective-permute-start.7
  0.5 0.0 collective-permute-start.8
  0.5 0.9 %shard_map.55 = (f32[32,1024]{1,0:T(8,128)S(1)}, bf16[32,1024]{1,0:T(8,128)(2,1)S(1)}, f32[8,1024]{1,0:T(8,128)S(1)}) custom-call(f32[32,1024]{1,0:T(8,128)} %bitcast.5, f32[3,1024]{1,0:T(4,128)} %velocity_hbm.1, f32[1,1024]{1,0:T(1,128)} %bitcast.6), custom_call_target="tpu_custom_call" | custom-call | flops 32768 | bytes 327680 | tf_op jit(solution)/shard_map/pallas_call | solution.py:64
  1.5 5.1 %collective-permute-start.5 = (bf16[32,1024]{1,0:T(8,128)(2,1)S(1)}, bf16[32,1024]{1,0:T(8,128)(2,1)S(1)}, u32[]{:S(2)}, u32[]{:S(2)}) collective-permute-start(bf16[32,1024]{1,0:T(8,128)(2,1)S(1)} %get-tuple-element.22.refs_0_), channel_id=1, source_target_pairs={{0,12},{1,13},{2,14},{3,15},{4,8},{5,9},{6,10},{7,11},{8,4},{9,5},... | collective-permute-start | bytes 196616 | tf_op jit(solution)/shard_map/ppermute | solution.py:22
  6.6 0.0 collective-permute-start.3
  6.6 0.6 %collective-permute-start.1 = (bf16[32,1024]{1,0:T(8,128)(2,1)S(1)}, bf16[32,1024]{1,0:T(8,128)(2,1)S(1)}, u32[]{:S(2)}, u32[]{:S(2)}) collective-permute-start(bf16[32,1024]{1,0:T(8,128)(2,1)S(1)} %get-tuple-element.22.refs_0_), channel_id=1, source_target_pairs={{0,4},{1,5},{2,6},{3,7},{4,0},{5,1},{6,2},{7,3},{8,12},{9,13},{10,... | collective-permute-start | bytes 196616 | tf_op jit(solution)/shard_map/ppermute | solution.py:22
  7.2 1.9 %collective-permute-done.5.refs_6_ = bf16[32,1024]{1,0:T(8,128)(2,1)S(1)} collective-permute-done((bf16[32,1024]{1,0:T(8,128)(2,1)S(1)}, bf16[32,1024]{1,0:T(8,128)(2,1)S(1)}, u32[]{:S(2)}, u32[]{:S(2)}) %collective-permute-start.5) | collective-permute-done | bytes 65568 | tf_op jit(solution)/shard_map/ppermute | solution.py:22
  9.1 1.7 %collective-permute-start = (bf16[32,1024]{1,0:T(8,128)(2,1)S(1)}, bf16[32,1024]{1,0:T(8,128)(2,1)S(1)}, u32[]{:S(2)}, u32[]{:S(2)}) collective-permute-start(bf16[32,1024]{1,0:T(8,128)(2,1)S(1)} %get-tuple-element.22.refs_0_), channel_id=1, source_target_pairs={{0,2},{1,3},{2,0},{3,1},{4,6},{5,7},{6,4},{7,5},{8,10},{9,11},{10,... | collective-permute-start | bytes 196616 | tf_op jit(solution)/shard_map/ppermute | solution.py:22
  10.9 1.5 %collective-permute-done.3.refs_4_ = bf16[32,1024]{1,0:T(8,128)(2,1)S(1)} collective-permute-done((bf16[32,1024]{1,0:T(8,128)(2,1)S(1)}, bf16[32,1024]{1,0:T(8,128)(2,1)S(1)}, u32[]{:S(2)}, u32[]{:S(2)}) %collective-permute-start.3) | collective-permute-done | bytes 65568 | tf_op jit(solution)/shard_map/ppermute | solution.py:22
  12.4 1.5 %collective-permute-start.6 = (bf16[32,1024]{1,0:T(8,128)(2,1)S(1)}, bf16[32,1024]{1,0:T(8,128)(2,1)S(1)}, u32[]{:S(2)}, u32[]{:S(2)}) collective-permute-start(bf16[32,1024]{1,0:T(8,128)(2,1)S(1)} %collective-permute-done.5.refs_6_), channel_id=1, source_target_pairs={{0,2},{1,3},{2,0},{3,1},{4,6},{5,7},{6,4},{7,5},{8,10},{9,11},{10,... | collective-permute-start | bytes 196616 | tf_op jit(solution)/shard_map/ppermute | solution.py:22
  13.9 0.0 collective-permute-done.1.refs_2_
  13.9 0.5 collective-permute-start.4
  14.4 0.0 collective-permute-done.refs_1_
  14.4 1.5 %collective-permute-start.2 = (bf16[32,1024]{1,0:T(8,128)(2,1)S(1)}, bf16[32,1024]{1,0:T(8,128)(2,1)S(1)}, u32[]{:S(2)}, u32[]{:S(2)}) collective-permute-start(bf16[32,1024]{1,0:T(8,128)(2,1)S(1)} %collective-permute-done.1.refs_2_), channel_id=1, source_target_pairs={{0,2},{1,3},{2,0},{3,1},{4,6},{5,7},{6,4},{7,5},{8,10},{9,11},{10,... | collective-permute-start | bytes 196616 | tf_op jit(solution)/shard_map/ppermute | solution.py:22
  15.9 1.6 %shard_map.56 = (bf16[1024,512]{1,0:T(8,128)(2,1)S(1)}, bf16[1024,512]{1,0:T(8,128)(2,1)S(1)}) custom-call(bf16[1024,512]{1,0:T(8,128)(2,1)} %a_hbm.1, bf16[1024,512]{1,0:T(8,128)(2,1)} %b_hbm.1), custom_call_target="tpu_custom_call" | custom-call | bytes 4194304 | tf_op jit(solution)/shard_map/pallas_call | solution.py:181
  17.5 0.0 collective-permute-done.6.refs_7_
  17.5 1.2 %collective-permute-done.4.refs_5_ = bf16[32,1024]{1,0:T(8,128)(2,1)S(1)} collective-permute-done((bf16[32,1024]{1,0:T(8,128)(2,1)S(1)}, bf16[32,1024]{1,0:T(8,128)(2,1)S(1)}, u32[]{:S(2)}, u32[]{:S(2)}) %collective-permute-start.4) | collective-permute-done | bytes 65568 | tf_op jit(solution)/shard_map/ppermute | solution.py:22
  18.7 0.7 %collective-permute-done.2.refs_3_ = bf16[32,1024]{1,0:T(8,128)(2,1)S(1)} collective-permute-done((bf16[32,1024]{1,0:T(8,128)(2,1)S(1)}, bf16[32,1024]{1,0:T(8,128)(2,1)S(1)}, u32[]{:S(2)}, u32[]{:S(2)}) %collective-permute-start.2) | collective-permute-done | bytes 65568 | tf_op jit(solution)/shard_map/ppermute | solution.py:22
  19.4 0.0 collective-permute-done.7.refs_10_.refs_2_
  19.4 0.0 collective-permute-done.8.refs_11_.refs_3_
  19.4 1.9 %shard_map.57 = (bf16[8,32,128]{2,1,0:T(8,128)(2,1)S(1)}, bf16[8,16,128]{2,1,0:T(8,128)(2,1)S(1)}) custom-call(bf16[32,1024]{1,0:T(8,128)(2,1)S(1)} %get-tuple-element.22.refs_0_, bf16[32,1024]{1,0:T(8,128)(2,1)S(1)} %collective-permute-done.refs_1_, bf16[32,1024]{1,0:T(8,128)(2,1)S(1)} %collective-permute-done.1.refs_2_, ...), custom_call_target="tpu_custom_call" | custom-call | flops 1073741824 | bytes 4718592 | tf_op jit(solution)/shard_map/pallas_call | solution.py:219
  21.3 1.6 %collective-permute-start.9 = (bf16[8,16,128]{2,1,0:T(8,128)(2,1)S(1)}, bf16[8,16,128]{2,1,0:T(8,128)(2,1)S(1)}, u32[]{:S(2)}, u32[]{:S(2)}) collective-permute-start(bf16[8,16,128]{2,1,0:T(8,128)(2,1)S(1)} %get-tuple-element.26), channel_id=1, source_target_pairs={{0,16},{16,0},{1,17},{17,1},{2,18},{18,2},{3,19},{19,3},{4,20},{20... | collective-permute-start | bytes 98312 | tf_op jit(solution)/shard_map/ppermute | solution.py:22
  22.8 2.4 %collective-permute-done.9 = bf16[8,16,128]{2,1,0:T(8,128)(2,1)S(1)} collective-permute-done((bf16[8,16,128]{2,1,0:T(8,128)(2,1)S(1)}, bf16[8,16,128]{2,1,0:T(8,128)(2,1)S(1)}, u32[]{:S(2)}, u32[]{:S(2)}) %collective-permute-start.9) | collective-permute-done | bytes 32800 | tf_op jit(solution)/shard_map/ppermute | solution.py:22
  25.2 3.1 %collective-permute-start.15 = (bf16[8,48,128]{2,1,0:T(8,128)(2,1)S(1)}, bf16[8,48,128]{2,1,0:T(8,128)(2,1)S(1)}, u32[]{:S(2)}, u32[]{:S(2)}) collective-permute-start(bf16[8,48,128]{2,1,0:T(8,128)(2,1)S(1)} %constant_dynamic-update-slice_fusion.refs_8_), channel_id=1, source_target_pairs={{0,12},{1,13},{2,14},{3,15},{4,8},{5,9},{6,10},{7,11},{8,4},{9,5},... | collective-permute-start | bytes 294920 | tf_op jit(solution)/shard_map/ppermute | solution.py:22
  28.3 0.0 collective-permute-start.13
  28.4 1.3 %collective-permute-start.11 = (bf16[8,48,128]{2,1,0:T(8,128)(2,1)S(1)}, bf16[8,48,128]{2,1,0:T(8,128)(2,1)S(1)}, u32[]{:S(2)}, u32[]{:S(2)}) collective-permute-start(bf16[8,48,128]{2,1,0:T(8,128)(2,1)S(1)} %constant_dynamic-update-slice_fusion.refs_8_), channel_id=1, source_target_pairs={{0,4},{1,5},{2,6},{3,7},{4,0},{5,1},{6,2},{7,3},{8,12},{9,13},{10,... | collective-permute-start | bytes 294920 | tf_op jit(solution)/shard_map/ppermute | solution.py:22
  29.6 1.0 %collective-permute-start.10 = (bf16[8,48,128]{2,1,0:T(8,128)(2,1)S(1)}, bf16[8,48,128]{2,1,0:T(8,128)(2,1)S(1)}, u32[]{:S(2)}, u32[]{:S(2)}) collective-permute-start(bf16[8,48,128]{2,1,0:T(8,128)(2,1)S(1)} %constant_dynamic-update-slice_fusion.refs_8_), channel_id=1, source_target_pairs={{0,2},{1,3},{2,0},{3,1},{4,6},{5,7},{6,4},{7,5},{8,10},{9,11},{10,... | collective-permute-start | bytes 294920 | tf_op jit(solution)/shard_map/ppermute | solution.py:22
  30.7 1.4 %collective-permute-done.15.refs_14_ = bf16[8,48,128]{2,1,0:T(8,128)(2,1)S(1)} collective-permute-done((bf16[8,48,128]{2,1,0:T(8,128)(2,1)S(1)}, bf16[8,48,128]{2,1,0:T(8,128)(2,1)S(1)}, u32[]{:S(2)}, u32[]{:S(2)}) %collective-permute-start.15) | collective-permute-done | bytes 98336 | tf_op jit(solution)/shard_map/ppermute | solution.py:22
  32.0 1.3 %collective-permute-start.16 = (bf16[8,48,128]{2,1,0:T(8,128)(2,1)S(1)}, bf16[8,48,128]{2,1,0:T(8,128)(2,1)S(1)}, u32[]{:S(2)}, u32[]{:S(2)}) collective-permute-start(bf16[8,48,128]{2,1,0:T(8,128)(2,1)S(1)} %collective-permute-done.15.refs_14_), channel_id=1, source_target_pairs={{0,2},{1,3},{2,0},{3,1},{4,6},{5,7},{6,4},{7,5},{8,10},{9,11},{10,... | collective-permute-start | bytes 294920 | tf_op jit(solution)/shard_map/ppermute | solution.py:22
  33.4 1.7 %collective-permute-done.13.refs_12_ = bf16[8,48,128]{2,1,0:T(8,128)(2,1)S(1)} collective-permute-done((bf16[8,48,128]{2,1,0:T(8,128)(2,1)S(1)}, bf16[8,48,128]{2,1,0:T(8,128)(2,1)S(1)}, u32[]{:S(2)}, u32[]{:S(2)}) %collective-permute-start.13) | collective-permute-done | bytes 98336 | tf_op jit(solution)/shard_map/ppermute | solution.py:22
  35.1 0.7 %collective-permute-start.14 = (bf16[8,48,128]{2,1,0:T(8,128)(2,1)S(1)}, bf16[8,48,128]{2,1,0:T(8,128)(2,1)S(1)}, u32[]{:S(2)}, u32[]{:S(2)}) collective-permute-start(bf16[8,48,128]{2,1,0:T(8,128)(2,1)S(1)} %collective-permute-done.13.refs_12_), channel_id=1, source_target_pairs={{0,2},{1,3},{2,0},{3,1},{4,6},{5,7},{6,4},{7,5},{8,10},{9,11},{10,... | collective-permute-start | bytes 294920 | tf_op jit(solution)/shard_map/ppermute | solution.py:22
  35.8 0.0 collective-permute-done.11.refs_10_
  35.8 1.3 %collective-permute-start.12 = (bf16[8,48,128]{2,1,0:T(8,128)(2,1)S(1)}, bf16[8,48,128]{2,1,0:T(8,128)(2,1)S(1)}, u32[]{:S(2)}, u32[]{:S(2)}) collective-permute-start(bf16[8,48,128]{2,1,0:T(8,128)(2,1)S(1)} %collective-permute-done.11.refs_10_), channel_id=1, source_target_pairs={{0,2},{1,3},{2,0},{3,1},{4,6},{5,7},{6,4},{7,5},{8,10},{9,11},{10,... | collective-permute-start | bytes 294920 | tf_op jit(solution)/shard_map/ppermute | solution.py:22
  37.1 0.0 collective-permute-done.10.refs_9_
  37.1 0.0 collective-permute-done.16.refs_15_
  37.1 2.7 %collective-permute-done.14.refs_13_ = bf16[8,48,128]{2,1,0:T(8,128)(2,1)S(1)} collective-permute-done((bf16[8,48,128]{2,1,0:T(8,128)(2,1)S(1)}, bf16[8,48,128]{2,1,0:T(8,128)(2,1)S(1)}, u32[]{:S(2)}, u32[]{:S(2)}) %collective-permute-start.14) | collective-permute-done | bytes 98336 | tf_op jit(solution)/shard_map/ppermute | solution.py:22
  39.8 1.1 %collective-permute-done.12.refs_11_ = bf16[8,48,128]{2,1,0:T(8,128)(2,1)S(1)} collective-permute-done((bf16[8,48,128]{2,1,0:T(8,128)(2,1)S(1)}, bf16[8,48,128]{2,1,0:T(8,128)(2,1)S(1)}, u32[]{:S(2)}, u32[]{:S(2)}) %collective-permute-start.12) | collective-permute-done | bytes 98336 | tf_op jit(solution)/shard_map/ppermute | solution.py:22
  40.9 0.5 shard_map.58
  41.4 0.1 collective-permute-start.17
  41.4 0.7 %shard_map.59.inner_ref = f32[8,32,1024]{2,1,0:T(8,128)S(1)} custom-call(f32[8,32,1024]{2,1,0:T(8,128)S(1)} %get-tuple-element.27.exact_ref, f32[8,16,1024]{2,1,0:T(8,128)S(1)} %get-tuple-element.28.edges_ref, f32[8,1024]{1,0:T(8,128)S(1)} %get-tuple-element.29.tables_ref), custom_call_target="tpu_custom_call" | custom-call | flops 5242880 | bytes 2097152 | tf_op jit(solution)/shard_map/pallas_call | solution.py:293
  42.1 1.2 %collective-permute-done.17.other_ref = bf16[8,32,1024]{2,1,0:T(8,128)(2,1)S(1)} collective-permute-done((bf16[8,32,1024]{2,1,0:T(8,128)(2,1)S(1)}, bf16[8,32,1024]{2,1,0:T(8,128)(2,1)S(1)}, u32[]{:S(2)}, u32[]{:S(2)}) %collective-permute-start.17) | collective-permute-done | bytes 524320 | tf_op jit(solution)/shard_map/ppermute | solution.py:22
  43.3 2.8 %shard_map.60 = (bf16[8,2,32,128]{3,2,1,0:T(8,128)(2,1)S(1)}, f32[32,1024]{1,0:T(8,128)S(1)}, f32[32,1024]{1,0:T(8,128)S(1)}) custom-call(f32[8,32,1024]{2,1,0:T(8,128)S(1)} %shard_map.59.inner_ref, bf16[8,32,1024]{2,1,0:T(8,128)(2,1)S(1)} %collective-permute-done.17.other_ref, f32[8,1024]{1,0:T(8,128)S(1)} %get-tuple-element.29.tables_ref, ...), custom_call_target="tpu_custom_call" | custom-call | flops 1073741824 | bytes 4718592 | tf_op jit(solution)/shard_map/pallas_call | solution.py:345
  46.1 11.0 %all_to_all.5.got_ref = bf16[8,2,32,128]{3,2,1,0:T(8,128)(2,1)S(1)} all-to-all(bf16[8,2,32,128]{3,2,1,0:T(8,128)(2,1)S(1)} %get-tuple-element.31), channel_id=1, replica_groups={{0,2,4,6,8,10,12,14},{1,3,5,7,9,11,13,15},{16,18,20,22,24,26,28,30},{17..., dimensions={0} | all-to-all | bytes 262144 | tf_op jit(solution)/shard_map/all_to_all | solution.py:405
  57.1 0.1 collective-permute-start.19
  57.2 1.6 %collective-permute-start.18 = (bf16[1,16,1024]{2,1,0:T(8,128)(2,1)S(1)}, bf16[1,16,1024]{2,1,0:T(8,128)(2,1)S(1)}, u32[]{:S(2)}, u32[]{:S(2)}) collective-permute-start(bf16[1,16,1024]{2,1,0:T(8,128)(2,1)S(1)} %get-tuple-element.35), channel_id=1, source_target_pairs={{0,16},{16,0},{1,17},{17,1},{2,18},{18,2},{3,19},{19,3},{4,20},{20... | collective-permute-start | bytes 98312 | tf_op jit(solution)/shard_map/ppermute | solution.py:22
  58.7 2.4 %collective-permute-done.18.edges_ref = bf16[1,16,1024]{2,1,0:T(8,128)(2,1)S(1)} collective-permute-done((bf16[1,16,1024]{2,1,0:T(8,128)(2,1)S(1)}, bf16[1,16,1024]{2,1,0:T(8,128)(2,1)S(1)}, u32[]{:S(2)}, u32[]{:S(2)}) %collective-permute-start.18) | collective-permute-done | bytes 32800 | tf_op jit(solution)/shard_map/ppermute | solution.py:22
  61.2 0.0 collective-permute-done.19.cells_ref
  61.2 0.8 %shard_map.62 = f32[32,1024]{1,0:T(8,128)} custom-call(f32[32,1024]{1,0:T(8,128)S(1)} %get-tuple-element.34.exact_ref, bf16[1,16,1024]{2,1,0:T(8,128)(2,1)S(1)} %collective-permute-done.18.edges_ref, bf16[2,32,1024]{2,1,0:T(8,128)(2,1)S(1)} %collective-permute-done.19.cells_ref, f32[8,1024]{1,0:T(8,128)S(1)} %get-tuple-element.29.tables_ref), custom_call_target="tpu_custom_call" | custom-call | flops 655360 | bytes 393216 | tf_op jit(solution)/shard_map/pallas_call | solution.py:422
  (3 shorter events, 0.1 us)
Async XLA Ops:
  0.0 19.4 %collective-permute-start.7 = (bf16[1024,512]{1,0:T(8,128)(2,1)}, bf16[1024,512]{1,0:T(8,128)(2,1)S(1)}, u32[]{:S(2)}, u32[]{:S(2)}) collective-permute-start(bf16[1024,512]{1,0:T(8,128)(2,1)} %a_hbm.1), channel_id=1, source_target_pairs={{0,1},{1,0},{2,3},{3,2},{4,5},{5,4},{6,7},{7,6},{8,9},{9,8},{10,11... | collective-permute-start | bytes 3145736 | tf_op jit(solution)/shard_map/ppermute | solution.py:22
  0.5 18.9 %collective-permute-start.8 = (bf16[1024,512]{1,0:T(8,128)(2,1)}, bf16[1024,512]{1,0:T(8,128)(2,1)S(1)}, u32[]{:S(2)}, u32[]{:S(2)}) collective-permute-start(bf16[1024,512]{1,0:T(8,128)(2,1)} %b_hbm.1), channel_id=1, source_target_pairs={{0,1},{1,0},{2,3},{3,2},{4,5},{5,4},{6,7},{7,6},{8,9},{9,8},{10,11... | collective-permute-start | bytes 3145736 | tf_op jit(solution)/shard_map/ppermute | solution.py:22
  1.5 7.7 %collective-permute-start.5 = (bf16[32,1024]{1,0:T(8,128)(2,1)S(1)}, bf16[32,1024]{1,0:T(8,128)(2,1)S(1)}, u32[]{:S(2)}, u32[]{:S(2)}) collective-permute-start(bf16[32,1024]{1,0:T(8,128)(2,1)S(1)} %get-tuple-element.22.refs_0_), channel_id=1, source_target_pairs={{0,12},{1,13},{2,14},{3,15},{4,8},{5,9},{6,10},{7,11},{8,4},{9,5},... | collective-permute-start | bytes 196616 | tf_op jit(solution)/shard_map/ppermute | solution.py:22
  6.6 5.8 %collective-permute-start.3 = (bf16[32,1024]{1,0:T(8,128)(2,1)S(1)}, bf16[32,1024]{1,0:T(8,128)(2,1)S(1)}, u32[]{:S(2)}, u32[]{:S(2)}) collective-permute-start(bf16[32,1024]{1,0:T(8,128)(2,1)S(1)} %get-tuple-element.22.refs_0_), channel_id=1, source_target_pairs={{0,8},{1,9},{2,10},{3,11},{4,12},{5,13},{6,14},{7,15},{8,0},{9,1},... | collective-permute-start | bytes 196616 | tf_op jit(solution)/shard_map/ppermute | solution.py:22
  6.6 7.3 %collective-permute-start.1 = (bf16[32,1024]{1,0:T(8,128)(2,1)S(1)}, bf16[32,1024]{1,0:T(8,128)(2,1)S(1)}, u32[]{:S(2)}, u32[]{:S(2)}) collective-permute-start(bf16[32,1024]{1,0:T(8,128)(2,1)S(1)} %get-tuple-element.22.refs_0_), channel_id=1, source_target_pairs={{0,4},{1,5},{2,6},{3,7},{4,0},{5,1},{6,2},{7,3},{8,12},{9,13},{10,... | collective-permute-start | bytes 196616 | tf_op jit(solution)/shard_map/ppermute | solution.py:22
  9.1 5.3 %collective-permute-start = (bf16[32,1024]{1,0:T(8,128)(2,1)S(1)}, bf16[32,1024]{1,0:T(8,128)(2,1)S(1)}, u32[]{:S(2)}, u32[]{:S(2)}) collective-permute-start(bf16[32,1024]{1,0:T(8,128)(2,1)S(1)} %get-tuple-element.22.refs_0_), channel_id=1, source_target_pairs={{0,2},{1,3},{2,0},{3,1},{4,6},{5,7},{6,4},{7,5},{8,10},{9,11},{10,... | collective-permute-start | bytes 196616 | tf_op jit(solution)/shard_map/ppermute | solution.py:22
  12.4 5.1 %collective-permute-start.6 = (bf16[32,1024]{1,0:T(8,128)(2,1)S(1)}, bf16[32,1024]{1,0:T(8,128)(2,1)S(1)}, u32[]{:S(2)}, u32[]{:S(2)}) collective-permute-start(bf16[32,1024]{1,0:T(8,128)(2,1)S(1)} %collective-permute-done.5.refs_6_), channel_id=1, source_target_pairs={{0,2},{1,3},{2,0},{3,1},{4,6},{5,7},{6,4},{7,5},{8,10},{9,11},{10,... | collective-permute-start | bytes 196616 | tf_op jit(solution)/shard_map/ppermute | solution.py:22
  13.9 4.8 %collective-permute-start.4 = (bf16[32,1024]{1,0:T(8,128)(2,1)S(1)}, bf16[32,1024]{1,0:T(8,128)(2,1)S(1)}, u32[]{:S(2)}, u32[]{:S(2)}) collective-permute-start(bf16[32,1024]{1,0:T(8,128)(2,1)S(1)} %collective-permute-done.3.refs_4_), channel_id=1, source_target_pairs={{0,2},{1,3},{2,0},{3,1},{4,6},{5,7},{6,4},{7,5},{8,10},{9,11},{10,... | collective-permute-start | bytes 196616 | tf_op jit(solution)/shard_map/ppermute | solution.py:22
  14.4 5.0 %collective-permute-start.2 = (bf16[32,1024]{1,0:T(8,128)(2,1)S(1)}, bf16[32,1024]{1,0:T(8,128)(2,1)S(1)}, u32[]{:S(2)}, u32[]{:S(2)}) collective-permute-start(bf16[32,1024]{1,0:T(8,128)(2,1)S(1)} %collective-permute-done.1.refs_2_), channel_id=1, source_target_pairs={{0,2},{1,3},{2,0},{3,1},{4,6},{5,7},{6,4},{7,5},{8,10},{9,11},{10,... | collective-permute-start | bytes 196616 | tf_op jit(solution)/shard_map/ppermute | solution.py:22
  21.3 4.0 %collective-permute-start.9 = (bf16[8,16,128]{2,1,0:T(8,128)(2,1)S(1)}, bf16[8,16,128]{2,1,0:T(8,128)(2,1)S(1)}, u32[]{:S(2)}, u32[]{:S(2)}) collective-permute-start(bf16[8,16,128]{2,1,0:T(8,128)(2,1)S(1)} %get-tuple-element.26), channel_id=1, source_target_pairs={{0,16},{16,0},{1,17},{17,1},{2,18},{18,2},{3,19},{19,3},{4,20},{20... | collective-permute-start | bytes 98312 | tf_op jit(solution)/shard_map/ppermute | solution.py:22
  25.2 6.8 %collective-permute-start.15 = (bf16[8,48,128]{2,1,0:T(8,128)(2,1)S(1)}, bf16[8,48,128]{2,1,0:T(8,128)(2,1)S(1)}, u32[]{:S(2)}, u32[]{:S(2)}) collective-permute-start(bf16[8,48,128]{2,1,0:T(8,128)(2,1)S(1)} %constant_dynamic-update-slice_fusion.refs_8_), channel_id=1, source_target_pairs={{0,12},{1,13},{2,14},{3,15},{4,8},{5,9},{6,10},{7,11},{8,4},{9,5},... | collective-permute-start | bytes 294920 | tf_op jit(solution)/shard_map/ppermute | solution.py:22
  28.3 6.7 %collective-permute-start.13 = (bf16[8,48,128]{2,1,0:T(8,128)(2,1)S(1)}, bf16[8,48,128]{2,1,0:T(8,128)(2,1)S(1)}, u32[]{:S(2)}, u32[]{:S(2)}) collective-permute-start(bf16[8,48,128]{2,1,0:T(8,128)(2,1)S(1)} %constant_dynamic-update-slice_fusion.refs_8_), channel_id=1, source_target_pairs={{0,8},{1,9},{2,10},{3,11},{4,12},{5,13},{6,14},{7,15},{8,0},{9,1},... | collective-permute-start | bytes 294920 | tf_op jit(solution)/shard_map/ppermute | solution.py:22
  28.4 7.5 %collective-permute-start.11 = (bf16[8,48,128]{2,1,0:T(8,128)(2,1)S(1)}, bf16[8,48,128]{2,1,0:T(8,128)(2,1)S(1)}, u32[]{:S(2)}, u32[]{:S(2)}) collective-permute-start(bf16[8,48,128]{2,1,0:T(8,128)(2,1)S(1)} %constant_dynamic-update-slice_fusion.refs_8_), channel_id=1, source_target_pairs={{0,4},{1,5},{2,6},{3,7},{4,0},{5,1},{6,2},{7,3},{8,12},{9,13},{10,... | collective-permute-start | bytes 294920 | tf_op jit(solution)/shard_map/ppermute | solution.py:22
  29.6 7.5 %collective-permute-start.10 = (bf16[8,48,128]{2,1,0:T(8,128)(2,1)S(1)}, bf16[8,48,128]{2,1,0:T(8,128)(2,1)S(1)}, u32[]{:S(2)}, u32[]{:S(2)}) collective-permute-start(bf16[8,48,128]{2,1,0:T(8,128)(2,1)S(1)} %constant_dynamic-update-slice_fusion.refs_8_), channel_id=1, source_target_pairs={{0,2},{1,3},{2,0},{3,1},{4,6},{5,7},{6,4},{7,5},{8,10},{9,11},{10,... | collective-permute-start | bytes 294920 | tf_op jit(solution)/shard_map/ppermute | solution.py:22
  32.0 5.1 %collective-permute-start.16 = (bf16[8,48,128]{2,1,0:T(8,128)(2,1)S(1)}, bf16[8,48,128]{2,1,0:T(8,128)(2,1)S(1)}, u32[]{:S(2)}, u32[]{:S(2)}) collective-permute-start(bf16[8,48,128]{2,1,0:T(8,128)(2,1)S(1)} %collective-permute-done.15.refs_14_), channel_id=1, source_target_pairs={{0,2},{1,3},{2,0},{3,1},{4,6},{5,7},{6,4},{7,5},{8,10},{9,11},{10,... | collective-permute-start | bytes 294920 | tf_op jit(solution)/shard_map/ppermute | solution.py:22
  35.1 4.7 %collective-permute-start.14 = (bf16[8,48,128]{2,1,0:T(8,128)(2,1)S(1)}, bf16[8,48,128]{2,1,0:T(8,128)(2,1)S(1)}, u32[]{:S(2)}, u32[]{:S(2)}) collective-permute-start(bf16[8,48,128]{2,1,0:T(8,128)(2,1)S(1)} %collective-permute-done.13.refs_12_), channel_id=1, source_target_pairs={{0,2},{1,3},{2,0},{3,1},{4,6},{5,7},{6,4},{7,5},{8,10},{9,11},{10,... | collective-permute-start | bytes 294920 | tf_op jit(solution)/shard_map/ppermute | solution.py:22
  35.8 5.1 %collective-permute-start.12 = (bf16[8,48,128]{2,1,0:T(8,128)(2,1)S(1)}, bf16[8,48,128]{2,1,0:T(8,128)(2,1)S(1)}, u32[]{:S(2)}, u32[]{:S(2)}) collective-permute-start(bf16[8,48,128]{2,1,0:T(8,128)(2,1)S(1)} %collective-permute-done.11.refs_10_), channel_id=1, source_target_pairs={{0,2},{1,3},{2,0},{3,1},{4,6},{5,7},{6,4},{7,5},{8,10},{9,11},{10,... | collective-permute-start | bytes 294920 | tf_op jit(solution)/shard_map/ppermute | solution.py:22
  41.4 2.0 %collective-permute-start.17 = (bf16[8,32,1024]{2,1,0:T(8,128)(2,1)S(1)}, bf16[8,32,1024]{2,1,0:T(8,128)(2,1)S(1)}, u32[]{:S(2)}, u32[]{:S(2)}) collective-permute-start(bf16[8,32,1024]{2,1,0:T(8,128)(2,1)S(1)} %get-tuple-element.30), channel_id=1, source_target_pairs={{0,1},{1,0},{2,3},{3,2},{4,5},{5,4},{6,7},{7,6},{8,9},{9,8},{10,11... | collective-permute-start | bytes 1572872 | tf_op jit(solution)/shard_map/ppermute | solution.py:22
  57.1 4.1 %collective-permute-start.19 = (bf16[2,32,1024]{2,1,0:T(8,128)(2,1)S(1)}, bf16[2,32,1024]{2,1,0:T(8,128)(2,1)S(1)}, u32[]{:S(2)}, u32[]{:S(2)}) collective-permute-start(bf16[2,32,1024]{2,1,0:T(8,128)(2,1)S(1)} %get-tuple-element.36), channel_id=1, source_target_pairs={{0,1},{1,0},{2,3},{3,2},{4,5},{5,4},{6,7},{7,6},{8,9},{9,8},{10,11... | collective-permute-start | bytes 393224 | tf_op jit(solution)/shard_map/ppermute | solution.py:22
  57.2 4.0 %collective-permute-start.18 = (bf16[1,16,1024]{2,1,0:T(8,128)(2,1)S(1)}, bf16[1,16,1024]{2,1,0:T(8,128)(2,1)S(1)}, u32[]{:S(2)}, u32[]{:S(2)}) collective-permute-start(bf16[1,16,1024]{2,1,0:T(8,128)(2,1)S(1)} %get-tuple-element.35), channel_id=1, source_target_pairs={{0,16},{16,0},{1,17},{17,1},{2,18},{18,2},{3,19},{19,3},{4,20},{20... | collective-permute-start | bytes 98312 | tf_op jit(solution)/shard_map/ppermute | solution.py:22

commit v8 on v7

--- a/solution.py
+++ b/solution.py
@@ -85,7 +85,7 @@
 def project(states, core, partner, own, copies):
     columns = partner[0].shape[1]
     width = columns // RANK
-    step = min(columns, 256)
+    step = min(columns, 512)
     total = jnp.zeros((states.shape[0], 2 * width), jnp.float32)
     for other, (a_ref, b_ref) in ((1, partner), (0, own)):
         if not other:
@@ -101,8 +101,9 @@
             source = lax.broadcasted_iota(jnp.int32, (step, 2 * width), 0) + at
             target = lax.broadcasted_iota(jnp.int32, (step, 2 * width), 1)
             adds = jnp.where((source >> 3) + first == target, 1.0, 0.0).astype(jnp.bfloat16)
-            total += jnp.dot(high, adds, preferred_element_type=jnp.float32)
-            total += jnp.dot(low, adds, preferred_element_type=jnp.float32)
+            split = jnp.concatenate([high, low], axis=1)
+            twice = jnp.concatenate([adds, adds], axis=0)
+            total += jnp.dot(split, twice, preferred_element_type=jnp.float32)
     return total
 
 
@@ -272,7 +273,7 @@
     chips, rows, size = exact_ref.shape
     depth = rows // layers
 
-    @pl.loop(0, chips)
+    @pl.loop(0, chips, unroll=True)
     def _(cell):
         for at in range(0, size, 128):
             lanes = slice(at, at + 128)
@@ -315,7 +316,7 @@
     away = 2 * core - 1
     _, rows, size = inner_ref.shape
 
-    @pl.loop(0, chips)
+    @pl.loop(0, chips, unroll=True)
     def _(cell):
         before, after = (cell - 1 + core) & (chips - 1), (cell + core) & (chips - 1)
         rolled = None

time: 62.2 us -> 61.1 us (0.982)
  Pallas kernels: 9.14 us -> 7.96 us
    pallas_call x1, Pallas kernels: 2.77 us -> 1.86 us  [second_collision(): pl.pallas_call(functools.partial(second_kernel, chips), out_shape=[jax.Sh...]
where the time goes in v8:
time: 61.1 us; the launch traced here: 60.9 us
  starting transfers between devices  23.6 us (39%)
  waiting for transfers between devices  18.3 us (30%)
  blocking collectives  10.9 us (18%)
  Pallas kernels  7.96 us (13%)
    ppermute x20, starting transfers between devices, swap(): return lax.ppermute(block, axis, [(i, i ^ bits) for i in range(count)])  23.6 us
    ppermute x20, waiting for transfers between devices, swap(): return lax.ppermute(block, axis, [(i, i ^ bits) for i in range(count)])  18.3 us
    all_to_all x1, blocking collectives, settled(): lax.all_to_all(sent, 'mom', split_axis=0, concat_axis=0, tiled=True, axis...  10.9 us
    pallas_call x1, Pallas kernels, second_collision(): pl.pallas_call(functools.partial(second_kernel, chips), out_shape=[jax.Sh...  1.86 us
    pallas_call x1, Pallas kernels, first_collision(): pl.pallas_call(functools.partial(first_kernel, chips, layers), out_shape=...  1.62 us
    pallas_call x1, Pallas kernels, keep(): pl.pallas_call(keep_kernel, out_shape=[jax.ShapeDtypeStruct(each.shape, e...  1.57 us
  transfers between devices with their start and end apart: 20, of which 11 were waited for; matrix products, arithmetic and copies ran while one was open for 0% of the time, Pallas kernels for 5%

profile of v8, /device:TPU:0, one launch (start us, length us, event | category | flops | bytes accessed | tf_op | source)
XLA Modules:
  0.0 60.9 jit_solution(4422064898476418292)
XLA Ops:
  0.0 0.5 collective-permute-start.7
  0.5 0.0 collective-permute-start.8
  0.5 0.9 %shard_map.55 = (f32[32,1024]{1,0:T(8,128)S(1)}, bf16[32,1024]{1,0:T(8,128)(2,1)S(1)}, f32[8,1024]{1,0:T(8,128)S(1)}) custom-call(f32[32,1024]{1,0:T(8,128)} %bitcast.5, f32[3,1024]{1,0:T(4,128)} %velocity_hbm.1, f32[1,1024]{1,0:T(1,128)} %bitcast.6), custom_call_target="tpu_custom_call" | custom-call | flops 32768 | bytes 327680 | tf_op jit(solution)/shard_map/pallas_call | solution.py:64
  1.5 5.1 %collective-permute-start.5 = (bf16[32,1024]{1,0:T(8,128)(2,1)S(1)}, bf16[32,1024]{1,0:T(8,128)(2,1)S(1)}, u32[]{:S(2)}, u32[]{:S(2)}) collective-permute-start(bf16[32,1024]{1,0:T(8,128)(2,1)S(1)} %get-tuple-element.22.refs_0_), channel_id=1, source_target_pairs={{0,12},{1,13},{2,14},{3,15},{4,8},{5,9},{6,10},{7,11},{8,4},{9,5},... | collective-permute-start | bytes 196616 | tf_op jit(solution)/shard_map/ppermute | solution.py:22
  6.6 0.0 collective-permute-start.3
  6.6 0.6 %collective-permute-start.1 = (bf16[32,1024]{1,0:T(8,128)(2,1)S(1)}, bf16[32,1024]{1,0:T(8,128)(2,1)S(1)}, u32[]{:S(2)}, u32[]{:S(2)}) collective-permute-start(bf16[32,1024]{1,0:T(8,128)(2,1)S(1)} %get-tuple-element.22.refs_0_), channel_id=1, source_target_pairs={{0,4},{1,5},{2,6},{3,7},{4,0},{5,1},{6,2},{7,3},{8,12},{9,13},{10,... | collective-permute-start | bytes 196616 | tf_op jit(solution)/shard_map/ppermute | solution.py:22
  7.2 1.9 %collective-permute-done.5.refs_6_ = bf16[32,1024]{1,0:T(8,128)(2,1)S(1)} collective-permute-done((bf16[32,1024]{1,0:T(8,128)(2,1)S(1)}, bf16[32,1024]{1,0:T(8,128)(2,1)S(1)}, u32[]{:S(2)}, u32[]{:S(2)}) %collective-permute-start.5) | collective-permute-done | bytes 65568 | tf_op jit(solution)/shard_map/ppermute | solution.py:22
  9.1 1.7 %collective-permute-start = (bf16[32,1024]{1,0:T(8,128)(2,1)S(1)}, bf16[32,1024]{1,0:T(8,128)(2,1)S(1)}, u32[]{:S(2)}, u32[]{:S(2)}) collective-permute-start(bf16[32,1024]{1,0:T(8,128)(2,1)S(1)} %get-tuple-element.22.refs_0_), channel_id=1, source_target_pairs={{0,2},{1,3},{2,0},{3,1},{4,6},{5,7},{6,4},{7,5},{8,10},{9,11},{10,... | collective-permute-start | bytes 196616 | tf_op jit(solution)/shard_map/ppermute | solution.py:22
  10.9 1.5 %collective-permute-done.3.refs_4_ = bf16[32,1024]{1,0:T(8,128)(2,1)S(1)} collective-permute-done((bf16[32,1024]{1,0:T(8,128)(2,1)S(1)}, bf16[32,1024]{1,0:T(8,128)(2,1)S(1)}, u32[]{:S(2)}, u32[]{:S(2)}) %collective-permute-start.3) | collective-permute-done | bytes 65568 | tf_op jit(solution)/shard_map/ppermute | solution.py:22
  12.4 1.5 %collective-permute-start.6 = (bf16[32,1024]{1,0:T(8,128)(2,1)S(1)}, bf16[32,1024]{1,0:T(8,128)(2,1)S(1)}, u32[]{:S(2)}, u32[]{:S(2)}) collective-permute-start(bf16[32,1024]{1,0:T(8,128)(2,1)S(1)} %collective-permute-done.5.refs_6_), channel_id=1, source_target_pairs={{0,2},{1,3},{2,0},{3,1},{4,6},{5,7},{6,4},{7,5},{8,10},{9,11},{10,... | collective-permute-start | bytes 196616 | tf_op jit(solution)/shard_map/ppermute | solution.py:22
  13.9 0.0 collective-permute-done.1.refs_2_
  13.9 0.5 collective-permute-start.4
  14.4 0.0 collective-permute-done.refs_1_
  14.4 1.5 %collective-permute-start.2 = (bf16[32,1024]{1,0:T(8,128)(2,1)S(1)}, bf16[32,1024]{1,0:T(8,128)(2,1)S(1)}, u32[]{:S(2)}, u32[]{:S(2)}) collective-permute-start(bf16[32,1024]{1,0:T(8,128)(2,1)S(1)} %collective-permute-done.1.refs_2_), channel_id=1, source_target_pairs={{0,2},{1,3},{2,0},{3,1},{4,6},{5,7},{6,4},{7,5},{8,10},{9,11},{10,... | collective-permute-start | bytes 196616 | tf_op jit(solution)/shard_map/ppermute | solution.py:22
  15.9 1.6 %shard_map.56 = (bf16[1024,512]{1,0:T(8,128)(2,1)S(1)}, bf16[1024,512]{1,0:T(8,128)(2,1)S(1)}) custom-call(bf16[1024,512]{1,0:T(8,128)(2,1)} %a_hbm.1, bf16[1024,512]{1,0:T(8,128)(2,1)} %b_hbm.1), custom_call_target="tpu_custom_call" | custom-call | bytes 4194304 | tf_op jit(solution)/shard_map/pallas_call | solution.py:182
  17.5 0.0 collective-permute-done.6.refs_7_
  17.5 1.2 %collective-permute-done.4.refs_5_ = bf16[32,1024]{1,0:T(8,128)(2,1)S(1)} collective-permute-done((bf16[32,1024]{1,0:T(8,128)(2,1)S(1)}, bf16[32,1024]{1,0:T(8,128)(2,1)S(1)}, u32[]{:S(2)}, u32[]{:S(2)}) %collective-permute-start.4) | collective-permute-done | bytes 65568 | tf_op jit(solution)/shard_map/ppermute | solution.py:22
  18.7 0.7 %collective-permute-done.2.refs_3_ = bf16[32,1024]{1,0:T(8,128)(2,1)S(1)} collective-permute-done((bf16[32,1024]{1,0:T(8,128)(2,1)S(1)}, bf16[32,1024]{1,0:T(8,128)(2,1)S(1)}, u32[]{:S(2)}, u32[]{:S(2)}) %collective-permute-start.2) | collective-permute-done | bytes 65568 | tf_op jit(solution)/shard_map/ppermute | solution.py:22
  19.4 0.0 collective-permute-done.7.refs_10_.refs_2_
  19.4 0.0 collective-permute-done.8.refs_11_.refs_3_
  19.4 1.6 %shard_map.57 = (bf16[8,32,128]{2,1,0:T(8,128)(2,1)S(1)}, bf16[8,16,128]{2,1,0:T(8,128)(2,1)S(1)}) custom-call(bf16[32,1024]{1,0:T(8,128)(2,1)S(1)} %get-tuple-element.22.refs_0_, bf16[32,1024]{1,0:T(8,128)(2,1)S(1)} %collective-permute-done.refs_1_, bf16[32,1024]{1,0:T(8,128)(2,1)S(1)} %collective-permute-done.1.refs_2_, ...), custom_call_target="tpu_custom_call" | custom-call | flops 1073741824 | bytes 4718592 | tf_op jit(solution)/shard_map/pallas_call | solution.py:220
  21.0 1.6 %collective-permute-start.9 = (bf16[8,16,128]{2,1,0:T(8,128)(2,1)S(1)}, bf16[8,16,128]{2,1,0:T(8,128)(2,1)S(1)}, u32[]{:S(2)}, u32[]{:S(2)}) collective-permute-start(bf16[8,16,128]{2,1,0:T(8,128)(2,1)S(1)} %get-tuple-element.26), channel_id=1, source_target_pairs={{0,16},{16,0},{1,17},{17,1},{2,18},{18,2},{3,19},{19,3},{4,20},{20... | collective-permute-start | bytes 98312 | tf_op jit(solution)/shard_map/ppermute | solution.py:22
  22.6 2.4 %collective-permute-done.9 = bf16[8,16,128]{2,1,0:T(8,128)(2,1)S(1)} collective-permute-done((bf16[8,16,128]{2,1,0:T(8,128)(2,1)S(1)}, bf16[8,16,128]{2,1,0:T(8,128)(2,1)S(1)}, u32[]{:S(2)}, u32[]{:S(2)}) %collective-permute-start.9) | collective-permute-done | bytes 32800 | tf_op jit(solution)/shard_map/ppermute | solution.py:22
  25.0 3.1 %collective-permute-start.15 = (bf16[8,48,128]{2,1,0:T(8,128)(2,1)S(1)}, bf16[8,48,128]{2,1,0:T(8,128)(2,1)S(1)}, u32[]{:S(2)}, u32[]{:S(2)}) collective-permute-start(bf16[8,48,128]{2,1,0:T(8,128)(2,1)S(1)} %constant_dynamic-update-slice_fusion.refs_8_), channel_id=1, source_target_pairs={{0,12},{1,13},{2,14},{3,15},{4,8},{5,9},{6,10},{7,11},{8,4},{9,5},... | collective-permute-start | bytes 294920 | tf_op jit(solution)/shard_map/ppermute | solution.py:22
  28.1 0.0 collective-permute-start.13
  28.1 1.3 %collective-permute-start.11 = (bf16[8,48,128]{2,1,0:T(8,128)(2,1)S(1)}, bf16[8,48,128]{2,1,0:T(8,128)(2,1)S(1)}, u32[]{:S(2)}, u32[]{:S(2)}) collective-permute-start(bf16[8,48,128]{2,1,0:T(8,128)(2,1)S(1)} %constant_dynamic-update-slice_fusion.refs_8_), channel_id=1, source_target_pairs={{0,4},{1,5},{2,6},{3,7},{4,0},{5,1},{6,2},{7,3},{8,12},{9,13},{10,... | collective-permute-start | bytes 294920 | tf_op jit(solution)/shard_map/ppermute | solution.py:22
  29.4 1.0 %collective-permute-start.10 = (bf16[8,48,128]{2,1,0:T(8,128)(2,1)S(1)}, bf16[8,48,128]{2,1,0:T(8,128)(2,1)S(1)}, u32[]{:S(2)}, u32[]{:S(2)}) collective-permute-start(bf16[8,48,128]{2,1,0:T(8,128)(2,1)S(1)} %constant_dynamic-update-slice_fusion.refs_8_), channel_id=1, source_target_pairs={{0,2},{1,3},{2,0},{3,1},{4,6},{5,7},{6,4},{7,5},{8,10},{9,11},{10,... | collective-permute-start | bytes 294920 | tf_op jit(solution)/shard_map/ppermute | solution.py:22
  30.4 1.4 %collective-permute-done.15.refs_14_ = bf16[8,48,128]{2,1,0:T(8,128)(2,1)S(1)} collective-permute-done((bf16[8,48,128]{2,1,0:T(8,128)(2,1)S(1)}, bf16[8,48,128]{2,1,0:T(8,128)(2,1)S(1)}, u32[]{:S(2)}, u32[]{:S(2)}) %collective-permute-start.15) | collective-permute-done | bytes 98336 | tf_op jit(solution)/shard_map/ppermute | solution.py:22
  31.8 1.3 %collective-permute-start.16 = (bf16[8,48,128]{2,1,0:T(8,128)(2,1)S(1)}, bf16[8,48,128]{2,1,0:T(8,128)(2,1)S(1)}, u32[]{:S(2)}, u32[]{:S(2)}) collective-permute-start(bf16[8,48,128]{2,1,0:T(8,128)(2,1)S(1)} %collective-permute-done.15.refs_14_), channel_id=1, source_target_pairs={{0,2},{1,3},{2,0},{3,1},{4,6},{5,7},{6,4},{7,5},{8,10},{9,11},{10,... | collective-permute-start | bytes 294920 | tf_op jit(solution)/shard_map/ppermute | solution.py:22
  33.1 1.7 %collective-permute-done.13.refs_12_ = bf16[8,48,128]{2,1,0:T(8,128)(2,1)S(1)} collective-permute-done((bf16[8,48,128]{2,1,0:T(8,128)(2,1)S(1)}, bf16[8,48,128]{2,1,0:T(8,128)(2,1)S(1)}, u32[]{:S(2)}, u32[]{:S(2)}) %collective-permute-start.13) | collective-permute-done | bytes 98336 | tf_op jit(solution)/shard_map/ppermute | solution.py:22
  34.9 0.7 %collective-permute-start.14 = (bf16[8,48,128]{2,1,0:T(8,128)(2,1)S(1)}, bf16[8,48,128]{2,1,0:T(8,128)(2,1)S(1)}, u32[]{:S(2)}, u32[]{:S(2)}) collective-permute-start(bf16[8,48,128]{2,1,0:T(8,128)(2,1)S(1)} %collective-permute-done.13.refs_12_), channel_id=1, source_target_pairs={{0,2},{1,3},{2,0},{3,1},{4,6},{5,7},{6,4},{7,5},{8,10},{9,11},{10,... | collective-permute-start | bytes 294920 | tf_op jit(solution)/shard_map/ppermute | solution.py:22
  35.6 0.0 collective-permute-done.11.refs_10_
  35.6 1.3 %collective-permute-start.12 = (bf16[8,48,128]{2,1,0:T(8,128)(2,1)S(1)}, bf16[8,48,128]{2,1,0:T(8,128)(2,1)S(1)}, u32[]{:S(2)}, u32[]{:S(2)}) collective-permute-start(bf16[8,48,128]{2,1,0:T(8,128)(2,1)S(1)} %collective-permute-done.11.refs_10_), channel_id=1, source_target_pairs={{0,2},{1,3},{2,0},{3,1},{4,6},{5,7},{6,4},{7,5},{8,10},{9,11},{10,... | collective-permute-start | bytes 294920 | tf_op jit(solution)/shard_map/ppermute | solution.py:22
  36.9 0.0 collective-permute-done.10.refs_9_
  36.9 0.0 collective-permute-done.16.refs_15_
  36.9 2.7 %collective-permute-done.14.refs_13_ = bf16[8,48,128]{2,1,0:T(8,128)(2,1)S(1)} collective-permute-done((bf16[8,48,128]{2,1,0:T(8,128)(2,1)S(1)}, bf16[8,48,128]{2,1,0:T(8,128)(2,1)S(1)}, u32[]{:S(2)}, u32[]{:S(2)}) %collective-permute-start.14) | collective-permute-done | bytes 98336 | tf_op jit(solution)/shard_map/ppermute | solution.py:22
  39.6 1.1 %collective-permute-done.12.refs_11_ = bf16[8,48,128]{2,1,0:T(8,128)(2,1)S(1)} collective-permute-done((bf16[8,48,128]{2,1,0:T(8,128)(2,1)S(1)}, bf16[8,48,128]{2,1,0:T(8,128)(2,1)S(1)}, u32[]{:S(2)}, u32[]{:S(2)}) %collective-permute-start.12) | collective-permute-done | bytes 98336 | tf_op jit(solution)/shard_map/ppermute | solution.py:22
  40.6 0.5 shard_map.58
  41.1 0.1 collective-permute-start.17
  41.2 0.6 shard_map.59.inner_ref
  41.8 1.3 %collective-permute-done.17.other_ref = bf16[8,32,1024]{2,1,0:T(8,128)(2,1)S(1)} collective-permute-done((bf16[8,32,1024]{2,1,0:T(8,128)(2,1)S(1)}, bf16[8,32,1024]{2,1,0:T(8,128)(2,1)S(1)}, u32[]{:S(2)}, u32[]{:S(2)}) %collective-permute-start.17) | collective-permute-done | bytes 524320 | tf_op jit(solution)/shard_map/ppermute | solution.py:22
  43.1 1.9 %shard_map.60 = (bf16[8,2,32,128]{3,2,1,0:T(8,128)(2,1)S(1)}, f32[32,1024]{1,0:T(8,128)S(1)}, f32[32,1024]{1,0:T(8,128)S(1)}) custom-call(f32[8,32,1024]{2,1,0:T(8,128)S(1)} %shard_map.59.inner_ref, bf16[8,32,1024]{2,1,0:T(8,128)(2,1)S(1)} %collective-permute-done.17.other_ref, f32[8,1024]{1,0:T(8,128)S(1)} %get-tuple-element.29.tables_ref, ...), custom_call_target="tpu_custom_call" | custom-call | flops 1073741824 | bytes 4718592 | tf_op jit(solution)/shard_map/pallas_call | solution.py:346
  45.0 10.9 %all_to_all.5.got_ref = bf16[8,2,32,128]{3,2,1,0:T(8,128)(2,1)S(1)} all-to-all(bf16[8,2,32,128]{3,2,1,0:T(8,128)(2,1)S(1)} %get-tuple-element.31), channel_id=1, replica_groups={{0,2,4,6,8,10,12,14},{1,3,5,7,9,11,13,15},{16,18,20,22,24,26,28,30},{17..., dimensions={0} | all-to-all | bytes 262144 | tf_op jit(solution)/shard_map/all_to_all | solution.py:406
  56.0 0.1 collective-permute-start.19
  56.0 1.6 %collective-permute-start.18 = (bf16[1,16,1024]{2,1,0:T(8,128)(2,1)S(1)}, bf16[1,16,1024]{2,1,0:T(8,128)(2,1)S(1)}, u32[]{:S(2)}, u32[]{:S(2)}) collective-permute-start(bf16[1,16,1024]{2,1,0:T(8,128)(2,1)S(1)} %get-tuple-element.35), channel_id=1, source_target_pairs={{0,16},{16,0},{1,17},{17,1},{2,18},{18,2},{3,19},{19,3},{4,20},{20... | collective-permute-start | bytes 98312 | tf_op jit(solution)/shard_map/ppermute | solution.py:22
  57.6 2.4 %collective-permute-done.18.edges_ref = bf16[1,16,1024]{2,1,0:T(8,128)(2,1)S(1)} collective-permute-done((bf16[1,16,1024]{2,1,0:T(8,128)(2,1)S(1)}, bf16[1,16,1024]{2,1,0:T(8,128)(2,1)S(1)}, u32[]{:S(2)}, u32[]{:S(2)}) %collective-permute-start.18) | collective-permute-done | bytes 32800 | tf_op jit(solution)/shard_map/ppermute | solution.py:22
  60.0 0.0 collective-permute-done.19.cells_ref
  60.0 0.8 %shard_map.62 = f32[32,1024]{1,0:T(8,128)} custom-call(f32[32,1024]{1,0:T(8,128)S(1)} %get-tuple-element.34.exact_ref, bf16[1,16,1024]{2,1,0:T(8,128)(2,1)S(1)} %collective-permute-done.18.edges_ref, bf16[2,32,1024]{2,1,0:T(8,128)(2,1)S(1)} %collective-permute-done.19.cells_ref, f32[8,1024]{1,0:T(8,128)S(1)} %get-tuple-element.29.tables_ref), custom_call_target="tpu_custom_call" | custom-call | flops 655360 | bytes 393216 | tf_op jit(solution)/shard_map/pallas_call | solution.py:423
  (3 shorter events, 0.1 us)
Async XLA Ops:
  0.0 19.4 %collective-permute-start.7 = (bf16[1024,512]{1,0:T(8,128)(2,1)}, bf16[1024,512]{1,0:T(8,128)(2,1)S(1)}, u32[]{:S(2)}, u32[]{:S(2)}) collective-permute-start(bf16[1024,512]{1,0:T(8,128)(2,1)} %a_hbm.1), channel_id=1, source_target_pairs={{0,1},{1,0},{2,3},{3,2},{4,5},{5,4},{6,7},{7,6},{8,9},{9,8},{10,11... | collective-permute-start | bytes 3145736 | tf_op jit(solution)/shard_map/ppermute | solution.py:22
  0.5 18.9 %collective-permute-start.8 = (bf16[1024,512]{1,0:T(8,128)(2,1)}, bf16[1024,512]{1,0:T(8,128)(2,1)S(1)}, u32[]{:S(2)}, u32[]{:S(2)}) collective-permute-start(bf16[1024,512]{1,0:T(8,128)(2,1)} %b_hbm.1), channel_id=1, source_target_pairs={{0,1},{1,0},{2,3},{3,2},{4,5},{5,4},{6,7},{7,6},{8,9},{9,8},{10,11... | collective-permute-start | bytes 3145736 | tf_op jit(solution)/shard_map/ppermute | solution.py:22
  1.5 7.7 %collective-permute-start.5 = (bf16[32,1024]{1,0:T(8,128)(2,1)S(1)}, bf16[32,1024]{1,0:T(8,128)(2,1)S(1)}, u32[]{:S(2)}, u32[]{:S(2)}) collective-permute-start(bf16[32,1024]{1,0:T(8,128)(2,1)S(1)} %get-tuple-element.22.refs_0_), channel_id=1, source_target_pairs={{0,12},{1,13},{2,14},{3,15},{4,8},{5,9},{6,10},{7,11},{8,4},{9,5},... | collective-permute-start | bytes 196616 | tf_op jit(solution)/shard_map/ppermute | solution.py:22
  6.6 5.8 %collective-permute-start.3 = (bf16[32,1024]{1,0:T(8,128)(2,1)S(1)}, bf16[32,1024]{1,0:T(8,128)(2,1)S(1)}, u32[]{:S(2)}, u32[]{:S(2)}) collective-permute-start(bf16[32,1024]{1,0:T(8,128)(2,1)S(1)} %get-tuple-element.22.refs_0_), channel_id=1, source_target_pairs={{0,8},{1,9},{2,10},{3,11},{4,12},{5,13},{6,14},{7,15},{8,0},{9,1},... | collective-permute-start | bytes 196616 | tf_op jit(solution)/shard_map/ppermute | solution.py:22
  6.6 7.3 %collective-permute-start.1 = (bf16[32,1024]{1,0:T(8,128)(2,1)S(1)}, bf16[32,1024]{1,0:T(8,128)(2,1)S(1)}, u32[]{:S(2)}, u32[]{:S(2)}) collective-permute-start(bf16[32,1024]{1,0:T(8,128)(2,1)S(1)} %get-tuple-element.22.refs_0_), channel_id=1, source_target_pairs={{0,4},{1,5},{2,6},{3,7},{4,0},{5,1},{6,2},{7,3},{8,12},{9,13},{10,... | collective-permute-start | bytes 196616 | tf_op jit(solution)/shard_map/ppermute | solution.py:22
  9.1 5.3 %collective-permute-start = (bf16[32,1024]{1,0:T(8,128)(2,1)S(1)}, bf16[32,1024]{1,0:T(8,128)(2,1)S(1)}, u32[]{:S(2)}, u32[]{:S(2)}) collective-permute-start(bf16[32,1024]{1,0:T(8,128)(2,1)S(1)} %get-tuple-element.22.refs_0_), channel_id=1, source_target_pairs={{0,2},{1,3},{2,0},{3,1},{4,6},{5,7},{6,4},{7,5},{8,10},{9,11},{10,... | collective-permute-start | bytes 196616 | tf_op jit(solution)/shard_map/ppermute | solution.py:22
  12.4 5.1 %collective-permute-start.6 = (bf16[32,1024]{1,0:T(8,128)(2,1)S(1)}, bf16[32,1024]{1,0:T(8,128)(2,1)S(1)}, u32[]{:S(2)}, u32[]{:S(2)}) collective-permute-start(bf16[32,1024]{1,0:T(8,128)(2,1)S(1)} %collective-permute-done.5.refs_6_), channel_id=1, source_target_pairs={{0,2},{1,3},{2,0},{3,1},{4,6},{5,7},{6,4},{7,5},{8,10},{9,11},{10,... | collective-permute-start | bytes 196616 | tf_op jit(solution)/shard_map/ppermute | solution.py:22
  13.9 4.8 %collective-permute-start.4 = (bf16[32,1024]{1,0:T(8,128)(2,1)S(1)}, bf16[32,1024]{1,0:T(8,128)(2,1)S(1)}, u32[]{:S(2)}, u32[]{:S(2)}) collective-permute-start(bf16[32,1024]{1,0:T(8,128)(2,1)S(1)} %collective-permute-done.3.refs_4_), channel_id=1, source_target_pairs={{0,2},{1,3},{2,0},{3,1},{4,6},{5,7},{6,4},{7,5},{8,10},{9,11},{10,... | collective-permute-start | bytes 196616 | tf_op jit(solution)/shard_map/ppermute | solution.py:22
  14.4 5.0 %collective-permute-start.2 = (bf16[32,1024]{1,0:T(8,128)(2,1)S(1)}, bf16[32,1024]{1,0:T(8,128)(2,1)S(1)}, u32[]{:S(2)}, u32[]{:S(2)}) collective-permute-start(bf16[32,1024]{1,0:T(8,128)(2,1)S(1)} %collective-permute-done.1.refs_2_), channel_id=1, source_target_pairs={{0,2},{1,3},{2,0},{3,1},{4,6},{5,7},{6,4},{7,5},{8,10},{9,11},{10,... | collective-permute-start | bytes 196616 | tf_op jit(solution)/shard_map/ppermute | solution.py:22
  21.0 4.0 %collective-permute-start.9 = (bf16[8,16,128]{2,1,0:T(8,128)(2,1)S(1)}, bf16[8,16,128]{2,1,0:T(8,128)(2,1)S(1)}, u32[]{:S(2)}, u32[]{:S(2)}) collective-permute-start(bf16[8,16,128]{2,1,0:T(8,128)(2,1)S(1)} %get-tuple-element.26), channel_id=1, source_target_pairs={{0,16},{16,0},{1,17},{17,1},{2,18},{18,2},{3,19},{19,3},{4,20},{20... | collective-permute-start | bytes 98312 | tf_op jit(solution)/shard_map/ppermute | solution.py:22
  25.0 6.8 %collective-permute-start.15 = (bf16[8,48,128]{2,1,0:T(8,128)(2,1)S(1)}, bf16[8,48,128]{2,1,0:T(8,128)(2,1)S(1)}, u32[]{:S(2)}, u32[]{:S(2)}) collective-permute-start(bf16[8,48,128]{2,1,0:T(8,128)(2,1)S(1)} %constant_dynamic-update-slice_fusion.refs_8_), channel_id=1, source_target_pairs={{0,12},{1,13},{2,14},{3,15},{4,8},{5,9},{6,10},{7,11},{8,4},{9,5},... | collective-permute-start | bytes 294920 | tf_op jit(solution)/shard_map/ppermute | solution.py:22
  28.1 6.7 %collective-permute-start.13 = (bf16[8,48,128]{2,1,0:T(8,128)(2,1)S(1)}, bf16[8,48,128]{2,1,0:T(8,128)(2,1)S(1)}, u32[]{:S(2)}, u32[]{:S(2)}) collective-permute-start(bf16[8,48,128]{2,1,0:T(8,128)(2,1)S(1)} %constant_dynamic-update-slice_fusion.refs_8_), channel_id=1, source_target_pairs={{0,8},{1,9},{2,10},{3,11},{4,12},{5,13},{6,14},{7,15},{8,0},{9,1},... | collective-permute-start | bytes 294920 | tf_op jit(solution)/shard_map/ppermute | solution.py:22
  28.1 7.5 %collective-permute-start.11 = (bf16[8,48,128]{2,1,0:T(8,128)(2,1)S(1)}, bf16[8,48,128]{2,1,0:T(8,128)(2,1)S(1)}, u32[]{:S(2)}, u32[]{:S(2)}) collective-permute-start(bf16[8,48,128]{2,1,0:T(8,128)(2,1)S(1)} %constant_dynamic-update-slice_fusion.refs_8_), channel_id=1, source_target_pairs={{0,4},{1,5},{2,6},{3,7},{4,0},{5,1},{6,2},{7,3},{8,12},{9,13},{10,... | collective-permute-start | bytes 294920 | tf_op jit(solution)/shard_map/ppermute | solution.py:22
  29.4 7.5 %collective-permute-start.10 = (bf16[8,48,128]{2,1,0:T(8,128)(2,1)S(1)}, bf16[8,48,128]{2,1,0:T(8,128)(2,1)S(1)}, u32[]{:S(2)}, u32[]{:S(2)}) collective-permute-start(bf16[8,48,128]{2,1,0:T(8,128)(2,1)S(1)} %constant_dynamic-update-slice_fusion.refs_8_), channel_id=1, source_target_pairs={{0,2},{1,3},{2,0},{3,1},{4,6},{5,7},{6,4},{7,5},{8,10},{9,11},{10,... | collective-permute-start | bytes 294920 | tf_op jit(solution)/shard_map/ppermute | solution.py:22
  31.8 5.1 %collective-permute-start.16 = (bf16[8,48,128]{2,1,0:T(8,128)(2,1)S(1)}, bf16[8,48,128]{2,1,0:T(8,128)(2,1)S(1)}, u32[]{:S(2)}, u32[]{:S(2)}) collective-permute-start(bf16[8,48,128]{2,1,0:T(8,128)(2,1)S(1)} %collective-permute-done.15.refs_14_), channel_id=1, source_target_pairs={{0,2},{1,3},{2,0},{3,1},{4,6},{5,7},{6,4},{7,5},{8,10},{9,11},{10,... | collective-permute-start | bytes 294920 | tf_op jit(solution)/shard_map/ppermute | solution.py:22
  34.9 4.7 %collective-permute-start.14 = (bf16[8,48,128]{2,1,0:T(8,128)(2,1)S(1)}, bf16[8,48,128]{2,1,0:T(8,128)(2,1)S(1)}, u32[]{:S(2)}, u32[]{:S(2)}) collective-permute-start(bf16[8,48,128]{2,1,0:T(8,128)(2,1)S(1)} %collective-permute-done.13.refs_12_), channel_id=1, source_target_pairs={{0,2},{1,3},{2,0},{3,1},{4,6},{5,7},{6,4},{7,5},{8,10},{9,11},{10,... | collective-permute-start | bytes 294920 | tf_op jit(solution)/shard_map/ppermute | solution.py:22
  35.6 5.1 %collective-permute-start.12 = (bf16[8,48,128]{2,1,0:T(8,128)(2,1)S(1)}, bf16[8,48,128]{2,1,0:T(8,128)(2,1)S(1)}, u32[]{:S(2)}, u32[]{:S(2)}) collective-permute-start(bf16[8,48,128]{2,1,0:T(8,128)(2,1)S(1)} %collective-permute-done.11.refs_10_), channel_id=1, source_target_pairs={{0,2},{1,3},{2,0},{3,1},{4,6},{5,7},{6,4},{7,5},{8,10},{9,11},{10,... | collective-permute-start | bytes 294920 | tf_op jit(solution)/shard_map/ppermute | solution.py:22
  41.1 2.0 %collective-permute-start.17 = (bf16[8,32,1024]{2,1,0:T(8,128)(2,1)S(1)}, bf16[8,32,1024]{2,1,0:T(8,128)(2,1)S(1)}, u32[]{:S(2)}, u32[]{:S(2)}) collective-permute-start(bf16[8,32,1024]{2,1,0:T(8,128)(2,1)S(1)} %get-tuple-element.30), channel_id=1, source_target_pairs={{0,1},{1,0},{2,3},{3,2},{4,5},{5,4},{6,7},{7,6},{8,9},{9,8},{10,11... | collective-permute-start | bytes 1572872 | tf_op jit(solution)/shard_map/ppermute | solution.py:22
  56.0 4.1 %collective-permute-start.19 = (bf16[2,32,1024]{2,1,0:T(8,128)(2,1)S(1)}, bf16[2,32,1024]{2,1,0:T(8,128)(2,1)S(1)}, u32[]{:S(2)}, u32[]{:S(2)}) collective-permute-start(bf16[2,32,1024]{2,1,0:T(8,128)(2,1)S(1)} %get-tuple-element.36), channel_id=1, source_target_pairs={{0,1},{1,0},{2,3},{3,2},{4,5},{5,4},{6,7},{7,6},{8,9},{9,8},{10,11... | collective-permute-start | bytes 393224 | tf_op jit(solution)/shard_map/ppermute | solution.py:22
  56.0 4.0 %collective-permute-start.18 = (bf16[1,16,1024]{2,1,0:T(8,128)(2,1)S(1)}, bf16[1,16,1024]{2,1,0:T(8,128)(2,1)S(1)}, u32[]{:S(2)}, u32[]{:S(2)}) collective-permute-start(bf16[1,16,1024]{2,1,0:T(8,128)(2,1)S(1)} %get-tuple-element.35), channel_id=1, source_target_pairs={{0,16},{16,0},{1,17},{17,1},{2,18},{18,2},{3,19},{19,3},{4,20},{20... | collective-permute-start | bytes 98312 | tf_op jit(solution)/shard_map/ppermute | solution.py:22
